TPU v7x, 32 devices: a whole 2x2x4 slice. The times are simulated.
32 devices in a mesh: tm: 8 (over z, x), chan: 4 (over y, core).
Axes of the slice: x: 2, y: 2, z: 4, core: 2. Of those that a mesh axis runs over, the one named last changes fastest.
Arguments:
- record: float32 [8192, 1024], P('tm', 'chan'), may hold values from -120 to 120
- test_matrix: float32 [64, 1024, 128], P(None, 'chan'), may hold values from -0.0234375 to 0.0234375
Outputs:
- basis: float32 [8192, 128], P('tm')
- coeffs: float32 [64, 1024, 128], P('tm', 'chan')
All inputs are finite; a program needn't handle non-finite values.
Results may differ from a plain program's by a relative error of at most 0.00024.
Values sent between devices are 32-bit elements; how exact they have to be, the bound alone decides.
No kernel may reach another device: no remote copies, remote signals or barrier semaphores. Data moves between devices by JAX's collectives and lax.ppermute only.
A program may use at most 256 MiB of HBM per device.

v0:
```python
import functools

import jax
import jax.numpy as jnp
from jax import lax
from jax.experimental import pallas as pl
from jax.experimental.pallas import tpu as pltpu
from jax.sharding import PartitionSpec as P


F32 = jnp.float32
BF16 = jnp.bfloat16
HIGHEST = lax.Precision.HIGHEST
STEP = 16
SMEM = pl.BlockSpec(memory_space=pltpu.SMEM)
VMEM = pl.BlockSpec(memory_space=pltpu.VMEM)


def cost(flops, size):
    return pl.CostEstimate(flops=flops, bytes_accessed=size, transcendentals=0)


def split(x):
    high = x.astype(BF16)
    return high, (x - high.astype(F32)).astype(BF16)


def three(a_high, a_low, b_high, b_low):
    dot = functools.partial(jnp.dot, preferred_element_type=F32)
    return dot(a_high, b_high) + dot(a_high, b_low) + dot(a_low, b_high)


def sketch_kernel(owner_ref, before_ref, record_ref, after_ref, weight_ref, *refs):
    *outs, high, low, even, odd, total = refs
    pair = pl.program_id(0)
    rows, width = total.shape
    groups = weight_ref.shape[0]
    tiles = 3
    tile = (rows + STEP) // tiles

    @pl.when(pair == 0)
    def _():
        first = 0
        for ref in (before_ref, record_ref, after_ref):
            size = ref.shape[0]
            high[first : first + size], low[first : first + size] = split(ref[...])
            first += size
        total[...] = jnp.zeros_like(total)

    weight = jnp.concatenate(
        [jnp.concatenate([weight_ref[a, 0], weight_ref[a, 1]], axis=1) for a in range(groups)],
        axis=0,
    )
    weight_high, weight_low = split(weight)
    for first in range(0, tiles * tile, tile):
        starts = [first + a * STEP for a in range(groups)]
        left_high = jnp.concatenate([high[s : s + tile] for s in starts], axis=1)
        left_low = jnp.concatenate([low[s : s + tile] for s in starts], axis=1)
        value = three(left_high, left_low, weight_high, weight_low)
        even[first : first + tile] = value[:, :width]
        odd[first : first + tile] = value[:, width:]
    total[...] += even[pl.ds(2 * pair, rows), :] + odd[pl.ds(2 * pair + 1, rows), :]

    @pl.when(pair == pl.num_programs(0) - 1)
    def _():
        share = rows // len(outs)
        for s, out in enumerate(outs):
            owner = lax.rem(owner_ref[0] + s, len(outs))
            out[...] = total[pl.ds(pl.multiple_of(owner * share, 8), share), :]


def sketch(owner, before, record, after, weights, shares):
    lags, chans, width = weights.shape
    rows = before.shape[0] + record.shape[0]
    length = rows + after.shape[0]
    share = rows // shares
    return pl.pallas_call(
        sketch_kernel,
        grid=(STEP // 2,),
        in_specs=[SMEM, VMEM, VMEM, VMEM]
        + [pl.BlockSpec((lags // STEP, 2, chans, width), lambda i: (0, i, 0, 0))],
        out_specs=[VMEM] * shares,
        out_shape=[jax.ShapeDtypeStruct((share, width), F32)] * shares,
        scratch_shapes=[
            pltpu.VMEM((length, chans), BF16),
            pltpu.VMEM((length, chans), BF16),
            pltpu.VMEM((rows + STEP, width), F32),
            pltpu.VMEM((rows + STEP, width), F32),
            pltpu.VMEM((rows, width), F32),
        ],
        compiler_params=pltpu.CompilerParams(vmem_limit_bytes=58 * 2**20),
        cost_estimate=cost(
            6 * rows * lags * chans * width,
            4 * (lags * chans * width + length * chans + rows * width),
        ),
        name="sketch",
    )(owner.reshape(1), before, record, after, weights.reshape(lags // STEP, STEP, chans, width))


def turn_kernel(block_ref, high_ref, low_ref):
    high_ref[...], low_ref[...] = split(block_ref[...].T)


def turn(block):
    rows, chans = block.shape
    return pl.pallas_call(
        turn_kernel,
        in_specs=[VMEM],
        out_specs=[VMEM] * 2,
        out_shape=[jax.ShapeDtypeStruct((chans, rows), BF16)] * 2,
        compiler_params=pltpu.CompilerParams(vmem_limit_bytes=12 * 2**20),
        cost_estimate=cost(0, 8 * rows * chans),
        name="turn",
    )(block)


def assemble_kernel(rim, bits_ref, own_ref, got_ref, out_ref, gram_ref):
    pieces, share, width = own_ref.shape
    blocks = pieces // 2
    low, high = bits_ref[0], bits_ref[1]

    def place(first_ref, second_ref):
        for b in range(blocks):
            for q in range(2):
                owner = 2 * jnp.bitwise_xor(high, q)
                first = pl.multiple_of(owner * share, 8)
                out_ref[b, pl.ds(first, share), :] = first_ref[2 * b + q]
                out_ref[b, pl.ds(pl.multiple_of(first + share, 8), share), :] = second_ref[blocks * q + b]

    @pl.when(low == 0)
    def _():
        place(own_ref, got_ref)

    @pl.when(low == 1)
    def _():
        place(got_ref, own_ref)

    gram = jnp.zeros((width, width), F32)
    for b in range(blocks):
        value = out_ref[b, rim:, :]
        gram = gram + lax.dot_general(
            value, value, (((0,), (0,)), ((), ())), precision=HIGHEST, preferred_element_type=F32
        )
    gram_ref[...] = gram


def assemble(bits, own, got, rim, shares):
    pieces, share, width = own.shape
    blocks = pieces // 2
    return pl.pallas_call(
        functools.partial(assemble_kernel, rim),
        in_specs=[SMEM, VMEM, VMEM],
        out_specs=[VMEM] * 2,
        out_shape=[
            jax.ShapeDtypeStruct((blocks, shares * share, width), F32),
            jax.ShapeDtypeStruct((width, width), F32),
        ],
        compiler_params=pltpu.CompilerParams(vmem_limit_bytes=20 * 2**20),
        cost_estimate=cost(
            12 * blocks * shares * share * width * width, 8 * blocks * shares * share * width
        ),
        name="assemble",
    )(bits, own, got)


def factor_kernel(gram_ref, out_ref):
    size = gram_ref.shape[0]
    tile = 8
    groups = size // tile
    row_of = lax.broadcasted_iota(jnp.int32, (tile, size), 0)
    col_of = lax.broadcasted_iota(jnp.int32, (tile, size), 1)
    g = [gram_ref[q * tile : (q + 1) * tile, :] for q in range(groups)]
    x = [jnp.where(col_of == row_of + q * tile, 1.0, 0.0).astype(F32) for q in range(groups)]
    for p in range(groups):
        pivots = jnp.ones((tile, 1), F32)
        for r in range(tile):
            j = p * tile + r
            g_row = g[p][r : r + 1, :]
            x_row = x[p][r : r + 1, :]
            pivot = g_row[:, j : j + 1]
            pivots = jnp.where(row_of[:, :1] == r, pivot, pivots)
            inverse = 1.0 / pivot
            g_row = g_row * inverse
            x_row = x_row * inverse
            for q in range(p, groups):
                column = g[q][:, j : j + 1]
                if q == p:
                    column = jnp.where(row_of[:, :1] > r, column, 0.0)
                g[q] = g[q] - column * g_row
                x[q] = x[q] - column * x_row
        out_ref[p * tile : (p + 1) * tile, :] = x[p] * (1.0 / jnp.sqrt(pivots))


def factor(gram):
    return pl.pallas_call(
        factor_kernel,
        in_specs=[VMEM],
        out_specs=VMEM,
        out_shape=jax.ShapeDtypeStruct(gram.shape, F32),
        compiler_params=pltpu.CompilerParams(vmem_limit_bytes=8 * 2**20),
        cost_estimate=cost(9 * 10**9, 2**17),
        name="factor",
    )(gram)


def lagged_kernel(places, lag_ref, *refs):
    count = len(places)
    highs, lows, (sketch_ref, out_ref) = refs[:count], refs[count : 2 * count], refs[2 * count :]
    width = out_ref.shape[2]
    rim = places[0][2]
    start = rim - (lag_ref[0] + 2 * pl.program_id(0))
    total = jnp.zeros((out_ref.shape[1], 2 * width), F32)
    for (block, first, _), high, low in zip(places, highs, lows):
        rows = high.shape[1]
        moved = jnp.concatenate(
            [
                sketch_ref[block, pl.ds(start + first, rows), :],
                sketch_ref[block, pl.ds(start + first - 1, rows), :],
            ],
            axis=1,
        )
        moved_high, moved_low = split(moved)
        total = total + three(high[...], low[...], moved_high, moved_low)
    out_ref[0] = total[:, :width]
    out_ref[1] = total[:, width:]


def lagged(lag, turned, places, sketches, lags):
    blocks, length, width = sketches.shape
    chans = turned[0][0].shape[0]
    rows = sum(h.shape[1] for h, _ in turned)
    return pl.pallas_call(
        functools.partial(lagged_kernel, places),
        grid=(lags // 2,),
        in_specs=[SMEM] + [VMEM] * (2 * len(turned) + 1),
        out_specs=pl.BlockSpec((2, chans, width), lambda i: (i, 0, 0)),
        out_shape=jax.ShapeDtypeStruct((lags, chans, width), F32),
        compiler_params=pltpu.CompilerParams(vmem_limit_bytes=28 * 2**20),
        cost_estimate=cost(
            6 * rows * chans * lags * width,
            4 * (rows * chans + lags * chans * width + blocks * length * width),
        ),
        name="lagged",
    )(lag.reshape(1), *[h for h, _ in turned], *[l for _, l in turned], sketches)


def finish_kernel(chunks, inverse_ref, kept_ref, *refs):
    *received, out_ref = refs
    lags, chans, width = out_ref.shape
    size = lags // chunks
    inverse_high, inverse_low = split(inverse_ref[...].T)
    for n in range(chunks):
        part = slice(n * size, (n + 1) * size)
        total = kept_ref[part]
        for ref in received[n::chunks]:
            total = total + ref[...]
        high, low = split(total.reshape(size * chans, width))
        out_ref[part] = three(high, low, inverse_high, inverse_low).reshape(size, chans, width)


def finish(inverse, kept, received, chunks):
    lags, chans, width = kept.shape
    return pl.pallas_call(
        functools.partial(finish_kernel, chunks),
        in_specs=[VMEM] * (2 + len(received)),
        out_specs=VMEM,
        out_shape=jax.ShapeDtypeStruct(kept.shape, F32),
        compiler_params=pltpu.CompilerParams(vmem_limit_bytes=28 * 2**20),
        cost_estimate=cost(6 * lags * chans * width * width, 12 * lags * chans * width),
        name="finish",
    )(inverse, kept, *received)


def on_device(record, test_matrix):
    rows, _ = record.shape
    lags, _, _ = test_matrix.shape
    n_time = lax.axis_size("tm")
    n_chan = lax.axis_size("chan")
    here = lax.axis_index("tm")
    mine = lax.axis_index("chan")
    half = n_time // 2
    mids = n_time // 4
    per = lags // n_time
    rim = lags

    def to(block, target, axis="tm"):
        count = lax.axis_size(axis)
        route = [(i, target(i)) for i in range(count) if 0 <= target(i) < count]
        return lax.ppermute(block, axis, route)

    def to_both(block, target):
        route = []
        for t in range(n_time):
            for c in range(n_chan):
                a, b = target(t, c)
                route.append((t * n_chan + c, a * n_chan + b))
        return lax.ppermute(block, ("tm", "chan"), route)

    def beside(t):
        return t ^ 1

    def across(t):
        return (t + half) % n_time

    before = to(record[rows - rim :], lambda i: i + 1)
    after = to(record[:rim], lambda i: i - 1)
    cut = [0, rows // 2, rows]
    parts = [record[a:b] for a, b in zip(cut, cut[1:])]
    beside_record = to(record, beside)
    across_parts = [to(part, across) for part in parts]
    both_parts = [to(part, beside) for part in across_parts]

    shares = sketch(mine, before, record, after, test_matrix, n_chan)
    share = shares[0].shape[0]
    own = shares[0]
    for s in range(1, n_chan):
        own = own + to(shares[s], lambda i: (i + s) % n_chan, "chan")
    row = mine * share + lax.broadcasted_iota(jnp.int32, (share, 1), 0)
    own = jnp.where((row >= rim) | (here > 0), own, 0.0)[None]

    def even(c):
        return c % 2 == 0

    got = to_both(own, lambda t, c: (t, c ^ 2) if even(c) else (across(t), c))
    own = jnp.concatenate([own, got], axis=0)
    got = to_both(own, lambda t, c: (across(t), c) if even(c) else (beside(t), c))
    own = jnp.concatenate([own, got], axis=0)
    got = to_both(own, lambda t, c: (beside(t), c) if even(c) else (t, c ^ 2))
    own = jnp.concatenate([own, got], axis=0)
    got = to(own, lambda i: i ^ 1, "chan")
    sketches, gram = assemble(jnp.stack([mine % 2, mine // 2]), own, got, rim, n_chan)
    distance = 2
    while distance < half:
        gram = gram + to(gram, lambda i: i ^ distance)
        distance *= 2

    turned = [turn(record)]
    turned += [turn(p) for p in across_parts]
    turned += [turn(beside_record)]
    turned += [turn(p) for p in both_parts]
    places = [(0, 0, rim)] + [(1, a, rim) for a in cut[:-1]] + [(2, 0, rim)] + [(3, a, rim) for a in cut[:-1]]

    middle = (here % half) // 2
    outer = here - 2 * middle

    def owner_lag(step):
        return (outer + 2 * ((middle + step) % mids)) * per

    chunks = 2 if per % 4 == 0 else 1
    size = per // chunks
    received = []
    for s in range(1, mids):
        def route(i):
            m = (i % half) // 2
            return i - 2 * m + 2 * ((m + s) % mids)

        for n in range(chunks):
            part = lagged(owner_lag(s) + n * size, turned, places, sketches, size)
            received.append(to(part, route))
    kept = lagged(owner_lag(0), turned, places, sketches, per)
    inverse = factor(gram)

    def whitened(x):
        return lax.dot_general(
            x, inverse, (((x.ndim - 1,), (1,)), ((), ())), precision=HIGHEST, preferred_element_type=F32
        )

    basis = whitened(sketches[0, rim:]) * jnp.sqrt(F32(rows * n_time))
    return basis, finish(inverse, kept, received, chunks)


def solution(mesh):
    return jax.shard_map(
        on_device,
        mesh=mesh,
        in_specs=(P("tm", "chan"), P(None, "chan", None)),
        out_specs=(P("tm", None), P("tm", "chan", None)),
        check_vma=False,
    )
```

profile of v0, /device:TPU:0, one launch (start us, length us, event | category | flops | bytes accessed | tf_op | source)
XLA Modules:
  0.0 179.2 jit_solution(14714397886990571943)
XLA Ops:
  0.6 0.9 fusion.4
  1.5 4.9 %collective-permute-start = (f32[64,256]{1,0:T(8,128)S(1)}, f32[64,256]{1,0:T(8,128)S(1)}, u32[]{:S(2)}, u32[]{:S(2)}) collective-permute-start(f32[64,256]{1,0:T(8,128)S(1)} %get-tuple-element.41), channel_id=1, source_target_pairs={{0,4},{4,8},{8,12},{12,16},{16,20},{20,24},{24,28},{1,5},{5,9},{9,... | collective-permute-start | bytes 196616 | tf_op jit(solution)/shard_map/ppermute | solution.py:289
  6.4 1.3 collective-permute-start.1
  7.7 0.6 collective-permute-done.before_ref
  8.3 4.3 %collective-permute-done.1.after_ref = f32[64,256]{1,0:T(8,128)S(1)} collective-permute-done((f32[64,256]{1,0:T(8,128)S(1)}, f32[64,256]{1,0:T(8,128)S(1)}, u32[]{:S(2)}, u32[]{:S(2)}) %collective-permute-start.1) | collective-permute-done | bytes 65568 | tf_op jit(solution)/shard_map/ppermute | solution.py:289
  12.6 0.0 copy-done.5
  12.6 0.6 copy-done.6
  13.2 19.3 %sketch.1 = (f32[272,128]{1,0:T(8,128)}, f32[272,128]{1,0:T(8,128)}, f32[272,128]{1,0:T(8,128)}, f32[272,128]{1,0:T(8,128)}) custom-call(s32[1]{0:T(128)} %bitcast.2.owner_ref, f32[64,256]{1,0:T(8,128)} %copy-done.5, f32[1024,256]{1,0:T(8,128)} %block_ref.1, f32[64,256]{1,0:T(8,128)} %copy-done.6, f32[4,16,256,128]{3,2,1,0:T(8,128)} %bitcast.13), custom_call_target="tpu_custom_call" | custom-call | flops 13690208256 | bytes 10125312 | tf_op jit(solution)/shard_map/sketch/pallas_call | solution.py:77
  32.4 0.0 collective-permute-start.2
  32.4 1.5 collective-permute-start.3
  34.0 1.4 collective-permute-start.4
  35.4 2.6 %collective-permute-done.2 = f32[272,128]{1,0:T(8,128)S(1)} collective-permute-done((f32[272,128]{1,0:T(8,128)}, f32[272,128]{1,0:T(8,128)S(1)}, u32[]{:S(2)}, u32[]{:S(2)}) %collective-permute-start.2) | collective-permute-done | bytes 139296 | tf_op jit(solution)/shard_map/ppermute | solution.py:289
  38.0 1.2 collective-permute-done.3
  39.2 1.5 collective-permute-done.4
  40.7 1.0 select_bitcast_fusion
  41.8 0.6 collective-permute-start.5
  42.3 4.5 %collective-permute-done.5 = f32[1,272,128]{2,1,0:T(8,128)S(1)} collective-permute-done((f32[1,272,128]{2,1,0:T(8,128)S(1)}, f32[1,272,128]{2,1,0:T(8,128)S(1)}, u32[]{:S(2)}, u32[]{:S(2)}) %collective-permute-start.5) | collective-permute-done | bytes 139296 | tf_op jit(solution)/shard_map/ppermute | solution.py:297
  46.9 2.7 %collective-permute-start.6 = (f32[2,272,128]{2,1,0:T(8,128)S(1)}, f32[2,272,128]{2,1,0:T(8,128)S(1)}, u32[]{:S(2)}, u32[]{:S(2)}) collective-permute-start(f32[2,272,128]{2,1,0:T(8,128)S(1)} %pad_maximum_fusion.2), channel_id=1, source_target_pairs={{0,16},{1,5},{2,18},{3,7},{4,20},{5,1},{6,22},{7,3},{8,24},{9,13},... | collective-permute-start | bytes 835592 | tf_op jit(solution)/shard_map/ppermute | solution.py:297
  49.6 7.8 %collective-permute-done.6 = f32[2,272,128]{2,1,0:T(8,128)S(1)} collective-permute-done((f32[2,272,128]{2,1,0:T(8,128)S(1)}, f32[2,272,128]{2,1,0:T(8,128)S(1)}, u32[]{:S(2)}, u32[]{:S(2)}) %collective-permute-start.6) | collective-permute-done | bytes 278560 | tf_op jit(solution)/shard_map/ppermute | solution.py:297
  57.4 0.1 pad_maximum_fusion.1
  57.5 0.0 copy-start
  57.5 2.5 %collective-permute-start.7 = (f32[4,272,128]{2,1,0:T(8,128)S(1)}, f32[4,272,128]{2,1,0:T(8,128)S(1)}, u32[]{:S(2)}, u32[]{:S(2)}) collective-permute-start(f32[4,272,128]{2,1,0:T(8,128)S(1)} %pad_maximum_fusion.1), channel_id=1, source_target_pairs={{0,4},{1,3},{2,6},{3,1},{4,0},{5,7},{6,2},{7,5},{8,12},{9,11},{10,... | collective-permute-start | bytes 1671176 | tf_op jit(solution)/shard_map/ppermute | solution.py:297
  60.0 7.5 %collective-permute-done.7 = f32[4,272,128]{2,1,0:T(8,128)S(1)} collective-permute-done((f32[4,272,128]{2,1,0:T(8,128)S(1)}, f32[4,272,128]{2,1,0:T(8,128)S(1)}, u32[]{:S(2)}, u32[]{:S(2)}) %collective-permute-start.7) | collective-permute-done | bytes 557088 | tf_op jit(solution)/shard_map/ppermute | solution.py:297
  67.5 0.1 pad_maximum_fusion.own_ref
  67.6 0.1 collective-permute-start.8
  67.7 0.0 copy-done
  67.7 0.1 fusion.3
  67.8 0.1 collective-permute-start.10
  67.8 2.9 %collective-permute-start.11 = (f32[512,256]{1,0:T(8,128)S(1)}, f32[512,256]{1,0:T(8,128)}, u32[]{:S(2)}, u32[]{:S(2)}) collective-permute-start(f32[512,256]{1,0:T(8,128)S(1)} %get-tuple-element.38), channel_id=1, source_target_pairs={{0,16},{4,20},{8,24},{12,28},{16,0},{20,4},{24,8},{28,12},{1,17},{... | collective-permute-start | bytes 1572872 | tf_op jit(solution)/shard_map/ppermute | solution.py:289
  70.8 2.0 %collective-permute-start.12 = (f32[1024,256]{1,0:T(8,128)S(1)}, f32[1024,256]{1,0:T(8,128)S(1)}, u32[]{:S(2)}, u32[]{:S(2)}) collective-permute-start(f32[1024,256]{1,0:T(8,128)S(1)} %copy-done), channel_id=1, source_target_pairs={{0,4},{4,0},{8,12},{12,8},{16,20},{20,16},{24,28},{28,24},{1,5},{5... | collective-permute-start | bytes 3145736 | tf_op jit(solution)/shard_map/ppermute | solution.py:289
  72.8 33.3 %collective-permute-done.10.block_ref = f32[512,256]{1,0:T(8,128)} collective-permute-done((f32[512,256]{1,0:T(8,128)S(1)}, f32[512,256]{1,0:T(8,128)}, u32[]{:S(2)}, u32[]{:S(2)}) %collective-permute-start.10) | collective-permute-done | bytes 524320 | tf_op jit(solution)/shard_map/ppermute | solution.py:289
  106.1 0.0 collective-permute-start.13
  106.1 10.8 %collective-permute-done.11.block_ref = f32[512,256]{1,0:T(8,128)} collective-permute-done((f32[512,256]{1,0:T(8,128)S(1)}, f32[512,256]{1,0:T(8,128)}, u32[]{:S(2)}, u32[]{:S(2)}) %collective-permute-start.11) | collective-permute-done | bytes 524320 | tf_op jit(solution)/shard_map/ppermute | solution.py:289
  116.8 0.4 collective-permute-start.14
  117.3 0.4 turn.6
  117.6 0.0 copy-start.1
  117.7 0.8 copy-done.1
  118.4 0.8 copy-done.3
  119.2 0.1 pad_add_fusion.bits_ref
  119.3 1.2 turn.7
  120.6 1.2 turn.8
  121.8 0.0 collective-permute-done.13.block_ref
  121.8 1.2 turn.10
  123.1 7.6 %collective-permute-done.14.block_ref = f32[512,256]{1,0:T(8,128)} collective-permute-done((f32[512,256]{1,0:T(8,128)}, f32[512,256]{1,0:T(8,128)}, u32[]{:S(2)}, u32[]{:S(2)}) %collective-permute-start.14) | collective-permute-done | bytes 524320 | tf_op jit(solution)/shard_map/ppermute | solution.py:289
  130.6 1.2 turn.11
  131.9 0.0 collective-permute-done.12.block_ref
  131.9 0.4 turn.9
  132.3 0.0 copy-start.2
  132.3 0.0 copy-start.4
  132.3 0.0 collective-permute-done.8.got_ref
  132.3 3.7 %assemble.1 = (f32[4,1088,128]{2,1,0:T(8,128)S(1)}, f32[128,128]{1,0:T(8,128)S(1)}) custom-call(s32[2]{0:T(128)S(1)} %pad_add_fusion.bits_ref, f32[8,272,128]{2,1,0:T(8,128)S(1)} %pad_maximum_fusion.own_ref, f32[8,272,128]{2,1,0:T(8,128)} %collective-permute-done.8.got_ref), custom_call_target="tpu_custom_call" | custom-call | flops 855638016 | bytes 4456448 | tf_op jit(solution)/shard_map/assemble/pallas_call | solution.py:150
  136.0 0.0 copy-done.2
  136.1 4.0 %lagged.5 = f32[4,256,128]{2,1,0:T(8,128)S(1)} custom-call(s32[1]{0:T(128)} %bitcast.8.lag_ref, bf16[256,1024]{1,0:T(8,128)(2,1)S(1)} %copy-done.2, bf16[256,512]{1,0:T(8,128)(2,1)S(1)} %get-tuple-element.27.refs_1_, bf16[256,512]{1,0:T(8,128)(2,1)S(1)} %get-tuple-element.28.refs_2_, bf16[256,1024]{1,0:T(8,128)(2,1)S(1)} %get-tuple-element.29.refs_3_, ...), custom_call_target="tpu_custom_call" | custom-call | flops 3221225472 | bytes 6946816 | tf_op jit(solution)/shard_map/lagged/pallas_call | solution.py:232
  140.0 0.1 collective-permute-start.16
  140.1 4.0 %lagged.4 = f32[4,256,128]{2,1,0:T(8,128)S(1)} custom-call(s32[1]{0:T(128)} %bitcast.7.lag_ref, bf16[256,1024]{1,0:T(8,128)(2,1)S(1)} %copy-done.2, bf16[256,512]{1,0:T(8,128)(2,1)S(1)} %get-tuple-element.27.refs_1_, bf16[256,512]{1,0:T(8,128)(2,1)S(1)} %get-tuple-element.28.refs_2_, bf16[256,1024]{1,0:T(8,128)(2,1)S(1)} %get-tuple-element.29.refs_3_, ...), custom_call_target="tpu_custom_call" | custom-call | flops 3221225472 | bytes 6946816 | tf_op jit(solution)/shard_map/lagged/pallas_call | solution.py:232
  144.1 2.0 %collective-permute-start.15 = (f32[4,256,128]{2,1,0:T(8,128)S(1)}, f32[4,256,128]{2,1,0:T(8,128)S(1)}, u32[]{:S(2)}, u32[]{:S(2)}) collective-permute-start(f32[4,256,128]{2,1,0:T(8,128)S(1)} %lagged.4), channel_id=1, source_target_pairs={{0,8},{4,12},{8,0},{12,4},{16,24},{20,28},{24,16},{28,20},{1,9},{5... | collective-permute-start | bytes 1572872 | tf_op jit(solution)/shard_map/ppermute | solution.py:289
  146.1 0.1 collective-permute-start.9
  146.2 7.7 %lagged.3.kept_ref = f32[8,256,128]{2,1,0:T(8,128)S(1)} custom-call(s32[1]{0:T(128)} %bitcast.6.lag_ref, bf16[256,1024]{1,0:T(8,128)(2,1)S(1)} %copy-done.2, bf16[256,512]{1,0:T(8,128)(2,1)S(1)} %get-tuple-element.27.refs_1_, bf16[256,512]{1,0:T(8,128)(2,1)S(1)} %get-tuple-element.28.refs_2_, bf16[256,1024]{1,0:T(8,128)(2,1)S(1)} %get-tuple-element.29.refs_3_, ...), custom_call_target="tpu_custom_call" | custom-call | flops 6442450944 | bytes 7471104 | tf_op jit(solution)/shard_map/lagged/pallas_call | solution.py:232
  154.0 11.4 %collective-permute-done.9 = f32[128,128]{1,0:T(8,128)S(1)} collective-permute-done((f32[128,128]{1,0:T(8,128)S(1)}, f32[128,128]{1,0:T(8,128)S(1)}, u32[]{:S(2)}, u32[]{:S(2)}) %collective-permute-start.9) | collective-permute-done | bytes 65568 | tf_op jit(solution)/shard_map/ppermute | solution.py:289
  165.4 10.8 %factor.1.inverse_ref = f32[128,128]{1,0:T(8,128)S(1)} custom-call(f32[128,128]{1,0:T(8,128)S(1)} %add.59.gram_ref), custom_call_target="tpu_custom_call" | custom-call | flops 8999999488 | bytes 131072 | tf_op jit(solution)/shard_map/factor/pallas_call | solution.py:195
  176.2 1.4 convolution_multiply_fusion
  177.6 0.0 collective-permute-done.16.refs_1_
  177.6 0.0 collective-permute-done.15.refs_0_
  177.6 1.6 finish.1
  (7 shorter events, 0.0 us)
Async XLA Ops:
  1.5 6.8 %collective-permute-start = (f32[64,256]{1,0:T(8,128)S(1)}, f32[64,256]{1,0:T(8,128)S(1)}, u32[]{:S(2)}, u32[]{:S(2)}) collective-permute-start(f32[64,256]{1,0:T(8,128)S(1)} %get-tuple-element.41), channel_id=1, source_target_pairs={{0,4},{4,8},{8,12},{12,16},{16,20},{20,24},{24,28},{1,5},{5,9},{9,... | collective-permute-start | bytes 196616 | tf_op jit(solution)/shard_map/ppermute | solution.py:289
  6.4 6.2 %collective-permute-start.1 = (f32[64,256]{1,0:T(8,128)S(1)}, f32[64,256]{1,0:T(8,128)S(1)}, u32[]{:S(2)}, u32[]{:S(2)}) collective-permute-start(f32[64,256]{1,0:T(8,128)S(1)} %get-tuple-element.40), channel_id=1, source_target_pairs={{4,0},{8,4},{12,8},{16,12},{20,16},{24,20},{28,24},{5,1},{9,5},{13... | collective-permute-start | bytes 196616 | tf_op jit(solution)/shard_map/ppermute | solution.py:289
  8.3 4.3 %copy-start.5 = (f32[64,256]{1,0:T(8,128)}, f32[64,256]{1,0:T(8,128)S(1)}, u32[]{:S(2)}) copy-start(f32[64,256]{1,0:T(8,128)S(1)} %collective-permute-done.before_ref) | copy-start | bytes 196612
  12.6 0.6 copy-start.6
  32.4 5.6 %collective-permute-start.2 = (f32[272,128]{1,0:T(8,128)}, f32[272,128]{1,0:T(8,128)S(1)}, u32[]{:S(2)}, u32[]{:S(2)}) collective-permute-start(f32[272,128]{1,0:T(8,128)} %get-tuple-element.21), channel_id=1, source_target_pairs={{0,1},{1,2},{2,3},{3,0},{4,5},{5,6},{6,7},{7,4},{8,9},{9,10},{10,1... | collective-permute-start | bytes 417800 | tf_op jit(solution)/shard_map/ppermute | solution.py:289
  32.4 6.8 %collective-permute-start.3 = (f32[272,128]{1,0:T(8,128)}, f32[272,128]{1,0:T(8,128)S(1)}, u32[]{:S(2)}, u32[]{:S(2)}) collective-permute-start(f32[272,128]{1,0:T(8,128)} %get-tuple-element.22), channel_id=1, source_target_pairs={{0,2},{1,3},{2,0},{3,1},{4,6},{5,7},{6,4},{7,5},{8,10},{9,11},{10,... | collective-permute-start | bytes 417800 | tf_op jit(solution)/shard_map/ppermute | solution.py:289
  34.0 6.8 %collective-permute-start.4 = (f32[272,128]{1,0:T(8,128)}, f32[272,128]{1,0:T(8,128)S(1)}, u32[]{:S(2)}, u32[]{:S(2)}) collective-permute-start(f32[272,128]{1,0:T(8,128)} %get-tuple-element.23), channel_id=1, source_target_pairs={{0,3},{1,0},{2,1},{3,2},{4,7},{5,4},{6,5},{7,6},{8,11},{9,8},{10,9... | collective-permute-start | bytes 417800 | tf_op jit(solution)/shard_map/ppermute | solution.py:289
  41.8 5.1 %collective-permute-start.5 = (f32[1,272,128]{2,1,0:T(8,128)S(1)}, f32[1,272,128]{2,1,0:T(8,128)S(1)}, u32[]{:S(2)}, u32[]{:S(2)}) collective-permute-start(f32[1,272,128]{2,1,0:T(8,128)S(1)} %select_bitcast_fusion), channel_id=1, source_target_pairs={{0,2},{1,17},{2,0},{3,19},{4,6},{5,21},{6,4},{7,23},{8,10},{9,25},... | collective-permute-start | bytes 417800 | tf_op jit(solution)/shard_map/ppermute | solution.py:297
  46.9 10.5 %collective-permute-start.6 = (f32[2,272,128]{2,1,0:T(8,128)S(1)}, f32[2,272,128]{2,1,0:T(8,128)S(1)}, u32[]{:S(2)}, u32[]{:S(2)}) collective-permute-start(f32[2,272,128]{2,1,0:T(8,128)S(1)} %pad_maximum_fusion.2), channel_id=1, source_target_pairs={{0,16},{1,5},{2,18},{3,7},{4,20},{5,1},{6,22},{7,3},{8,24},{9,13},... | collective-permute-start | bytes 835592 | tf_op jit(solution)/shard_map/ppermute | solution.py:297
  57.5 10.2 %copy-start = (f32[1024,256]{1,0:T(8,128)S(1)}, f32[1024,256]{1,0:T(8,128)}, u32[]{:S(2)}) copy-start(f32[1024,256]{1,0:T(8,128)} %block_ref.1) | copy-start | bytes 3145732
  57.5 10.0 %collective-permute-start.7 = (f32[4,272,128]{2,1,0:T(8,128)S(1)}, f32[4,272,128]{2,1,0:T(8,128)S(1)}, u32[]{:S(2)}, u32[]{:S(2)}) collective-permute-start(f32[4,272,128]{2,1,0:T(8,128)S(1)} %pad_maximum_fusion.1), channel_id=1, source_target_pairs={{0,4},{1,3},{2,6},{3,1},{4,0},{5,7},{6,2},{7,5},{8,12},{9,11},{10,... | collective-permute-start | bytes 1671176 | tf_op jit(solution)/shard_map/ppermute | solution.py:297
  67.6 64.7 %collective-permute-start.8 = (f32[8,272,128]{2,1,0:T(8,128)S(1)}, f32[8,272,128]{2,1,0:T(8,128)}, u32[]{:S(2)}, u32[]{:S(2)}) collective-permute-start(f32[8,272,128]{2,1,0:T(8,128)S(1)} %pad_maximum_fusion.own_ref), channel_id=1, source_target_pairs={{0,1},{1,0},{2,3},{3,2},{4,5},{5,4},{6,7},{7,6},{8,9},{9,8},{10,11... | collective-permute-start | bytes 3342344 | tf_op jit(solution)/shard_map/ppermute | solution.py:289
  67.8 38.3 %collective-permute-start.10 = (f32[512,256]{1,0:T(8,128)S(1)}, f32[512,256]{1,0:T(8,128)}, u32[]{:S(2)}, u32[]{:S(2)}) collective-permute-start(f32[512,256]{1,0:T(8,128)S(1)} %get-tuple-element.39), channel_id=1, source_target_pairs={{0,16},{4,20},{8,24},{12,28},{16,0},{20,4},{24,8},{28,12},{1,17},{... | collective-permute-start | bytes 1572872 | tf_op jit(solution)/shard_map/ppermute | solution.py:289
  67.8 49.0 %collective-permute-start.11 = (f32[512,256]{1,0:T(8,128)S(1)}, f32[512,256]{1,0:T(8,128)}, u32[]{:S(2)}, u32[]{:S(2)}) collective-permute-start(f32[512,256]{1,0:T(8,128)S(1)} %get-tuple-element.38), channel_id=1, source_target_pairs={{0,16},{4,20},{8,24},{12,28},{16,0},{20,4},{24,8},{28,12},{1,17},{... | collective-permute-start | bytes 1572872 | tf_op jit(solution)/shard_map/ppermute | solution.py:289
  70.8 61.1 %collective-permute-start.12 = (f32[1024,256]{1,0:T(8,128)S(1)}, f32[1024,256]{1,0:T(8,128)S(1)}, u32[]{:S(2)}, u32[]{:S(2)}) collective-permute-start(f32[1024,256]{1,0:T(8,128)S(1)} %copy-done), channel_id=1, source_target_pairs={{0,4},{4,0},{8,12},{12,8},{16,20},{20,16},{24,28},{28,24},{1,5},{5... | collective-permute-start | bytes 3145736 | tf_op jit(solution)/shard_map/ppermute | solution.py:289
  106.1 15.7 %collective-permute-start.13 = (f32[512,256]{1,0:T(8,128)}, f32[512,256]{1,0:T(8,128)}, u32[]{:S(2)}, u32[]{:S(2)}) collective-permute-start(f32[512,256]{1,0:T(8,128)} %collective-permute-done.10.block_ref), channel_id=1, source_target_pairs={{0,4},{4,0},{8,12},{12,8},{16,20},{20,16},{24,28},{28,24},{1,5},{5... | collective-permute-start | bytes 1572872 | tf_op jit(solution)/shard_map/ppermute | solution.py:289
  116.8 13.8 %collective-permute-start.14 = (f32[512,256]{1,0:T(8,128)}, f32[512,256]{1,0:T(8,128)}, u32[]{:S(2)}, u32[]{:S(2)}) collective-permute-start(f32[512,256]{1,0:T(8,128)} %collective-permute-done.11.block_ref), channel_id=1, source_target_pairs={{0,4},{4,0},{8,12},{12,8},{16,20},{20,16},{24,28},{28,24},{1,5},{5... | collective-permute-start | bytes 1572872 | tf_op jit(solution)/shard_map/ppermute | solution.py:289
  117.6 0.8 copy-start.1
  118.4 0.8 copy-start.3
  132.3 3.8 %copy-start.2 = (bf16[256,1024]{1,0:T(8,128)(2,1)S(1)}, bf16[256,1024]{1,0:T(8,128)(2,1)}, u32[]{:S(2)}) copy-start(bf16[256,1024]{1,0:T(8,128)(2,1)} %copy-done.1) | copy-start | bytes 1572868
  132.3 3.8 %copy-start.4 = (bf16[256,1024]{1,0:T(8,128)(2,1)S(1)}, bf16[256,1024]{1,0:T(8,128)(2,1)}, u32[]{:S(2)}) copy-start(bf16[256,1024]{1,0:T(8,128)(2,1)} %copy-done.3) | copy-start | bytes 1572868
  140.0 37.5 %collective-permute-start.16 = (f32[4,256,128]{2,1,0:T(8,128)S(1)}, f32[4,256,128]{2,1,0:T(8,128)S(1)}, u32[]{:S(2)}, u32[]{:S(2)}) collective-permute-start(f32[4,256,128]{2,1,0:T(8,128)S(1)} %lagged.5), channel_id=1, source_target_pairs={{0,8},{4,12},{8,0},{12,4},{16,24},{20,28},{24,16},{28,20},{1,9},{5... | collective-permute-start | bytes 1572872 | tf_op jit(solution)/shard_map/ppermute | solution.py:289
  144.1 33.4 %collective-permute-start.15 = (f32[4,256,128]{2,1,0:T(8,128)S(1)}, f32[4,256,128]{2,1,0:T(8,128)S(1)}, u32[]{:S(2)}, u32[]{:S(2)}) collective-permute-start(f32[4,256,128]{2,1,0:T(8,128)S(1)} %lagged.4), channel_id=1, source_target_pairs={{0,8},{4,12},{8,0},{12,4},{16,24},{20,28},{24,16},{28,20},{1,9},{5... | collective-permute-start | bytes 1572872 | tf_op jit(solution)/shard_map/ppermute | solution.py:289
  146.1 19.3 %collective-permute-start.9 = (f32[128,128]{1,0:T(8,128)S(1)}, f32[128,128]{1,0:T(8,128)S(1)}, u32[]{:S(2)}, u32[]{:S(2)}) collective-permute-start(f32[128,128]{1,0:T(8,128)S(1)} %get-tuple-element.25), channel_id=1, source_target_pairs={{0,8},{4,12},{8,0},{12,4},{16,24},{20,28},{24,16},{28,20},{1,9},{5... | collective-permute-start | bytes 196616 | tf_op jit(solution)/shard_map/ppermute | solution.py:289
where the time goes:
time: 180 us; the launch traced here: 179 us
  waiting for transfers between devices  93.1 us (52%)
  Pallas kernels  56.8 us (32%)
  starting transfers between devices  22.6 us (13%)
  local copies, waits for them, and re-layouts  3.17 us (2%)
    ppermute x14, waiting for transfers between devices, to(): return lax.ppermute(block, axis, route)  73.2 us
    ppermute x3, waiting for transfers between devices, to_both(): return lax.ppermute(block, ('tm', 'chan'), route)  19.9 us
    pallas_call x1, Pallas kernels, sketch(): pl.pallas_call(sketch_kernel, grid=(STEP // 2,), in_specs=[SMEM, VMEM, VM...  19.3 us
    ppermute x14, starting transfers between devices, to(): return lax.ppermute(block, axis, route)  16.8 us
    pallas_call x3, Pallas kernels, lagged(): pl.pallas_call(functools.partial(lagged_kernel, places), grid=(lags // 2,...  15.7 us
    pallas_call x1, Pallas kernels, factor(): pl.pallas_call(factor_kernel, in_specs=[VMEM], out_specs=VMEM, out_shape=...  10.8 us
    ppermute x3, starting transfers between devices, to_both(): return lax.ppermute(block, ('tm', 'chan'), route)  5.75 us
    pallas_call x6, Pallas kernels, turn(): pl.pallas_call(turn_kernel, in_specs=[VMEM], out_specs=[VMEM] * 2, out_sh...  5.71 us
  transfers between devices with their start and end apart: 17, of which 12 were waited for; matrix products, arithmetic and copies ran while one was open for 1% of the time, Pallas kernels for 16%

commit v1 on v0

--- a/solution.py
+++ b/solution.py
@@ -31,7 +31,7 @@
 
 
 def sketch_kernel(owner_ref, before_ref, record_ref, after_ref, weight_ref, *refs):
-    *outs, high, low, even, odd, total = refs
+    keep_ref, give_ref, high, low, even, odd, total = refs
     pair = pl.program_id(0)
     rows, width = total.shape
     groups = weight_ref.shape[0]
@@ -63,10 +63,11 @@
 
     @pl.when(pair == pl.num_programs(0) - 1)
     def _():
-        share = rows // len(outs)
-        for s, out in enumerate(outs):
-            owner = lax.rem(owner_ref[0] + s, len(outs))
-            out[...] = total[pl.ds(pl.multiple_of(owner * share, 8), share), :]
+        share = keep_ref.shape[1]
+        for ref, flip in ((keep_ref, 0), (give_ref, 1)):
+            for n in range(2):
+                owner = jnp.bitwise_xor(owner_ref[0], 2 * n + flip)
+                ref[n] = total[pl.ds(pl.multiple_of(owner * share, 8), share), :]
 
 
 def sketch(owner, before, record, after, weights, shares):
@@ -79,8 +80,8 @@
         grid=(STEP // 2,),
         in_specs=[SMEM, VMEM, VMEM, VMEM]
         + [pl.BlockSpec((lags // STEP, 2, chans, width), lambda i: (0, i, 0, 0))],
-        out_specs=[VMEM] * shares,
-        out_shape=[jax.ShapeDtypeStruct((share, width), F32)] * shares,
+        out_specs=[VMEM] * 2,
+        out_shape=[jax.ShapeDtypeStruct((2, share, width), F32)] * 2,
         scratch_shapes=[
             pltpu.VMEM((length, chans), BF16),
             pltpu.VMEM((length, chans), BF16),
@@ -114,8 +115,8 @@
     )(block)
 
 
-def assemble_kernel(rim, bits_ref, own_ref, got_ref, out_ref, gram_ref):
-    pieces, share, width = own_ref.shape
+def assemble_kernel(bits_ref, own_ref, got_ref, out_ref):
+    pieces, share, _ = own_ref.shape
     blocks = pieces // 2
     low, high = bits_ref[0], bits_ref[1]
 
@@ -135,32 +136,62 @@
     def _():
         place(got_ref, own_ref)
 
-    gram = jnp.zeros((width, width), F32)
-    for b in range(blocks):
-        value = out_ref[b, rim:, :]
-        gram = gram + lax.dot_general(
+
+def assemble(bits, own, got, shares):
+    pieces, share, width = own.shape
+    blocks = pieces // 2
+    return pl.pallas_call(
+        assemble_kernel,
+        in_specs=[SMEM, VMEM, VMEM],
+        out_specs=VMEM,
+        out_shape=jax.ShapeDtypeStruct((blocks, shares * share, width), F32),
+        compiler_params=pltpu.CompilerParams(vmem_limit_bytes=20 * 2**20),
+        cost_estimate=cost(0, 8 * blocks * shares * share * width),
+        name="assemble",
+    )(bits, own, got)
+
+
+def gram_kernel(rim, bits_ref, own_ref, out_ref):
+    pieces, share, width = own_ref.shape
+    blocks = pieces // 2
+    low, high = bits_ref[0], bits_ref[1]
+    kept = lax.broadcasted_iota(jnp.int32, (share, width), 0) >= rim
+
+    def gram(value):
+        return lax.dot_general(
             value, value, (((0,), (0,)), ((), ())), precision=HIGHEST, preferred_element_type=F32
         )
-    gram_ref[...] = gram
-
-
-def assemble(bits, own, got, rim, shares):
+
+    @pl.when(low == 0)
+    def _():
+        halves = []
+        for q in range(2):
+            value = jnp.concatenate(
+                [jnp.where(kept | (high != q), own_ref[2 * b + q], 0.0) for b in range(blocks)], axis=0
+            )
+            halves.append(gram(value))
+        out_ref[...] = halves[0] + halves[1]
+
+    @pl.when(low == 1)
+    def _():
+        halves = []
+        for q in range(2):
+            value = jnp.concatenate([own_ref[blocks * q + b] for b in range(blocks)], axis=0)
+            halves.append(gram(value))
+        out_ref[...] = halves[0] + halves[1]
+
+
+def gram_of(bits, own, rim):
     pieces, share, width = own.shape
-    blocks = pieces // 2
-    return pl.pallas_call(
-        functools.partial(assemble_kernel, rim),
-        in_specs=[SMEM, VMEM, VMEM],
-        out_specs=[VMEM] * 2,
-        out_shape=[
-            jax.ShapeDtypeStruct((blocks, shares * share, width), F32),
-            jax.ShapeDtypeStruct((width, width), F32),
-        ],
+    return pl.pallas_call(
+        functools.partial(gram_kernel, rim),
+        in_specs=[SMEM, VMEM],
+        out_specs=VMEM,
+        out_shape=jax.ShapeDtypeStruct((width, width), F32),
         compiler_params=pltpu.CompilerParams(vmem_limit_bytes=20 * 2**20),
-        cost_estimate=cost(
-            12 * blocks * shares * share * width * width, 8 * blocks * shares * share * width
-        ),
-        name="assemble",
-    )(bits, own, got)
+        cost_estimate=cost(12 * pieces * share * width * width, 4 * pieces * share * width),
+        name="gram",
+    )(bits, own)
 
 
 def factor_kernel(gram_ref, out_ref):
@@ -235,7 +266,7 @@
         in_specs=[SMEM] + [VMEM] * (2 * len(turned) + 1),
         out_specs=pl.BlockSpec((2, chans, width), lambda i: (i, 0, 0)),
         out_shape=jax.ShapeDtypeStruct((lags, chans, width), F32),
-        compiler_params=pltpu.CompilerParams(vmem_limit_bytes=28 * 2**20),
+        compiler_params=pltpu.CompilerParams(vmem_limit_bytes=20 * 2**20),
         cost_estimate=cost(
             6 * rows * chans * lags * width,
             4 * (rows * chans + lags * chans * width + blocks * length * width),
@@ -265,7 +296,7 @@
         in_specs=[VMEM] * (2 + len(received)),
         out_specs=VMEM,
         out_shape=jax.ShapeDtypeStruct(kept.shape, F32),
-        compiler_params=pltpu.CompilerParams(vmem_limit_bytes=28 * 2**20),
+        compiler_params=pltpu.CompilerParams(vmem_limit_bytes=20 * 2**20),
         cost_estimate=cost(6 * lags * chans * width * width, 12 * lags * chans * width),
         name="finish",
     )(inverse, kept, *received)
@@ -304,19 +335,18 @@
 
     before = to(record[rows - rim :], lambda i: i + 1)
     after = to(record[:rim], lambda i: i - 1)
-    cut = [0, rows // 2, rows]
+    cut = [0, rows // 2, 3 * rows // 4, rows]
     parts = [record[a:b] for a, b in zip(cut, cut[1:])]
     beside_record = to(record, beside)
     across_parts = [to(part, across) for part in parts]
     both_parts = [to(part, beside) for part in across_parts]
 
-    shares = sketch(mine, before, record, after, test_matrix, n_chan)
-    share = shares[0].shape[0]
-    own = shares[0]
-    for s in range(1, n_chan):
-        own = own + to(shares[s], lambda i: (i + s) % n_chan, "chan")
-    row = mine * share + lax.broadcasted_iota(jnp.int32, (share, 1), 0)
-    own = jnp.where((row >= rim) | (here > 0), own, 0.0)[None]
+    keep, give = sketch(mine, before, record, after, test_matrix, n_chan)
+    share = keep.shape[1]
+    keep = keep + to(give, lambda i: i ^ 1, "chan")
+    own = keep[:1] + to(keep[1:], lambda i: i ^ 2, "chan")
+    row = mine * share + lax.broadcasted_iota(jnp.int32, (1, share, 1), 1)
+    own = jnp.where((row >= rim) | (here > 0), own, 0.0)
 
     def even(c):
         return c % 2 == 0
@@ -328,11 +358,14 @@
     got = to_both(own, lambda t, c: (beside(t), c) if even(c) else (t, c ^ 2))
     own = jnp.concatenate([own, got], axis=0)
     got = to(own, lambda i: i ^ 1, "chan")
-    sketches, gram = assemble(jnp.stack([mine % 2, mine // 2]), own, got, rim, n_chan)
+    bits = jnp.stack([mine % 2, mine // 2])
+    gram = gram_of(bits, own, rim)
     distance = 2
     while distance < half:
         gram = gram + to(gram, lambda i: i ^ distance)
         distance *= 2
+    gram = gram + to(gram, lambda i: i ^ 1, "chan")
+    sketches = assemble(bits, own, got, n_chan)
 
     turned = [turn(record)]
     turned += [turn(p) for p in across_parts]

time: 180 us -> 177 us (0.983)
  waiting for transfers between devices: 93.1 us -> 85.3 us
    ppermute x14 -> x16, waiting for transfers between devices: 73.2 us -> 54.8 us  [to(): return lax.ppermute(block, axis, route)]
    ppermute x3, waiting for transfers between devices: 19.9 us -> 30.5 us  [to_both(): return lax.ppermute(block, ('tm', 'chan'), route)]
    add x0 -> x2, other arithmetic: none -> 1.88 us  [the longest x1 0.99 us: on_device(): keep = keep + to(give, lambda i: i ^ 1, 'chan')]
    pallas_call x6 -> x8, Pallas kernels: 5.71 us -> 6.93 us  [turn(): pl.pallas_call(turn_kernel, in_specs=[VMEM], out_specs=[VMEM] * 2, out_sh...]
    pallas_call x1 -> x2, Pallas kernels: 3.73 us -> 2.68 us  [the longest x1 1.8 us: gram_of(): pl.pallas_call(functools.partial(gram_kernel, rim), in_specs=[SMEM, VMEM]...]
    ppermute x14 -> x16, starting transfers between devices: 16.8 us -> 16.6 us  [to(): return lax.ppermute(block, axis, route)]
  transfers between devices with their start and end apart: 17 -> 19, of which waited for: 12 -> 13; matrix products, arithmetic and copies ran while one was open for 1% -> 1% of each run, Pallas kernels for 16% -> 15%
where the time goes in v1:
time: 177 us; the launch traced here: 176 us
  waiting for transfers between devices  85.3 us (48%)
  Pallas kernels  57 us (32%)
  starting transfers between devices  24 us (14%)
  local copies, waits for them, and re-layouts  4.96 us (3%)
  other arithmetic  2.85 us (2%)
    ppermute x16, waiting for transfers between devices, to(): return lax.ppermute(block, axis, route)  54.8 us
    ppermute x3, waiting for transfers between devices, to_both(): return lax.ppermute(block, ('tm', 'chan'), route)  30.5 us
    pallas_call x1, Pallas kernels, sketch(): pl.pallas_call(sketch_kernel, grid=(STEP // 2,), in_specs=[SMEM, VMEM, VM...  19.2 us
    ppermute x16, starting transfers between devices, to(): return lax.ppermute(block, axis, route)  16.6 us
    pallas_call x3, Pallas kernels, lagged(): pl.pallas_call(functools.partial(lagged_kernel, places), grid=(lags // 2,...  15.7 us
    pallas_call x1, Pallas kernels, factor(): pl.pallas_call(factor_kernel, in_specs=[VMEM], out_specs=VMEM, out_shape=...  10.8 us
    ppermute x3, starting transfers between devices, to_both(): return lax.ppermute(block, ('tm', 'chan'), route)  7.36 us
    pallas_call x8, Pallas kernels, turn(): pl.pallas_call(turn_kernel, in_specs=[VMEM], out_specs=[VMEM] * 2, out_sh...  6.93 us
  transfers between devices with their start and end apart: 19, of which 13 were waited for; matrix products, arithmetic and copies ran while one was open for 1% of the time, Pallas kernels for 15%

profile of v1, /device:TPU:0, one launch (start us, length us, event | category | flops | bytes accessed | tf_op | source)
XLA Modules:
  0.0 176.4 jit_solution(8025093537660429502)
XLA Ops:
  0.6 0.9 fusion.3
  1.5 1.3 collective-permute-start.1
  2.8 5.5 %collective-permute-start = (f32[64,256]{1,0:T(8,128)S(1)}, f32[64,256]{1,0:T(8,128)S(1)}, u32[]{:S(2)}, u32[]{:S(2)}) collective-permute-start(f32[64,256]{1,0:T(8,128)S(1)} %get-tuple-element.41), channel_id=1, source_target_pairs={{0,4},{4,8},{8,12},{12,16},{16,20},{20,24},{24,28},{1,5},{5,9},{9,... | collective-permute-start | bytes 196616 | tf_op jit(solution)/shard_map/ppermute | solution.py:320
  8.3 0.3 collective-permute-done.1.after_ref
  8.6 1.7 collective-permute-done.before_ref
  10.4 0.6 copy-done.8
  11.0 19.2 %sketch.1 = (f32[2,272,128]{2,1,0:T(8,128)}, f32[2,272,128]{2,1,0:T(8,128)}) custom-call(s32[1]{0:T(128)} %bitcast.2.owner_ref, f32[64,256]{1,0:T(8,128)} %copy-done.8, f32[1024,256]{1,0:T(8,128)} %block_ref.1, f32[64,256]{1,0:T(8,128)} %copy-done.7, f32[4,16,256,128]{3,2,1,0:T(8,128)} %bitcast.11), custom_call_target="tpu_custom_call" | custom-call | flops 13690208256 | bytes 10125312 | tf_op jit(solution)/shard_map/sketch/pallas_call | solution.py:78
  30.2 0.0 collective-permute-start.2
  30.2 1.8 %collective-permute-done.2 = f32[2,272,128]{2,1,0:T(8,128)S(1)} collective-permute-done((f32[2,272,128]{2,1,0:T(8,128)}, f32[2,272,128]{2,1,0:T(8,128)S(1)}, u32[]{:S(2)}, u32[]{:S(2)}) %collective-permute-start.2) | collective-permute-done | bytes 278560 | tf_op jit(solution)/shard_map/ppermute | solution.py:320
  32.0 1.0 add.56
  33.0 2.0 %collective-permute-start.3 = (f32[1,272,128]{2,1,0:T(8,128)S(1)}, f32[1,272,128]{2,1,0:T(8,128)S(1)}, u32[]{:S(2)}, u32[]{:S(2)}) collective-permute-start(f32[1,272,128]{2,1,0:T(8,128)S(1)} %slice.33), channel_id=1, source_target_pairs={{0,2},{1,3},{2,0},{3,1},{4,6},{5,7},{6,4},{7,5},{8,10},{9,11},{10,... | collective-permute-start | bytes 417800 | tf_op jit(solution)/shard_map/ppermute | solution.py:320
  35.0 4.0 %collective-permute-done.3 = f32[1,272,128]{2,1,0:T(8,128)S(1)} collective-permute-done((f32[1,272,128]{2,1,0:T(8,128)S(1)}, f32[1,272,128]{2,1,0:T(8,128)S(1)}, u32[]{:S(2)}, u32[]{:S(2)}) %collective-permute-start.3) | collective-permute-done | bytes 139296 | tf_op jit(solution)/shard_map/ppermute | solution.py:320
  38.9 0.1 fusion
  39.1 1.8 %collective-permute-start.4 = (f32[1,272,128]{2,1,0:T(8,128)S(1)}, f32[1,272,128]{2,1,0:T(8,128)S(1)}, u32[]{:S(2)}, u32[]{:S(2)}) collective-permute-start(f32[1,272,128]{2,1,0:T(8,128)S(1)} %fusion), channel_id=1, source_target_pairs={{0,2},{1,17},{2,0},{3,19},{4,6},{5,21},{6,4},{7,23},{8,10},{9,25},... | collective-permute-start | bytes 417800 | tf_op jit(solution)/shard_map/ppermute | solution.py:328
  40.9 3.3 %collective-permute-done.4 = f32[1,272,128]{2,1,0:T(8,128)S(1)} collective-permute-done((f32[1,272,128]{2,1,0:T(8,128)S(1)}, f32[1,272,128]{2,1,0:T(8,128)S(1)}, u32[]{:S(2)}, u32[]{:S(2)}) %collective-permute-start.4) | collective-permute-done | bytes 139296 | tf_op jit(solution)/shard_map/ppermute | solution.py:328
  44.2 5.5 %collective-permute-start.5 = (f32[2,272,128]{2,1,0:T(8,128)S(1)}, f32[2,272,128]{2,1,0:T(8,128)S(1)}, u32[]{:S(2)}, u32[]{:S(2)}) collective-permute-start(f32[2,272,128]{2,1,0:T(8,128)S(1)} %pad_maximum_fusion.2), channel_id=1, source_target_pairs={{0,16},{1,5},{2,18},{3,7},{4,20},{5,1},{6,22},{7,3},{8,24},{9,13},... | collective-permute-start | bytes 835592 | tf_op jit(solution)/shard_map/ppermute | solution.py:328
  49.7 0.1 collective-permute-start.10
  49.8 27.2 %collective-permute-done.5 = f32[2,272,128]{2,1,0:T(8,128)S(1)} collective-permute-done((f32[2,272,128]{2,1,0:T(8,128)S(1)}, f32[2,272,128]{2,1,0:T(8,128)S(1)}, u32[]{:S(2)}, u32[]{:S(2)}) %collective-permute-start.5) | collective-permute-done | bytes 278560 | tf_op jit(solution)/shard_map/ppermute | solution.py:328
  77.0 0.1 pad_maximum_fusion.1
  77.1 0.1 collective-permute-start.6
  77.2 2.0 %collective-permute-start.13 = (f32[1024,256]{1,0:T(8,128)S(1)}, f32[1024,256]{1,0:T(8,128)}, u32[]{:S(2)}, u32[]{:S(2)}) collective-permute-start(f32[1024,256]{1,0:T(8,128)S(1)} %copy-done), channel_id=1, source_target_pairs={{0,4},{4,0},{8,12},{12,8},{16,20},{20,16},{24,28},{28,24},{1,5},{5... | collective-permute-start | bytes 3145736 | tf_op jit(solution)/shard_map/ppermute | solution.py:320
  79.2 0.8 fusion.2
  80.0 0.0 collective-permute-start.12
  80.0 2.9 %collective-permute-start.11 = (f32[256,256]{1,0:T(8,128)}, f32[256,256]{1,0:T(8,128)S(1)}, u32[]{:S(2)}, u32[]{:S(2)}) collective-permute-start(f32[256,256]{1,0:T(8,128)} %get-tuple-element.39), channel_id=1, source_target_pairs={{0,16},{4,20},{8,24},{12,28},{16,0},{20,4},{24,8},{28,12},{1,17},{... | collective-permute-start | bytes 786440 | tf_op jit(solution)/shard_map/ppermute | solution.py:320
  82.9 11.1 %collective-permute-done.10.block_ref = f32[512,256]{1,0:T(8,128)} collective-permute-done((f32[512,256]{1,0:T(8,128)S(1)}, f32[512,256]{1,0:T(8,128)}, u32[]{:S(2)}, u32[]{:S(2)}) %collective-permute-start.10) | collective-permute-done | bytes 524320 | tf_op jit(solution)/shard_map/ppermute | solution.py:320
  94.0 0.0 collective-permute-start.14
  94.0 0.1 pad_add_fusion.bits_ref
  94.1 0.0 collective-permute-done.6
  94.1 0.1 pad_maximum_fusion.own_ref
  94.2 1.8 %gram.1 = f32[128,128]{1,0:T(8,128)S(1)} custom-call(s32[2]{0:T(128)S(1)} %pad_add_fusion.bits_ref, f32[8,272,128]{2,1,0:T(8,128)S(1)} %pad_maximum_fusion.own_ref), custom_call_target="tpu_custom_call" | custom-call | flops 427819008 | bytes 1114112 | tf_op jit(solution)/shard_map/gram/pallas_call | solution.py:186
  96.0 0.6 collective-permute-start.8
  96.6 2.8 %collective-permute-done.12.block_ref = f32[256,256]{1,0:T(8,128)} collective-permute-done((f32[256,256]{1,0:T(8,128)}, f32[256,256]{1,0:T(8,128)}, u32[]{:S(2)}, u32[]{:S(2)}) %collective-permute-start.12) | collective-permute-done | bytes 262176 | tf_op jit(solution)/shard_map/ppermute | solution.py:320
  99.4 2.8 %collective-permute-done.11.block_ref = f32[256,256]{1,0:T(8,128)S(1)} collective-permute-done((f32[256,256]{1,0:T(8,128)}, f32[256,256]{1,0:T(8,128)S(1)}, u32[]{:S(2)}, u32[]{:S(2)}) %collective-permute-start.11) | collective-permute-done | bytes 262176 | tf_op jit(solution)/shard_map/ppermute | solution.py:320
  102.2 0.6 collective-permute-done.8
  102.8 0.1 collective-permute-start.15
  102.9 0.6 add.58
  103.6 14.0 %collective-permute-done.16.block_ref = f32[256,256]{1,0:T(8,128)S(1)} collective-permute-done((f32[256,256]{1,0:T(8,128)}, f32[256,256]{1,0:T(8,128)S(1)}, u32[]{:S(2)}, u32[]{:S(2)}) %collective-permute-start.16) | collective-permute-done | bytes 262176 | tf_op jit(solution)/shard_map/ppermute | solution.py:320
  117.6 0.7 copy-done.1
  118.3 0.4 turn.8
  118.7 0.0 copy-start.3
  118.7 0.8 copy-done.3
  119.5 0.8 copy-done.5
  120.2 1.1 turn.11
  121.4 0.1 turn.10
  121.5 1.2 turn.9
  122.8 0.1 turn.15
  122.9 1.1 turn.14
  124.0 1.2 turn.13
  125.3 1.6 turn.12
  126.9 0.9 add.59.gram_ref
  127.8 10.8 %factor.1.inverse_ref = f32[128,128]{1,0:T(8,128)S(1)} custom-call(f32[128,128]{1,0:T(8,128)S(1)} %add.59.gram_ref), custom_call_target="tpu_custom_call" | custom-call | flops 8999999488 | bytes 131072 | tf_op jit(solution)/shard_map/factor/pallas_call | solution.py:226
  138.6 0.0 copy-start.4
  138.6 0.0 copy-start.6
  138.6 0.9 assemble.1.refs_16_
  139.5 0.1 copy-done.4
  139.7 0.2 copy-done.6
  139.8 4.0 %lagged.5 = f32[4,256,128]{2,1,0:T(8,128)S(1)} custom-call(s32[1]{0:T(128)} %bitcast.7.lag_ref, bf16[256,1024]{1,0:T(8,128)(2,1)S(1)} %copy-done.4, bf16[256,512]{1,0:T(8,128)(2,1)S(1)} %get-tuple-element.23.refs_1_, bf16[256,256]{1,0:T(8,128)(2,1)S(1)} %get-tuple-element.24.refs_2_, bf16[256,256]{1,0:T(8,128)(2,1)S(1)} %get-tuple-element.25.refs_3_, ...), custom_call_target="tpu_custom_call" | custom-call | flops 3221225472 | bytes 6946816 | tf_op jit(solution)/shard_map/lagged/pallas_call | solution.py:263
  143.8 4.0 %lagged.4 = f32[4,256,128]{2,1,0:T(8,128)S(1)} custom-call(s32[1]{0:T(128)} %bitcast.6.lag_ref, bf16[256,1024]{1,0:T(8,128)(2,1)S(1)} %copy-done.4, bf16[256,512]{1,0:T(8,128)(2,1)S(1)} %get-tuple-element.23.refs_1_, bf16[256,256]{1,0:T(8,128)(2,1)S(1)} %get-tuple-element.24.refs_2_, bf16[256,256]{1,0:T(8,128)(2,1)S(1)} %get-tuple-element.25.refs_3_, ...), custom_call_target="tpu_custom_call" | custom-call | flops 3221225472 | bytes 6946816 | tf_op jit(solution)/shard_map/lagged/pallas_call | solution.py:263
  147.8 1.4 convolution_multiply_fusion
  149.2 2.0 %collective-permute-start.18 = (f32[4,256,128]{2,1,0:T(8,128)S(1)}, f32[4,256,128]{2,1,0:T(8,128)S(1)}, u32[]{:S(2)}, u32[]{:S(2)}) collective-permute-start(f32[4,256,128]{2,1,0:T(8,128)S(1)} %lagged.5), channel_id=1, source_target_pairs={{0,8},{4,12},{8,0},{12,4},{16,24},{20,28},{24,16},{28,20},{1,9},{5... | collective-permute-start | bytes 1572872 | tf_op jit(solution)/shard_map/ppermute | solution.py:320
  151.2 7.7 %lagged.3.kept_ref = f32[8,256,128]{2,1,0:T(8,128)S(1)} custom-call(s32[1]{0:T(128)} %bitcast.5.lag_ref, bf16[256,1024]{1,0:T(8,128)(2,1)S(1)} %copy-done.4, bf16[256,512]{1,0:T(8,128)(2,1)S(1)} %get-tuple-element.23.refs_1_, bf16[256,256]{1,0:T(8,128)(2,1)S(1)} %get-tuple-element.24.refs_2_, bf16[256,256]{1,0:T(8,128)(2,1)S(1)} %get-tuple-element.25.refs_3_, ...), custom_call_target="tpu_custom_call" | custom-call | flops 6442450944 | bytes 7471104 | tf_op jit(solution)/shard_map/lagged/pallas_call | solution.py:263
  158.9 5.0 %collective-permute-done.17.refs_0_ = f32[4,256,128]{2,1,0:T(8,128)S(1)} collective-permute-done((f32[4,256,128]{2,1,0:T(8,128)S(1)}, f32[4,256,128]{2,1,0:T(8,128)S(1)}, u32[]{:S(2)}, u32[]{:S(2)}) %collective-permute-start.17) | collective-permute-done | bytes 524320 | tf_op jit(solution)/shard_map/ppermute | solution.py:320
  164.0 10.8 %collective-permute-done.18.refs_1_ = f32[4,256,128]{2,1,0:T(8,128)S(1)} collective-permute-done((f32[4,256,128]{2,1,0:T(8,128)S(1)}, f32[4,256,128]{2,1,0:T(8,128)S(1)}, u32[]{:S(2)}, u32[]{:S(2)}) %collective-permute-start.18) | collective-permute-done | bytes 524320 | tf_op jit(solution)/shard_map/ppermute | solution.py:320
  174.7 1.6 finish.1
  (22 shorter events, 0.1 us)
Async XLA Ops:
  1.5 7.1 %collective-permute-start.1 = (f32[64,256]{1,0:T(8,128)S(1)}, f32[64,256]{1,0:T(8,128)S(1)}, u32[]{:S(2)}, u32[]{:S(2)}) collective-permute-start(f32[64,256]{1,0:T(8,128)S(1)} %get-tuple-element.40), channel_id=1, source_target_pairs={{4,0},{8,4},{12,8},{16,12},{20,16},{24,20},{28,24},{5,1},{9,5},{13... | collective-permute-start | bytes 196616 | tf_op jit(solution)/shard_map/ppermute | solution.py:320
  2.8 7.5 %collective-permute-start = (f32[64,256]{1,0:T(8,128)S(1)}, f32[64,256]{1,0:T(8,128)S(1)}, u32[]{:S(2)}, u32[]{:S(2)}) collective-permute-start(f32[64,256]{1,0:T(8,128)S(1)} %get-tuple-element.41), channel_id=1, source_target_pairs={{0,4},{4,8},{8,12},{12,16},{16,20},{20,24},{24,28},{1,5},{5,9},{9,... | collective-permute-start | bytes 196616 | tf_op jit(solution)/shard_map/ppermute | solution.py:320
  8.6 1.7 copy-start.7
  10.4 0.6 copy-start.8
  30.2 19.5 %copy-start = (f32[1024,256]{1,0:T(8,128)S(1)}, f32[1024,256]{1,0:T(8,128)}, u32[]{:S(2)}) copy-start(f32[1024,256]{1,0:T(8,128)} %block_ref.1) | copy-start | bytes 3145732
  30.2 1.8 %collective-permute-start.2 = (f32[2,272,128]{2,1,0:T(8,128)}, f32[2,272,128]{2,1,0:T(8,128)S(1)}, u32[]{:S(2)}, u32[]{:S(2)}) collective-permute-start(f32[2,272,128]{2,1,0:T(8,128)} %get-tuple-element.21), channel_id=1, source_target_pairs={{0,1},{1,0},{2,3},{3,2},{4,5},{5,4},{6,7},{7,6},{8,9},{9,8},{10,11... | collective-permute-start | bytes 835592 | tf_op jit(solution)/shard_map/ppermute | solution.py:320
  33.0 5.9 %collective-permute-start.3 = (f32[1,272,128]{2,1,0:T(8,128)S(1)}, f32[1,272,128]{2,1,0:T(8,128)S(1)}, u32[]{:S(2)}, u32[]{:S(2)}) collective-permute-start(f32[1,272,128]{2,1,0:T(8,128)S(1)} %slice.33), channel_id=1, source_target_pairs={{0,2},{1,3},{2,0},{3,1},{4,6},{5,7},{6,4},{7,5},{8,10},{9,11},{10,... | collective-permute-start | bytes 417800 | tf_op jit(solution)/shard_map/ppermute | solution.py:320
  39.1 5.1 %collective-permute-start.4 = (f32[1,272,128]{2,1,0:T(8,128)S(1)}, f32[1,272,128]{2,1,0:T(8,128)S(1)}, u32[]{:S(2)}, u32[]{:S(2)}) collective-permute-start(f32[1,272,128]{2,1,0:T(8,128)S(1)} %fusion), channel_id=1, source_target_pairs={{0,2},{1,17},{2,0},{3,19},{4,6},{5,21},{6,4},{7,23},{8,10},{9,25},... | collective-permute-start | bytes 417800 | tf_op jit(solution)/shard_map/ppermute | solution.py:328
  44.2 32.8 %collective-permute-start.5 = (f32[2,272,128]{2,1,0:T(8,128)S(1)}, f32[2,272,128]{2,1,0:T(8,128)S(1)}, u32[]{:S(2)}, u32[]{:S(2)}) collective-permute-start(f32[2,272,128]{2,1,0:T(8,128)S(1)} %pad_maximum_fusion.2), channel_id=1, source_target_pairs={{0,16},{1,5},{2,18},{3,7},{4,20},{5,1},{6,22},{7,3},{8,24},{9,13},... | collective-permute-start | bytes 835592 | tf_op jit(solution)/shard_map/ppermute | solution.py:328
  49.7 44.3 %collective-permute-start.10 = (f32[512,256]{1,0:T(8,128)S(1)}, f32[512,256]{1,0:T(8,128)}, u32[]{:S(2)}, u32[]{:S(2)}) collective-permute-start(f32[512,256]{1,0:T(8,128)S(1)} %slice.29), channel_id=1, source_target_pairs={{0,16},{4,20},{8,24},{12,28},{16,0},{20,4},{24,8},{28,12},{1,17},{... | collective-permute-start | bytes 1572872 | tf_op jit(solution)/shard_map/ppermute | solution.py:320
  77.1 17.0 %collective-permute-start.6 = (f32[4,272,128]{2,1,0:T(8,128)S(1)}, f32[4,272,128]{2,1,0:T(8,128)S(1)}, u32[]{:S(2)}, u32[]{:S(2)}) collective-permute-start(f32[4,272,128]{2,1,0:T(8,128)S(1)} %pad_maximum_fusion.1), channel_id=1, source_target_pairs={{0,4},{1,3},{2,6},{3,1},{4,0},{5,7},{6,2},{7,5},{8,12},{9,11},{10,... | collective-permute-start | bytes 1671176 | tf_op jit(solution)/shard_map/ppermute | solution.py:328
  77.2 48.1 %collective-permute-start.13 = (f32[1024,256]{1,0:T(8,128)S(1)}, f32[1024,256]{1,0:T(8,128)}, u32[]{:S(2)}, u32[]{:S(2)}) collective-permute-start(f32[1024,256]{1,0:T(8,128)S(1)} %copy-done), channel_id=1, source_target_pairs={{0,4},{4,0},{8,12},{12,8},{16,20},{20,16},{24,28},{28,24},{1,5},{5... | collective-permute-start | bytes 3145736 | tf_op jit(solution)/shard_map/ppermute | solution.py:320
  80.0 19.4 %collective-permute-start.12 = (f32[256,256]{1,0:T(8,128)}, f32[256,256]{1,0:T(8,128)}, u32[]{:S(2)}, u32[]{:S(2)}) collective-permute-start(f32[256,256]{1,0:T(8,128)} %get-tuple-element.38), channel_id=1, source_target_pairs={{0,16},{4,20},{8,24},{12,28},{16,0},{20,4},{24,8},{28,12},{1,17},{... | collective-permute-start | bytes 786440 | tf_op jit(solution)/shard_map/ppermute | solution.py:320
  80.0 22.2 %collective-permute-start.11 = (f32[256,256]{1,0:T(8,128)}, f32[256,256]{1,0:T(8,128)S(1)}, u32[]{:S(2)}, u32[]{:S(2)}) collective-permute-start(f32[256,256]{1,0:T(8,128)} %get-tuple-element.39), channel_id=1, source_target_pairs={{0,16},{4,20},{8,24},{12,28},{16,0},{20,4},{24,8},{28,12},{1,17},{... | collective-permute-start | bytes 786440 | tf_op jit(solution)/shard_map/ppermute | solution.py:320
  94.0 30.0 %collective-permute-start.14 = (f32[512,256]{1,0:T(8,128)}, f32[512,256]{1,0:T(8,128)}, u32[]{:S(2)}, u32[]{:S(2)}) collective-permute-start(f32[512,256]{1,0:T(8,128)} %collective-permute-done.10.block_ref), channel_id=1, source_target_pairs={{0,4},{4,0},{8,12},{12,8},{16,20},{20,16},{24,28},{28,24},{1,5},{5... | collective-permute-start | bytes 1572872 | tf_op jit(solution)/shard_map/ppermute | solution.py:320
  96.0 6.8 %collective-permute-start.8 = (f32[128,128]{1,0:T(8,128)S(1)}, f32[128,128]{1,0:T(8,128)S(1)}, u32[]{:S(2)}, u32[]{:S(2)}) collective-permute-start(f32[128,128]{1,0:T(8,128)S(1)} %gram.1), channel_id=1, source_target_pairs={{0,8},{4,12},{8,0},{12,4},{16,24},{20,28},{24,16},{28,20},{1,9},{5... | collective-permute-start | bytes 196616 | tf_op jit(solution)/shard_map/ppermute | solution.py:320
  99.4 18.2 %collective-permute-start.16 = (f32[256,256]{1,0:T(8,128)}, f32[256,256]{1,0:T(8,128)S(1)}, u32[]{:S(2)}, u32[]{:S(2)}) collective-permute-start(f32[256,256]{1,0:T(8,128)} %collective-permute-done.12.block_ref), channel_id=1, source_target_pairs={{0,4},{4,0},{8,12},{12,8},{16,20},{20,16},{24,28},{28,24},{1,5},{5... | collective-permute-start | bytes 786440 | tf_op jit(solution)/shard_map/ppermute | solution.py:320
  102.2 36.4 %collective-permute-start.7 = (f32[8,272,128]{2,1,0:T(8,128)S(1)}, f32[8,272,128]{2,1,0:T(8,128)S(1)}, u32[]{:S(2)}, u32[]{:S(2)}) collective-permute-start(f32[8,272,128]{2,1,0:T(8,128)S(1)} %pad_maximum_fusion.own_ref), channel_id=1, source_target_pairs={{0,1},{1,0},{2,3},{3,2},{4,5},{5,4},{6,7},{7,6},{8,9},{9,8},{10,11... | collective-permute-start | bytes 3342344 | tf_op jit(solution)/shard_map/ppermute | solution.py:320
  102.8 20.1 %collective-permute-start.15 = (f32[256,256]{1,0:T(8,128)S(1)}, f32[256,256]{1,0:T(8,128)}, u32[]{:S(2)}, u32[]{:S(2)}) collective-permute-start(f32[256,256]{1,0:T(8,128)S(1)} %collective-permute-done.11.block_ref), channel_id=1, source_target_pairs={{0,4},{4,0},{8,12},{12,8},{16,20},{20,16},{24,28},{28,24},{1,5},{5... | collective-permute-start | bytes 786440 | tf_op jit(solution)/shard_map/ppermute | solution.py:320
  117.6 0.7 copy-start.1
  118.3 8.6 %collective-permute-start.9 = (f32[128,128]{1,0:T(8,128)}, f32[128,128]{1,0:T(8,128)}, u32[]{:S(2)}, u32[]{:S(2)}) collective-permute-start(f32[128,128]{1,0:T(8,128)} %add.58), channel_id=1, source_target_pairs={{0,1},{1,0},{2,3},{3,2},{4,5},{5,4},{6,7},{7,6},{8,9},{9,8},{10,11... | collective-permute-start | bytes 196616 | tf_op jit(solution)/shard_map/ppermute | solution.py:320
  118.7 0.8 copy-start.3
  119.5 0.8 copy-start.5
  120.2 2.5 %copy-start.2 = (f32[256,256]{1,0:T(8,128)S(1)}, f32[256,256]{1,0:T(8,128)}, u32[]{:S(2)}) copy-start(f32[256,256]{1,0:T(8,128)} %copy-done.1) | copy-start | bytes 786436
  138.6 1.0 copy-start.4
  138.6 1.2 copy-start.6
  149.2 14.8 %collective-permute-start.17 = (f32[4,256,128]{2,1,0:T(8,128)S(1)}, f32[4,256,128]{2,1,0:T(8,128)S(1)}, u32[]{:S(2)}, u32[]{:S(2)}) collective-permute-start(f32[4,256,128]{2,1,0:T(8,128)S(1)} %lagged.4), channel_id=1, source_target_pairs={{0,8},{4,12},{8,0},{12,4},{16,24},{20,28},{24,16},{28,20},{1,9},{5... | collective-permute-start | bytes 1572872 | tf_op jit(solution)/shard_map/ppermute | solution.py:320
  149.2 25.6 %collective-permute-start.18 = (f32[4,256,128]{2,1,0:T(8,128)S(1)}, f32[4,256,128]{2,1,0:T(8,128)S(1)}, u32[]{:S(2)}, u32[]{:S(2)}) collective-permute-start(f32[4,256,128]{2,1,0:T(8,128)S(1)} %lagged.5), channel_id=1, source_target_pairs={{0,8},{4,12},{8,0},{12,4},{16,24},{20,28},{24,16},{28,20},{1,9},{5... | collective-permute-start | bytes 1572872 | tf_op jit(solution)/shard_map/ppermute | solution.py:320

commit v2 on v1

--- a/solution.py
+++ b/solution.py
@@ -30,11 +30,24 @@
     return dot(a_high, b_high) + dot(a_high, b_low) + dot(a_low, b_high)
 
 
-def sketch_kernel(owner_ref, before_ref, record_ref, after_ref, weight_ref, *refs):
-    keep_ref, give_ref, high, low, even, odd, total = refs
+def sketch_kernel(place_ref, before_ref, record_ref, after_ref, weight_ref, *refs):
+    keep_ref, give_ref, high, low, even, odd, total, buffer, arrived = refs
     pair = pl.program_id(0)
     rows, width = total.shape
     groups = weight_ref.shape[0]
+
+    def fetch(n):
+        slot = lax.rem(n, 2)
+        return pltpu.make_async_copy(weight_ref.at[:, pl.ds(2 * n, 2)], buffer.at[slot], arrived.at[slot])
+
+    @pl.when(pair == 0)
+    def _():
+        fetch(pair).start()
+
+    @pl.when(pair + 1 < pl.num_programs(0))
+    def _():
+        fetch(pair + 1).start()
+
     tiles = 3
     tile = (rows + STEP) // tiles
 
@@ -47,8 +60,10 @@
             first += size
         total[...] = jnp.zeros_like(total)
 
+    fetch(pair).wait()
+    slot = lax.rem(pair, 2)
     weight = jnp.concatenate(
-        [jnp.concatenate([weight_ref[a, 0], weight_ref[a, 1]], axis=1) for a in range(groups)],
+        [jnp.concatenate([buffer[slot, a, 0], buffer[slot, a, 1]], axis=1) for a in range(groups)],
         axis=0,
     )
     weight_high, weight_low = split(weight)
@@ -66,11 +81,11 @@
         share = keep_ref.shape[1]
         for ref, flip in ((keep_ref, 0), (give_ref, 1)):
             for n in range(2):
-                owner = jnp.bitwise_xor(owner_ref[0], 2 * n + flip)
+                owner = jnp.bitwise_xor(place_ref[0], 2 * n + flip)
                 ref[n] = total[pl.ds(pl.multiple_of(owner * share, 8), share), :]
 
 
-def sketch(owner, before, record, after, weights, shares):
+def sketch(place, before, record, after, weights, shares):
     lags, chans, width = weights.shape
     rows = before.shape[0] + record.shape[0]
     length = rows + after.shape[0]
@@ -78,8 +93,7 @@
     return pl.pallas_call(
         sketch_kernel,
         grid=(STEP // 2,),
-        in_specs=[SMEM, VMEM, VMEM, VMEM]
-        + [pl.BlockSpec((lags // STEP, 2, chans, width), lambda i: (0, i, 0, 0))],
+        in_specs=[SMEM, VMEM, VMEM, VMEM, pl.BlockSpec(memory_space=pltpu.HBM)],
         out_specs=[VMEM] * 2,
         out_shape=[jax.ShapeDtypeStruct((2, share, width), F32)] * 2,
         scratch_shapes=[
@@ -88,14 +102,16 @@
             pltpu.VMEM((rows + STEP, width), F32),
             pltpu.VMEM((rows + STEP, width), F32),
             pltpu.VMEM((rows, width), F32),
+            pltpu.VMEM((2, lags // STEP, 2, chans, width), F32),
+            pltpu.SemaphoreType.DMA((2,)),
         ],
-        compiler_params=pltpu.CompilerParams(vmem_limit_bytes=58 * 2**20),
+        compiler_params=pltpu.CompilerParams(vmem_limit_bytes=24 * 2**20),
         cost_estimate=cost(
             6 * rows * lags * chans * width,
             4 * (lags * chans * width + length * chans + rows * width),
         ),
         name="sketch",
-    )(owner.reshape(1), before, record, after, weights.reshape(lags // STEP, STEP, chans, width))
+    )(place, before, record, after, weights.reshape(lags // STEP, STEP, chans, width))
 
 
 def turn_kernel(block_ref, high_ref, low_ref):
@@ -115,10 +131,10 @@
     )(block)
 
 
-def assemble_kernel(bits_ref, own_ref, got_ref, out_ref):
+def assemble_kernel(place_ref, own_ref, got_ref, out_ref):
     pieces, share, _ = own_ref.shape
     blocks = pieces // 2
-    low, high = bits_ref[0], bits_ref[1]
+    low, high = place_ref[2], place_ref[3]
 
     def place(first_ref, second_ref):
         for b in range(blocks):
@@ -137,7 +153,7 @@
         place(got_ref, own_ref)
 
 
-def assemble(bits, own, got, shares):
+def assemble(place, own, got, shares):
     pieces, share, width = own.shape
     blocks = pieces // 2
     return pl.pallas_call(
@@ -148,13 +164,13 @@
         compiler_params=pltpu.CompilerParams(vmem_limit_bytes=20 * 2**20),
         cost_estimate=cost(0, 8 * blocks * shares * share * width),
         name="assemble",
-    )(bits, own, got)
-
-
-def gram_kernel(rim, bits_ref, own_ref, out_ref):
+    )(place, own, got)
+
+
+def gram_kernel(rim, place_ref, own_ref, out_ref):
     pieces, share, width = own_ref.shape
     blocks = pieces // 2
-    low, high = bits_ref[0], bits_ref[1]
+    low, high = place_ref[2], place_ref[3]
     kept = lax.broadcasted_iota(jnp.int32, (share, width), 0) >= rim
 
     def gram(value):
@@ -181,7 +197,7 @@
         out_ref[...] = halves[0] + halves[1]
 
 
-def gram_of(bits, own, rim):
+def gram_of(place, own, rim):
     pieces, share, width = own.shape
     return pl.pallas_call(
         functools.partial(gram_kernel, rim),
@@ -191,16 +207,17 @@
         compiler_params=pltpu.CompilerParams(vmem_limit_bytes=20 * 2**20),
         cost_estimate=cost(12 * pieces * share * width * width, 4 * pieces * share * width),
         name="gram",
-    )(bits, own)
-
-
-def factor_kernel(gram_ref, out_ref):
+    )(place, own)
+
+
+def factor_kernel(gram_ref, other_ref, out_ref):
     size = gram_ref.shape[0]
     tile = 8
     groups = size // tile
     row_of = lax.broadcasted_iota(jnp.int32, (tile, size), 0)
     col_of = lax.broadcasted_iota(jnp.int32, (tile, size), 1)
-    g = [gram_ref[q * tile : (q + 1) * tile, :] for q in range(groups)]
+    tiles = [slice(q * tile, (q + 1) * tile) for q in range(groups)]
+    g = [gram_ref[t, :] + other_ref[t, :] for t in tiles]
     x = [jnp.where(col_of == row_of + q * tile, 1.0, 0.0).astype(F32) for q in range(groups)]
     for p in range(groups):
         pivots = jnp.ones((tile, 1), F32)
@@ -222,16 +239,16 @@
         out_ref[p * tile : (p + 1) * tile, :] = x[p] * (1.0 / jnp.sqrt(pivots))
 
 
-def factor(gram):
+def factor(gram, other):
     return pl.pallas_call(
         factor_kernel,
-        in_specs=[VMEM],
+        in_specs=[VMEM] * 2,
         out_specs=VMEM,
         out_shape=jax.ShapeDtypeStruct(gram.shape, F32),
         compiler_params=pltpu.CompilerParams(vmem_limit_bytes=8 * 2**20),
         cost_estimate=cost(9 * 10**9, 2**17),
         name="factor",
-    )(gram)
+    )(gram, other)
 
 
 def lagged_kernel(places, lag_ref, *refs):
@@ -302,9 +319,64 @@
     )(inverse, kept, *received)
 
 
+def small(body, out_shapes, *args, smem=0):
+    shapes = [jax.ShapeDtypeStruct(shape, F32) for shape in out_shapes]
+    size = sum(a.size for a in args) + sum(s.size for s in shapes)
+    outs = pl.pallas_call(
+        body,
+        in_specs=[SMEM] * smem + [VMEM] * (len(args) - smem),
+        out_specs=[VMEM] * len(shapes),
+        out_shape=shapes,
+        compiler_params=pltpu.CompilerParams(vmem_limit_bytes=6 * 2**20),
+        cost_estimate=cost(size, 4 * size),
+    )(*args)
+    return outs[0] if len(outs) == 1 else outs
+
+
+def cut_kernel(record_ref, *outs):
+    rows = record_ref.shape[0]
+    before_ref, after_ref, *parts = outs
+    rim = after_ref.shape[0]
+    before_ref[...] = record_ref[rows - rim :]
+    after_ref[...] = record_ref[:rim]
+    first = 0
+    for ref in parts:
+        ref[...] = record_ref[first : first + ref.shape[0]]
+        first += ref.shape[0]
+
+
+def add_pair_kernel(keep_ref, got_ref, own_ref, pass_ref):
+    own_ref[...] = keep_ref[:1] + got_ref[:1]
+    pass_ref[...] = keep_ref[1:] + got_ref[1:]
+
+
+def add_masked_kernel(rim, place_ref, own_ref, got_ref, out_ref):
+    value = own_ref[...] + got_ref[...]
+    row = lax.broadcasted_iota(jnp.int32, value.shape, 1)
+    kept = (row >= rim) | (place_ref[0] > 0) | (place_ref[1] > 0)
+    out_ref[...] = jnp.where(kept, value, 0.0)
+
+
+def join_kernel(a_ref, b_ref, out_ref):
+    out_ref[: a_ref.shape[0]] = a_ref[...]
+    out_ref[a_ref.shape[0] :] = b_ref[...]
+
+
+def add_kernel(a_ref, b_ref, out_ref):
+    out_ref[...] = a_ref[...] + b_ref[...]
+
+
+def joined(a, b):
+    return small(join_kernel, [(a.shape[0] + b.shape[0],) + a.shape[1:]], a, b)
+
+
+def added(a, b):
+    return small(add_kernel, [a.shape], a, b)
+
+
 def on_device(record, test_matrix):
-    rows, _ = record.shape
-    lags, _, _ = test_matrix.shape
+    rows, chans = record.shape
+    lags, _, width = test_matrix.shape
     n_time = lax.axis_size("tm")
     n_chan = lax.axis_size("chan")
     here = lax.axis_index("tm")
@@ -313,6 +385,7 @@
     mids = n_time // 4
     per = lags // n_time
     rim = lags
+    place = jnp.stack([mine, here, mine % 2, mine // 2])
 
     def to(block, target, axis="tm"):
         count = lax.axis_size(axis)
@@ -333,39 +406,40 @@
     def across(t):
         return (t + half) % n_time
 
-    before = to(record[rows - rim :], lambda i: i + 1)
-    after = to(record[:rim], lambda i: i - 1)
     cut = [0, rows // 2, 3 * rows // 4, rows]
-    parts = [record[a:b] for a, b in zip(cut, cut[1:])]
+    sizes = [rim, rim] + [b - a for a, b in zip(cut, cut[1:])]
+    before, after, *parts = small(cut_kernel, [(n, chans) for n in sizes], record)
+    before = to(before, lambda i: i + 1)
+    after = to(after, lambda i: i - 1)
     beside_record = to(record, beside)
     across_parts = [to(part, across) for part in parts]
     both_parts = [to(part, beside) for part in across_parts]
 
-    keep, give = sketch(mine, before, record, after, test_matrix, n_chan)
+    keep, give = sketch(place, before, record, after, test_matrix, n_chan)
     share = keep.shape[1]
-    keep = keep + to(give, lambda i: i ^ 1, "chan")
-    own = keep[:1] + to(keep[1:], lambda i: i ^ 2, "chan")
-    row = mine * share + lax.broadcasted_iota(jnp.int32, (1, share, 1), 1)
-    own = jnp.where((row >= rim) | (here > 0), own, 0.0)
+    got = to(give, lambda i: i ^ 1, "chan")
+    own, passed = small(add_pair_kernel, [(1, share, width)] * 2, keep, got)
+    got = to(passed, lambda i: i ^ 2, "chan")
+    own = small(functools.partial(add_masked_kernel, rim), [own.shape], place, own, got, smem=1)
 
     def even(c):
         return c % 2 == 0
 
     got = to_both(own, lambda t, c: (t, c ^ 2) if even(c) else (across(t), c))
-    own = jnp.concatenate([own, got], axis=0)
+    own = joined(own, got)
     got = to_both(own, lambda t, c: (across(t), c) if even(c) else (beside(t), c))
-    own = jnp.concatenate([own, got], axis=0)
+    own = joined(own, got)
     got = to_both(own, lambda t, c: (beside(t), c) if even(c) else (t, c ^ 2))
-    own = jnp.concatenate([own, got], axis=0)
+    own = joined(own, got)
     got = to(own, lambda i: i ^ 1, "chan")
-    bits = jnp.stack([mine % 2, mine // 2])
-    gram = gram_of(bits, own, rim)
+    gram = gram_of(place, own, rim)
     distance = 2
     while distance < half:
-        gram = gram + to(gram, lambda i: i ^ distance)
+        other = to(gram, lambda i: i ^ distance)
+        gram = added(gram, other)
         distance *= 2
-    gram = gram + to(gram, lambda i: i ^ 1, "chan")
-    sketches = assemble(bits, own, got, n_chan)
+    gram_other = to(gram, lambda i: i ^ 1, "chan")
+    sketches = assemble(place, own, got, n_chan)
 
     turned = [turn(record)]
     turned += [turn(p) for p in across_parts]
@@ -379,7 +453,7 @@
     def owner_lag(step):
         return (outer + 2 * ((middle + step) % mids)) * per
 
-    chunks = 2 if per % 4 == 0 else 1
+    chunks = max(per // 2, 1)
     size = per // chunks
     received = []
     for s in range(1, mids):
@@ -391,7 +465,7 @@
             part = lagged(owner_lag(s) + n * size, turned, places, sketches, size)
             received.append(to(part, route))
     kept = lagged(owner_lag(0), turned, places, sketches, per)
-    inverse = factor(gram)
+    inverse = factor(gram, gram_other)
 
     def whitened(x):
         return lax.dot_general(

time: 177 us -> 171 us (0.966)
  waiting for transfers between devices: 85.3 us -> 68.5 us
  starting transfers between devices: 24 us -> 32.9 us
  Pallas kernels: 57 us -> 60.4 us
  other arithmetic: 2.85 us -> 0.08 us
    ppermute x16 -> x18, waiting for transfers between devices: 54.8 us -> 41.2 us  [to(): return lax.ppermute(block, axis, route)]
    ppermute x16 -> x18, starting transfers between devices: 16.6 us -> 25.8 us  [to(): return lax.ppermute(block, axis, route)]
    pallas_call x1 -> x8, Pallas kernels: 10.8 us -> 14.3 us  [the longest x1 11.7 us: factor(): pl.pallas_call(factor_kernel, in_specs=[VMEM] * 2, out_specs=VMEM, out_sh...]
    unnamed x18 -> x10, local copies, waits for them, and re-layouts: 3.21 us -> 6.68 us
    ppermute x3, waiting for transfers between devices: 30.5 us -> 27.3 us  [to_both(): return lax.ppermute(block, ('tm', 'chan'), route)]
    add x3 -> x0, other arithmetic: 2.51 us -> none  [the longest x1 0.99 us: on_device(): keep = keep + to(give, lambda i: i ^ 1, 'chan')]
    pallas_call x3 -> x5, Pallas kernels: 15.7 us -> 15.8 us  [lagged(): pl.pallas_call(functools.partial(lagged_kernel, places), grid=(lags // 2,...]
  transfers between devices with their start and end apart: 19 -> 21, of which waited for: 13 -> 14; matrix products, arithmetic and copies ran while one was open for 1% -> 1% of each run, Pallas kernels for 15% -> 17%
where the time goes in v2:
time: 171 us
  waiting for transfers between devices  68.5 us (40%)
  Pallas kernels  60.4 us (35%)
  starting transfers between devices  32.9 us (19%)
  local copies, waits for them, and re-layouts  6.68 us (4%)
    ppermute x18, waiting for transfers between devices, to(): return lax.ppermute(block, axis, route)  41.2 us
    ppermute x3, waiting for transfers between devices, to_both(): return lax.ppermute(block, ('tm', 'chan'), route)  27.3 us
    ppermute x18, starting transfers between devices, to(): return lax.ppermute(block, axis, route)  25.8 us
    pallas_call x1, Pallas kernels, sketch(): pl.pallas_call(sketch_kernel, grid=(STEP // 2,), in_specs=[SMEM, VMEM, VM...  18.8 us
    pallas_call x5, Pallas kernels, lagged(): pl.pallas_call(functools.partial(lagged_kernel, places), grid=(lags // 2,...  15.8 us
    pallas_call x1, Pallas kernels, factor(): pl.pallas_call(factor_kernel, in_specs=[VMEM] * 2, out_specs=VMEM, out_sh...  11.7 us
    pallas_call x8, Pallas kernels, turn(): pl.pallas_call(turn_kernel, in_specs=[VMEM], out_specs=[VMEM] * 2, out_sh...  7.13 us
    ppermute x3, starting transfers between devices, to_both(): return lax.ppermute(block, ('tm', 'chan'), route)  7.12 us
  transfers between devices with their start and end apart: 21, of which 14 were waited for; matrix products, arithmetic and copies ran while one was open for 1% of the time, Pallas kernels for 17%

profile of v2, /device:TPU:0, one launch (start us, length us, event | category | flops | bytes accessed | tf_op | source)
XLA Modules:
  0.0 170.8 jit_solution(1574512594815011792)
XLA Ops:
  0.6 1.3 shard_map.41
  1.9 4.9 %collective-permute-start = (f32[64,256]{1,0:T(8,128)S(1)}, f32[64,256]{1,0:T(8,128)S(1)}, u32[]{:S(2)}, u32[]{:S(2)}) collective-permute-start(f32[64,256]{1,0:T(8,128)S(1)} %get-tuple-element.27), channel_id=1, source_target_pairs={{0,4},{4,8},{8,12},{12,16},{16,20},{20,24},{24,28},{1,5},{5,9},{9,... | collective-permute-start | bytes 196616 | tf_op jit(solution)/shard_map/ppermute | solution.py:393
  6.8 1.3 collective-permute-start.1
  8.1 0.1 pad_add_fusion.place_ref
  8.2 0.5 collective-permute-done.before_ref
  8.7 4.3 %collective-permute-done.1.after_ref = f32[64,256]{1,0:T(8,128)S(1)} collective-permute-done((f32[64,256]{1,0:T(8,128)S(1)}, f32[64,256]{1,0:T(8,128)S(1)}, u32[]{:S(2)}, u32[]{:S(2)}) %collective-permute-start.1) | collective-permute-done | bytes 65568 | tf_op jit(solution)/shard_map/ppermute | solution.py:393
  13.0 3.4 %copy-done.4 = f32[64,256,128]{2,1,0:T(8,128)S(1)} copy-done((f32[64,256,128]{2,1,0:T(8,128)S(1)}, f32[64,256,128]{2,1,0:T(8,128)}, u32[]{:S(2)}) %copy-start.4) | copy-done | bytes 8388632
  16.4 18.8 %sketch.1 = (f32[2,272,128]{2,1,0:T(8,128)S(1)}, f32[2,272,128]{2,1,0:T(8,128)S(1)}) custom-call(s32[4]{0:T(128)S(1)} %pad_add_fusion.place_ref, f32[64,256]{1,0:T(8,128)S(1)} %collective-permute-done.before_ref, f32[1024,256]{1,0:T(8,128)} %block_ref.1, f32[64,256]{1,0:T(8,128)S(1)} %collective-permute-done.1.after_ref, f32[4,16,256,128]{3,2,1,0:T(8,128)S(1)} %bitcast.14), custom_call_target="tpu_custom_call" | custom-call | flops 13690208256 | bytes 10125312 | tf_op jit(solution)/shard_map/sketch/pallas_call | solution.py:93
  35.2 0.1 collective-permute-start.2
  35.2 1.5 collective-permute-done.2.got_ref
  36.8 1.6 collective-permute-start.3
  38.4 4.2 %collective-permute-done.3.got_ref = f32[1,272,128]{2,1,0:T(8,128)S(1)} collective-permute-done((f32[1,272,128]{2,1,0:T(8,128)S(1)}, f32[1,272,128]{2,1,0:T(8,128)S(1)}, u32[]{:S(2)}, u32[]{:S(2)}) %collective-permute-start.3) | collective-permute-done | bytes 139296 | tf_op jit(solution)/shard_map/ppermute | solution.py:393
  42.6 0.6 shard_map.43.a_ref
  43.2 1.6 collective-permute-start.4
  44.7 3.5 %collective-permute-done.4.b_ref = f32[1,272,128]{2,1,0:T(8,128)S(1)} collective-permute-done((f32[1,272,128]{2,1,0:T(8,128)S(1)}, f32[1,272,128]{2,1,0:T(8,128)S(1)}, u32[]{:S(2)}, u32[]{:S(2)}) %collective-permute-start.4) | collective-permute-done | bytes 139296 | tf_op jit(solution)/shard_map/ppermute | solution.py:401
  48.3 2.7 %collective-permute-start.5 = (f32[2,272,128]{2,1,0:T(8,128)S(1)}, f32[2,272,128]{2,1,0:T(8,128)S(1)}, u32[]{:S(2)}, u32[]{:S(2)}) collective-permute-start(f32[2,272,128]{2,1,0:T(8,128)S(1)} %shard_map.44.a_ref), channel_id=1, source_target_pairs={{0,16},{1,5},{2,18},{3,7},{4,20},{5,1},{6,22},{7,3},{8,24},{9,13},... | collective-permute-start | bytes 835592 | tf_op jit(solution)/shard_map/ppermute | solution.py:401
  51.0 2.4 %collective-permute-start.13 = (f32[1024,256]{1,0:T(8,128)}, f32[1024,256]{1,0:T(8,128)}, u32[]{:S(2)}, u32[]{:S(2)}) collective-permute-start(f32[1024,256]{1,0:T(8,128)} %block_ref.1), channel_id=1, source_target_pairs={{0,4},{4,0},{8,12},{12,8},{16,20},{20,16},{24,28},{28,24},{1,5},{5... | collective-permute-start | bytes 3145736 | tf_op jit(solution)/shard_map/ppermute | solution.py:393
  53.4 0.3 collective-permute-start.10
  53.7 23.8 %collective-permute-done.5.b_ref = f32[2,272,128]{2,1,0:T(8,128)S(1)} collective-permute-done((f32[2,272,128]{2,1,0:T(8,128)S(1)}, f32[2,272,128]{2,1,0:T(8,128)S(1)}, u32[]{:S(2)}, u32[]{:S(2)}) %collective-permute-start.5) | collective-permute-done | bytes 278560 | tf_op jit(solution)/shard_map/ppermute | solution.py:401
  77.6 2.9 %collective-permute-start.6 = (f32[4,272,128]{2,1,0:T(8,128)S(1)}, f32[4,272,128]{2,1,0:T(8,128)S(1)}, u32[]{:S(2)}, u32[]{:S(2)}) collective-permute-start(f32[4,272,128]{2,1,0:T(8,128)S(1)} %shard_map.45.a_ref), channel_id=1, source_target_pairs={{0,4},{1,3},{2,6},{3,1},{4,0},{5,7},{6,2},{7,5},{8,12},{9,11},{10,... | collective-permute-start | bytes 1671176 | tf_op jit(solution)/shard_map/ppermute | solution.py:401
  80.4 0.0 collective-permute-start.11
  80.5 2.9 %collective-permute-start.12 = (f32[256,256]{1,0:T(8,128)S(1)}, f32[256,256]{1,0:T(8,128)S(1)}, u32[]{:S(2)}, u32[]{:S(2)}) collective-permute-start(f32[256,256]{1,0:T(8,128)S(1)} %get-tuple-element.38), channel_id=1, source_target_pairs={{0,16},{4,20},{8,24},{12,28},{16,0},{20,4},{24,8},{28,12},{1,17},{... | collective-permute-start | bytes 786440 | tf_op jit(solution)/shard_map/ppermute | solution.py:393
  83.4 11.1 %collective-permute-done.10.block_ref = f32[512,256]{1,0:T(8,128)} collective-permute-done((f32[512,256]{1,0:T(8,128)S(1)}, f32[512,256]{1,0:T(8,128)}, u32[]{:S(2)}, u32[]{:S(2)}) %collective-permute-start.10) | collective-permute-done | bytes 524320 | tf_op jit(solution)/shard_map/ppermute | solution.py:393
  94.5 2.8 %collective-permute-start.14 = (f32[512,256]{1,0:T(8,128)}, f32[512,256]{1,0:T(8,128)}, u32[]{:S(2)}, u32[]{:S(2)}) collective-permute-start(f32[512,256]{1,0:T(8,128)} %collective-permute-done.10.block_ref), channel_id=1, source_target_pairs={{0,4},{4,0},{8,12},{12,8},{16,20},{20,16},{24,28},{28,24},{1,5},{5... | collective-permute-start | bytes 1572872 | tf_op jit(solution)/shard_map/ppermute | solution.py:393
  97.3 0.1 shard_map.46.own_ref
  97.4 1.8 %gram.1.a_ref = f32[128,128]{1,0:T(8,128)S(1)} custom-call(s32[4]{0:T(128)S(1)} %pad_add_fusion.place_ref, f32[8,272,128]{2,1,0:T(8,128)S(1)} %shard_map.46.own_ref), custom_call_target="tpu_custom_call" | custom-call | flops 427819008 | bytes 1114112 | tf_op jit(solution)/shard_map/gram/pallas_call | solution.py:202
  99.2 0.1 collective-permute-start.8
  99.3 0.8 collective-permute-done.11.block_ref
  100.1 2.8 %collective-permute-start.15 = (f32[256,256]{1,0:T(8,128)S(1)}, f32[256,256]{1,0:T(8,128)S(1)}, u32[]{:S(2)}, u32[]{:S(2)}) collective-permute-start(f32[256,256]{1,0:T(8,128)S(1)} %collective-permute-done.11.block_ref), channel_id=1, source_target_pairs={{0,4},{4,0},{8,12},{12,8},{16,20},{20,16},{24,28},{28,24},{1,5},{5... | collective-permute-start | bytes 786440 | tf_op jit(solution)/shard_map/ppermute | solution.py:393
  102.9 0.7 copy-done
  103.6 0.2 collective-permute-done.12.block_ref
  103.8 1.3 collective-permute-done.8.b_ref
  105.1 2.4 %collective-permute-start.16 = (f32[256,256]{1,0:T(8,128)S(1)}, f32[256,256]{1,0:T(8,128)}, u32[]{:S(2)}, u32[]{:S(2)}) collective-permute-start(f32[256,256]{1,0:T(8,128)S(1)} %collective-permute-done.12.block_ref), channel_id=1, source_target_pairs={{0,4},{4,0},{8,12},{12,8},{16,20},{20,16},{24,28},{28,24},{1,5},{5... | collective-permute-start | bytes 786440 | tf_op jit(solution)/shard_map/ppermute | solution.py:393
  107.6 0.6 shard_map.47.gram_ref
  108.2 4.9 %collective-permute-done.15.block_ref = f32[256,256]{1,0:T(8,128)S(1)} collective-permute-done((f32[256,256]{1,0:T(8,128)S(1)}, f32[256,256]{1,0:T(8,128)S(1)}, u32[]{:S(2)}, u32[]{:S(2)}) %collective-permute-start.15) | collective-permute-done | bytes 262176 | tf_op jit(solution)/shard_map/ppermute | solution.py:393
  113.1 0.7 copy-done.2
  113.8 1.6 turn.8
  115.4 0.0 copy-start.1
  115.4 0.9 copy-done.1
  116.4 0.1 turn.10
  116.5 0.1 turn.11
  116.7 1.2 turn.9
  117.9 0.0 copy-start.3
  117.9 0.9 copy-done.3
  118.9 0.1 turn.14
  119.0 1.1 turn.15
  120.1 1.6 turn.12
  121.7 1.2 turn.13
  123.0 11.7 %factor.1.inverse_ref = f32[128,128]{1,0:T(8,128)S(1)} custom-call(f32[128,128]{1,0:T(8,128)} %shard_map.47.gram_ref, f32[128,128]{1,0:T(8,128)} %collective-permute-done.9.other_ref), custom_call_target="tpu_custom_call" | custom-call | flops 8999999488 | bytes 131072 | tf_op jit(solution)/shard_map/factor/pallas_call | solution.py:243
  134.7 0.9 assemble.1.refs_16_
  135.5 2.0 %lagged.9 = f32[2,256,128]{2,1,0:T(8,128)S(1)} custom-call(s32[1]{0:T(128)} %bitcast.10.lag_ref, bf16[256,1024]{1,0:T(8,128)(2,1)S(1)} %get-tuple-element.33.refs_0_, bf16[256,512]{1,0:T(8,128)(2,1)S(1)} %get-tuple-element.35.refs_1_, bf16[256,256]{1,0:T(8,128)(2,1)S(1)} %get-tuple-element.37.refs_2_, bf16[256,256]{1,0:T(8,128)(2,1)S(1)} %get-tuple-element.39.refs_3_, ...), custom_call_target="tpu_custom_call" | custom-call | flops 1610612736 | bytes 6684672 | tf_op jit(solution)/shard_map/lagged/pallas_call | solution.py:280
  137.5 2.0 %lagged.8 = f32[2,256,128]{2,1,0:T(8,128)S(1)} custom-call(s32[1]{0:T(128)} %bitcast.9.lag_ref, bf16[256,1024]{1,0:T(8,128)(2,1)S(1)} %get-tuple-element.33.refs_0_, bf16[256,512]{1,0:T(8,128)(2,1)S(1)} %get-tuple-element.35.refs_1_, bf16[256,256]{1,0:T(8,128)(2,1)S(1)} %get-tuple-element.37.refs_2_, bf16[256,256]{1,0:T(8,128)(2,1)S(1)} %get-tuple-element.39.refs_3_, ...), custom_call_target="tpu_custom_call" | custom-call | flops 1610612736 | bytes 6684672 | tf_op jit(solution)/shard_map/lagged/pallas_call | solution.py:280
  139.6 2.0 %lagged.7 = f32[2,256,128]{2,1,0:T(8,128)S(1)} custom-call(s32[1]{0:T(128)} %bitcast.8.lag_ref, bf16[256,1024]{1,0:T(8,128)(2,1)S(1)} %get-tuple-element.33.refs_0_, bf16[256,512]{1,0:T(8,128)(2,1)S(1)} %get-tuple-element.35.refs_1_, bf16[256,256]{1,0:T(8,128)(2,1)S(1)} %get-tuple-element.37.refs_2_, bf16[256,256]{1,0:T(8,128)(2,1)S(1)} %get-tuple-element.39.refs_3_, ...), custom_call_target="tpu_custom_call" | custom-call | flops 1610612736 | bytes 6684672 | tf_op jit(solution)/shard_map/lagged/pallas_call | solution.py:280
  141.6 2.0 %lagged.6 = f32[2,256,128]{2,1,0:T(8,128)S(1)} custom-call(s32[1]{0:T(128)} %bitcast.7.lag_ref, bf16[256,1024]{1,0:T(8,128)(2,1)S(1)} %get-tuple-element.33.refs_0_, bf16[256,512]{1,0:T(8,128)(2,1)S(1)} %get-tuple-element.35.refs_1_, bf16[256,256]{1,0:T(8,128)(2,1)S(1)} %get-tuple-element.37.refs_2_, bf16[256,256]{1,0:T(8,128)(2,1)S(1)} %get-tuple-element.39.refs_3_, ...), custom_call_target="tpu_custom_call" | custom-call | flops 1610612736 | bytes 6684672 | tf_op jit(solution)/shard_map/lagged/pallas_call | solution.py:280
  143.6 0.1 collective-permute-start.17
  143.6 2.0 %collective-permute-start.18 = (f32[2,256,128]{2,1,0:T(8,128)S(1)}, f32[2,256,128]{2,1,0:T(8,128)S(1)}, u32[]{:S(2)}, u32[]{:S(2)}) collective-permute-start(f32[2,256,128]{2,1,0:T(8,128)S(1)} %lagged.7), channel_id=1, source_target_pairs={{0,8},{4,12},{8,0},{12,4},{16,24},{20,28},{24,16},{28,20},{1,9},{5... | collective-permute-start | bytes 786440 | tf_op jit(solution)/shard_map/ppermute | solution.py:393
  145.6 0.1 collective-permute-start.19
  145.7 1.9 %collective-permute-start.20 = (f32[2,256,128]{2,1,0:T(8,128)S(1)}, f32[2,256,128]{2,1,0:T(8,128)S(1)}, u32[]{:S(2)}, u32[]{:S(2)}) collective-permute-start(f32[2,256,128]{2,1,0:T(8,128)S(1)} %lagged.9), channel_id=1, source_target_pairs={{0,8},{4,12},{8,0},{12,4},{16,24},{20,28},{24,16},{28,20},{1,9},{5... | collective-permute-start | bytes 786440 | tf_op jit(solution)/shard_map/ppermute | solution.py:393
  147.7 7.8 %lagged.5.kept_ref = f32[8,256,128]{2,1,0:T(8,128)S(1)} custom-call(s32[1]{0:T(128)} %bitcast.6.lag_ref, bf16[256,1024]{1,0:T(8,128)(2,1)S(1)} %get-tuple-element.33.refs_0_, bf16[256,512]{1,0:T(8,128)(2,1)S(1)} %get-tuple-element.35.refs_1_, bf16[256,256]{1,0:T(8,128)(2,1)S(1)} %get-tuple-element.37.refs_2_, ...), custom_call_target="tpu_custom_call" | custom-call | flops 6442450944 | bytes 7471104 | tf_op jit(solution)/shard_map/lagged/pallas_call | solution.py:280
  155.5 1.4 convolution_multiply_fusion
  156.9 1.5 collective-permute-done.18.refs_1_
  158.4 5.6 %collective-permute-done.19.refs_2_ = f32[2,256,128]{2,1,0:T(8,128)S(1)} collective-permute-done((f32[2,256,128]{2,1,0:T(8,128)S(1)}, f32[2,256,128]{2,1,0:T(8,128)S(1)}, u32[]{:S(2)}, u32[]{:S(2)}) %collective-permute-start.19) | collective-permute-done | bytes 262176 | tf_op jit(solution)/shard_map/ppermute | solution.py:393
  164.0 5.2 %collective-permute-done.20.refs_3_ = f32[2,256,128]{2,1,0:T(8,128)S(1)} collective-permute-done((f32[2,256,128]{2,1,0:T(8,128)S(1)}, f32[2,256,128]{2,1,0:T(8,128)S(1)}, u32[]{:S(2)}, u32[]{:S(2)}) %collective-permute-start.20) | collective-permute-done | bytes 262176 | tf_op jit(solution)/shard_map/ppermute | solution.py:393
  169.2 1.6 finish.1
  (15 shorter events, 0.1 us)
Async XLA Ops:
  1.9 6.8 %collective-permute-start = (f32[64,256]{1,0:T(8,128)S(1)}, f32[64,256]{1,0:T(8,128)S(1)}, u32[]{:S(2)}, u32[]{:S(2)}) collective-permute-start(f32[64,256]{1,0:T(8,128)S(1)} %get-tuple-element.27), channel_id=1, source_target_pairs={{0,4},{4,8},{8,12},{12,16},{16,20},{20,24},{24,28},{1,5},{5,9},{9,... | collective-permute-start | bytes 196616 | tf_op jit(solution)/shard_map/ppermute | solution.py:393
  6.8 6.2 %collective-permute-start.1 = (f32[64,256]{1,0:T(8,128)S(1)}, f32[64,256]{1,0:T(8,128)S(1)}, u32[]{:S(2)}, u32[]{:S(2)}) collective-permute-start(f32[64,256]{1,0:T(8,128)S(1)} %get-tuple-element.28), channel_id=1, source_target_pairs={{4,0},{8,4},{12,8},{16,12},{20,16},{24,20},{28,24},{5,1},{9,5},{13... | collective-permute-start | bytes 196616 | tf_op jit(solution)/shard_map/ppermute | solution.py:393
  13.0 3.4 %copy-start.4 = (f32[64,256,128]{2,1,0:T(8,128)S(1)}, f32[64,256,128]{2,1,0:T(8,128)}, u32[]{:S(2)}) copy-start(f32[64,256,128]{2,1,0:T(8,128)} %param.3) | copy-start | bytes 25165828
  35.2 1.6 collective-permute-start.2
  36.8 5.8 %collective-permute-start.3 = (f32[1,272,128]{2,1,0:T(8,128)S(1)}, f32[1,272,128]{2,1,0:T(8,128)S(1)}, u32[]{:S(2)}, u32[]{:S(2)}) collective-permute-start(f32[1,272,128]{2,1,0:T(8,128)S(1)} %get-tuple-element.32), channel_id=1, source_target_pairs={{0,2},{1,3},{2,0},{3,1},{4,6},{5,7},{6,4},{7,5},{8,10},{9,11},{10,... | collective-permute-start | bytes 417800 | tf_op jit(solution)/shard_map/ppermute | solution.py:393
  43.2 5.1 %collective-permute-start.4 = (f32[1,272,128]{2,1,0:T(8,128)S(1)}, f32[1,272,128]{2,1,0:T(8,128)S(1)}, u32[]{:S(2)}, u32[]{:S(2)}) collective-permute-start(f32[1,272,128]{2,1,0:T(8,128)S(1)} %shard_map.43.a_ref), channel_id=1, source_target_pairs={{0,2},{1,17},{2,0},{3,19},{4,6},{5,21},{6,4},{7,23},{8,10},{9,25},... | collective-permute-start | bytes 417800 | tf_op jit(solution)/shard_map/ppermute | solution.py:401
  48.3 29.2 %collective-permute-start.5 = (f32[2,272,128]{2,1,0:T(8,128)S(1)}, f32[2,272,128]{2,1,0:T(8,128)S(1)}, u32[]{:S(2)}, u32[]{:S(2)}) collective-permute-start(f32[2,272,128]{2,1,0:T(8,128)S(1)} %shard_map.44.a_ref), channel_id=1, source_target_pairs={{0,16},{1,5},{2,18},{3,7},{4,20},{5,1},{6,22},{7,3},{8,24},{9,13},... | collective-permute-start | bytes 835592 | tf_op jit(solution)/shard_map/ppermute | solution.py:401
  51.0 69.2 %collective-permute-start.13 = (f32[1024,256]{1,0:T(8,128)}, f32[1024,256]{1,0:T(8,128)}, u32[]{:S(2)}, u32[]{:S(2)}) collective-permute-start(f32[1024,256]{1,0:T(8,128)} %block_ref.1), channel_id=1, source_target_pairs={{0,4},{4,0},{8,12},{12,8},{16,20},{20,16},{24,28},{28,24},{1,5},{5... | collective-permute-start | bytes 3145736 | tf_op jit(solution)/shard_map/ppermute | solution.py:393
  53.4 41.1 %collective-permute-start.10 = (f32[512,256]{1,0:T(8,128)S(1)}, f32[512,256]{1,0:T(8,128)}, u32[]{:S(2)}, u32[]{:S(2)}) collective-permute-start(f32[512,256]{1,0:T(8,128)S(1)} %get-tuple-element.34), channel_id=1, source_target_pairs={{0,16},{4,20},{8,24},{12,28},{16,0},{20,4},{24,8},{28,12},{1,17},{... | collective-permute-start | bytes 1572872 | tf_op jit(solution)/shard_map/ppermute | solution.py:393
  77.6 19.7 %collective-permute-start.6 = (f32[4,272,128]{2,1,0:T(8,128)S(1)}, f32[4,272,128]{2,1,0:T(8,128)S(1)}, u32[]{:S(2)}, u32[]{:S(2)}) collective-permute-start(f32[4,272,128]{2,1,0:T(8,128)S(1)} %shard_map.45.a_ref), channel_id=1, source_target_pairs={{0,4},{1,3},{2,6},{3,1},{4,0},{5,7},{6,2},{7,5},{8,12},{9,11},{10,... | collective-permute-start | bytes 1671176 | tf_op jit(solution)/shard_map/ppermute | solution.py:401
  80.4 19.6 %collective-permute-start.11 = (f32[256,256]{1,0:T(8,128)S(1)}, f32[256,256]{1,0:T(8,128)S(1)}, u32[]{:S(2)}, u32[]{:S(2)}) collective-permute-start(f32[256,256]{1,0:T(8,128)S(1)} %get-tuple-element.36), channel_id=1, source_target_pairs={{0,16},{4,20},{8,24},{12,28},{16,0},{20,4},{24,8},{28,12},{1,17},{... | collective-permute-start | bytes 786440 | tf_op jit(solution)/shard_map/ppermute | solution.py:393
  80.5 23.4 %collective-permute-start.12 = (f32[256,256]{1,0:T(8,128)S(1)}, f32[256,256]{1,0:T(8,128)S(1)}, u32[]{:S(2)}, u32[]{:S(2)}) collective-permute-start(f32[256,256]{1,0:T(8,128)S(1)} %get-tuple-element.38), channel_id=1, source_target_pairs={{0,16},{4,20},{8,24},{12,28},{16,0},{20,4},{24,8},{28,12},{1,17},{... | collective-permute-start | bytes 786440 | tf_op jit(solution)/shard_map/ppermute | solution.py:393
  94.5 27.2 %collective-permute-start.14 = (f32[512,256]{1,0:T(8,128)}, f32[512,256]{1,0:T(8,128)}, u32[]{:S(2)}, u32[]{:S(2)}) collective-permute-start(f32[512,256]{1,0:T(8,128)} %collective-permute-done.10.block_ref), channel_id=1, source_target_pairs={{0,4},{4,0},{8,12},{12,8},{16,20},{20,16},{24,28},{28,24},{1,5},{5... | collective-permute-start | bytes 1572872 | tf_op jit(solution)/shard_map/ppermute | solution.py:393
  99.2 6.0 %collective-permute-start.8 = (f32[128,128]{1,0:T(8,128)S(1)}, f32[128,128]{1,0:T(8,128)S(1)}, u32[]{:S(2)}, u32[]{:S(2)}) collective-permute-start(f32[128,128]{1,0:T(8,128)S(1)} %gram.1.a_ref), channel_id=1, source_target_pairs={{0,8},{4,12},{8,0},{12,4},{16,24},{20,28},{24,16},{28,20},{1,9},{5... | collective-permute-start | bytes 196616 | tf_op jit(solution)/shard_map/ppermute | solution.py:393
  100.1 13.0 %collective-permute-start.15 = (f32[256,256]{1,0:T(8,128)S(1)}, f32[256,256]{1,0:T(8,128)S(1)}, u32[]{:S(2)}, u32[]{:S(2)}) collective-permute-start(f32[256,256]{1,0:T(8,128)S(1)} %collective-permute-done.11.block_ref), channel_id=1, source_target_pairs={{0,4},{4,0},{8,12},{12,8},{16,20},{20,16},{24,28},{28,24},{1,5},{5... | collective-permute-start | bytes 786440 | tf_op jit(solution)/shard_map/ppermute | solution.py:393
  102.9 0.7 copy-start
  103.8 30.8 %collective-permute-start.7 = (f32[8,272,128]{2,1,0:T(8,128)S(1)}, f32[8,272,128]{2,1,0:T(8,128)S(1)}, u32[]{:S(2)}, u32[]{:S(2)}) collective-permute-start(f32[8,272,128]{2,1,0:T(8,128)S(1)} %shard_map.46.own_ref), channel_id=1, source_target_pairs={{0,1},{1,0},{2,3},{3,2},{4,5},{5,4},{6,7},{7,6},{8,9},{9,8},{10,11... | collective-permute-start | bytes 3342344 | tf_op jit(solution)/shard_map/ppermute | solution.py:393
  105.1 13.9 %collective-permute-start.16 = (f32[256,256]{1,0:T(8,128)S(1)}, f32[256,256]{1,0:T(8,128)}, u32[]{:S(2)}, u32[]{:S(2)}) collective-permute-start(f32[256,256]{1,0:T(8,128)S(1)} %collective-permute-done.12.block_ref), channel_id=1, source_target_pairs={{0,4},{4,0},{8,12},{12,8},{16,20},{20,16},{24,28},{28,24},{1,5},{5... | collective-permute-start | bytes 786440 | tf_op jit(solution)/shard_map/ppermute | solution.py:393
  113.1 0.7 copy-start.2
  113.8 9.1 %collective-permute-start.9 = (f32[128,128]{1,0:T(8,128)}, f32[128,128]{1,0:T(8,128)}, u32[]{:S(2)}, u32[]{:S(2)}) collective-permute-start(f32[128,128]{1,0:T(8,128)} %shard_map.47.gram_ref), channel_id=1, source_target_pairs={{0,1},{1,0},{2,3},{3,2},{4,5},{5,4},{6,7},{7,6},{8,9},{9,8},{10,11... | collective-permute-start | bytes 196616 | tf_op jit(solution)/shard_map/ppermute | solution.py:393
  115.4 1.0 copy-start.1
  117.9 1.0 copy-start.3
  143.6 13.4 %collective-permute-start.17 = (f32[2,256,128]{2,1,0:T(8,128)S(1)}, f32[2,256,128]{2,1,0:T(8,128)S(1)}, u32[]{:S(2)}, u32[]{:S(2)}) collective-permute-start(f32[2,256,128]{2,1,0:T(8,128)S(1)} %lagged.6), channel_id=1, source_target_pairs={{0,8},{4,12},{8,0},{12,4},{16,24},{20,28},{24,16},{28,20},{1,9},{5... | collective-permute-start | bytes 786440 | tf_op jit(solution)/shard_map/ppermute | solution.py:393
  143.6 14.8 %collective-permute-start.18 = (f32[2,256,128]{2,1,0:T(8,128)S(1)}, f32[2,256,128]{2,1,0:T(8,128)S(1)}, u32[]{:S(2)}, u32[]{:S(2)}) collective-permute-start(f32[2,256,128]{2,1,0:T(8,128)S(1)} %lagged.7), channel_id=1, source_target_pairs={{0,8},{4,12},{8,0},{12,4},{16,24},{20,28},{24,16},{28,20},{1,9},{5... | collective-permute-start | bytes 786440 | tf_op jit(solution)/shard_map/ppermute | solution.py:393
  145.6 18.4 %collective-permute-start.19 = (f32[2,256,128]{2,1,0:T(8,128)S(1)}, f32[2,256,128]{2,1,0:T(8,128)S(1)}, u32[]{:S(2)}, u32[]{:S(2)}) collective-permute-start(f32[2,256,128]{2,1,0:T(8,128)S(1)} %lagged.8), channel_id=1, source_target_pairs={{0,8},{4,12},{8,0},{12,4},{16,24},{20,28},{24,16},{28,20},{1,9},{5... | collective-permute-start | bytes 786440 | tf_op jit(solution)/shard_map/ppermute | solution.py:393
  145.7 23.5 %collective-permute-start.20 = (f32[2,256,128]{2,1,0:T(8,128)S(1)}, f32[2,256,128]{2,1,0:T(8,128)S(1)}, u32[]{:S(2)}, u32[]{:S(2)}) collective-permute-start(f32[2,256,128]{2,1,0:T(8,128)S(1)} %lagged.9), channel_id=1, source_target_pairs={{0,8},{4,12},{8,0},{12,4},{16,24},{20,28},{24,16},{28,20},{1,9},{5... | collective-permute-start | bytes 786440 | tf_op jit(solution)/shard_map/ppermute | solution.py:393

commit v3 on v2

--- a/solution.py
+++ b/solution.py
@@ -30,7 +30,7 @@
     return dot(a_high, b_high) + dot(a_high, b_low) + dot(a_low, b_high)
 
 
-def sketch_kernel(place_ref, before_ref, record_ref, after_ref, weight_ref, *refs):
+def sketch_kernel(place_ref, beside_ref, record_ref, beyond_ref, weight_ref, *refs):
     keep_ref, give_ref, high, low, even, odd, total, buffer, arrived = refs
     pair = pl.program_id(0)
     rows, width = total.shape
@@ -53,11 +53,24 @@
 
     @pl.when(pair == 0)
     def _():
-        first = 0
-        for ref in (before_ref, record_ref, after_ref):
-            size = ref.shape[0]
-            high[first : first + size], low[first : first + size] = split(ref[...])
-            first += size
+        def place_rows(first, ref):
+            part = slice(first, first + ref.shape[0])
+            high[part], low[part] = split(ref[...])
+
+        rim = beside_ref.shape[0]
+        last = rim + record_ref.shape[0]
+        place_rows(rim, record_ref)
+
+        @pl.when(lax.rem(place_ref[1], 2) == 0)
+        def _():
+            place_rows(0, beyond_ref)
+            place_rows(last, beside_ref)
+
+        @pl.when(lax.rem(place_ref[1], 2) == 1)
+        def _():
+            place_rows(0, beside_ref)
+            place_rows(last, beyond_ref)
+
         total[...] = jnp.zeros_like(total)
 
     fetch(pair).wait()
@@ -85,10 +98,10 @@
                 ref[n] = total[pl.ds(pl.multiple_of(owner * share, 8), share), :]
 
 
-def sketch(place, before, record, after, weights, shares):
+def sketch(place, beside, record, beyond, weights, shares):
     lags, chans, width = weights.shape
-    rows = before.shape[0] + record.shape[0]
-    length = rows + after.shape[0]
+    rows = beside.shape[0] + record.shape[0]
+    length = rows + beyond.shape[0]
     share = rows // shares
     return pl.pallas_call(
         sketch_kernel,
@@ -111,7 +124,7 @@
             4 * (lags * chans * width + length * chans + rows * width),
         ),
         name="sketch",
-    )(place, before, record, after, weights.reshape(lags // STEP, STEP, chans, width))
+    )(place, beside, record, beyond, pltpu.with_memory_space_constraint(weights.reshape(lags // STEP, STEP, chans, width), pltpu.HBM))
 
 
 def turn_kernel(block_ref, high_ref, low_ref):
@@ -213,30 +226,42 @@
 def factor_kernel(gram_ref, other_ref, out_ref):
     size = gram_ref.shape[0]
     tile = 8
-    groups = size // tile
+    tiles = [slice(q, q + tile) for q in range(0, size, tile)]
     row_of = lax.broadcasted_iota(jnp.int32, (tile, size), 0)
     col_of = lax.broadcasted_iota(jnp.int32, (tile, size), 1)
-    tiles = [slice(q * tile, (q + 1) * tile) for q in range(groups)]
     g = [gram_ref[t, :] + other_ref[t, :] for t in tiles]
-    x = [jnp.where(col_of == row_of + q * tile, 1.0, 0.0).astype(F32) for q in range(groups)]
-    for p in range(groups):
-        pivots = jnp.ones((tile, 1), F32)
-        for r in range(tile):
-            j = p * tile + r
-            g_row = g[p][r : r + 1, :]
-            x_row = x[p][r : r + 1, :]
-            pivot = g_row[:, j : j + 1]
-            pivots = jnp.where(row_of[:, :1] == r, pivot, pivots)
-            inverse = 1.0 / pivot
-            g_row = g_row * inverse
-            x_row = x_row * inverse
-            for q in range(p, groups):
-                column = g[q][:, j : j + 1]
-                if q == p:
-                    column = jnp.where(row_of[:, :1] > r, column, 0.0)
-                g[q] = g[q] - column * g_row
-                x[q] = x[q] - column * x_row
-        out_ref[p * tile : (p + 1) * tile, :] = x[p] * (1.0 / jnp.sqrt(pivots))
+    x = [jnp.where(col_of == row_of + t.start, 1.0, 0.0).astype(F32) for t in tiles]
+    for p, t in enumerate(tiles):
+        first = t.start
+        square = [
+            [jnp.broadcast_to(g[p][a : a + 1, first + b : first + b + 1], (1, size)) for b in range(tile)]
+            for a in range(tile)
+        ]
+        g_rows = [g[p][a : a + 1, :] for a in range(tile)]
+        x_rows = [x[p][a : a + 1, :] for a in range(tile)]
+        inverse, ratio = [], {}
+        for a in range(tile):
+            inverse.append(1.0 / square[a][a])
+            for b in range(a + 1, tile):
+                ratio[b, a] = square[a][b] * inverse[a]
+                for c in range(b, tile):
+                    square[b][c] = square[b][c] - ratio[b, a] * square[a][c]
+                g_rows[b] = g_rows[b] - ratio[b, a] * g_rows[a]
+                x_rows[b] = x_rows[b] - ratio[b, a] * x_rows[a]
+        g_scaled = [v * i for v, i in zip(g_rows, inverse)]
+        x_scaled = [v * i for v, i in zip(x_rows, inverse)]
+        for q in range(p + 1, len(tiles)):
+            columns = [
+                jnp.broadcast_to(g[q][:, first + a : first + a + 1], (tile, size)) for a in range(tile)
+            ]
+            for a in range(tile):
+                for b in range(a + 1, tile):
+                    columns[b] = columns[b] - ratio[b, a] * columns[a]
+            for a in range(tile):
+                g[q] = g[q] - columns[a] * g_scaled[a]
+                x[q] = x[q] - columns[a] * x_scaled[a]
+        for a in range(tile):
+            out_ref[first + a : first + a + 1, :] = x_rows[a] * (1.0 / jnp.sqrt(square[a][a]))
 
 
 def factor(gram, other):
@@ -246,7 +271,7 @@
         out_specs=VMEM,
         out_shape=jax.ShapeDtypeStruct(gram.shape, F32),
         compiler_params=pltpu.CompilerParams(vmem_limit_bytes=8 * 2**20),
-        cost_estimate=cost(9 * 10**9, 2**17),
+        cost_estimate=cost(3 * 10**9, 2**17),
         name="factor",
     )(gram, other)
 
@@ -293,30 +318,32 @@
 
 
 def finish_kernel(chunks, inverse_ref, kept_ref, *refs):
-    *received, out_ref = refs
-    lags, chans, width = out_ref.shape
-    size = lags // chunks
+    received, out_ref = refs[:chunks], refs[-1]
+    size, chans, width = received[0].shape
     inverse_high, inverse_low = split(inverse_ref[...].T)
-    for n in range(chunks):
+    for n, ref in enumerate(received):
         part = slice(n * size, (n + 1) * size)
-        total = kept_ref[part]
-        for ref in received[n::chunks]:
-            total = total + ref[...]
-        high, low = split(total.reshape(size * chans, width))
+        high, low = split((kept_ref[part] + ref[...]).reshape(size * chans, width))
         out_ref[part] = three(high, low, inverse_high, inverse_low).reshape(size, chans, width)
 
 
-def finish(inverse, kept, received, chunks):
-    lags, chans, width = kept.shape
-    return pl.pallas_call(
-        functools.partial(finish_kernel, chunks),
-        in_specs=[VMEM] * (2 + len(received)),
-        out_specs=VMEM,
+def finish(inverse, kept, received, first, out=None):
+    _, chans, width = kept.shape
+    size = received[0].shape[0]
+    count = len(received)
+    block = pl.BlockSpec((count * size, chans, width), lambda i: (first // count, 0, 0))
+    extra = [] if out is None else [out]
+    return pl.pallas_call(
+        functools.partial(finish_kernel, count),
+        grid=(1,),
+        in_specs=[VMEM, block] + [VMEM] * count + [pl.BlockSpec(memory_space=pl.ANY)] * len(extra),
+        out_specs=block,
         out_shape=jax.ShapeDtypeStruct(kept.shape, F32),
-        compiler_params=pltpu.CompilerParams(vmem_limit_bytes=20 * 2**20),
-        cost_estimate=cost(6 * lags * chans * width * width, 12 * lags * chans * width),
+        input_output_aliases={} if out is None else {2 + count: 0},
+        compiler_params=pltpu.CompilerParams(vmem_limit_bytes=12 * 2**20),
+        cost_estimate=cost(6 * count * size * chans * width * width, 12 * count * size * chans * width),
         name="finish",
-    )(inverse, kept, *received)
+    )(inverse, kept, *received, *extra)
 
 
 def small(body, out_shapes, *args, smem=0):
@@ -333,12 +360,21 @@
     return outs[0] if len(outs) == 1 else outs
 
 
-def cut_kernel(record_ref, *outs):
+def cut_kernel(place_ref, record_ref, *outs):
     rows = record_ref.shape[0]
-    before_ref, after_ref, *parts = outs
-    rim = after_ref.shape[0]
-    before_ref[...] = record_ref[rows - rim :]
-    after_ref[...] = record_ref[:rim]
+    beside_ref, beyond_ref, *parts = outs
+    rim = beside_ref.shape[0]
+
+    @pl.when(lax.rem(place_ref[1], 2) == 0)
+    def _():
+        beside_ref[...] = record_ref[rows - rim :]
+        beyond_ref[...] = record_ref[:rim]
+
+    @pl.when(lax.rem(place_ref[1], 2) == 1)
+    def _():
+        beside_ref[...] = record_ref[:rim]
+        beyond_ref[...] = record_ref[rows - rim :]
+
     first = 0
     for ref in parts:
         ref[...] = record_ref[first : first + ref.shape[0]]
@@ -408,14 +444,14 @@
 
     cut = [0, rows // 2, 3 * rows // 4, rows]
     sizes = [rim, rim] + [b - a for a, b in zip(cut, cut[1:])]
-    before, after, *parts = small(cut_kernel, [(n, chans) for n in sizes], record)
-    before = to(before, lambda i: i + 1)
-    after = to(after, lambda i: i - 1)
+    at_beside, at_beyond, *parts = small(cut_kernel, [(n, chans) for n in sizes], place, record, smem=1)
+    at_beyond = to(at_beyond, lambda i: i - 1 + 2 * (i % 2))
+    at_beside = to(at_beside, beside)
     beside_record = to(record, beside)
     across_parts = [to(part, across) for part in parts]
     both_parts = [to(part, beside) for part in across_parts]
 
-    keep, give = sketch(place, before, record, after, test_matrix, n_chan)
+    keep, give = sketch(place, at_beside, record, at_beyond, test_matrix, n_chan)
     share = keep.shape[1]
     got = to(give, lambda i: i ^ 1, "chan")
     own, passed = small(add_pair_kernel, [(1, share, width)] * 2, keep, got)
@@ -473,7 +509,17 @@
         )
 
     basis = whitened(sketches[0, rim:]) * jnp.sqrt(F32(rows * n_time))
-    return basis, finish(inverse, kept, received, chunks)
+    totals = []
+    for n in range(chunks):
+        total = received[n]
+        for more in received[n + chunks :: chunks]:
+            total = added(total, more)
+        totals.append(total)
+    coeffs = None
+    for first, count in ((0, chunks // 2), (chunks // 2, chunks // 4), (3 * chunks // 4, chunks - 3 * chunks // 4)):
+        if count:
+            coeffs = finish(inverse, kept, totals[first : first + count], first, coeffs)
+    return basis, coeffs
 
 
 def solution(mesh):

time: 171 us -> 167 us (0.977)
  Pallas kernels: 60.4 us -> 55.1 us
  waiting for transfers between devices: 68.5 us -> 72 us
  local copies, waits for them, and re-layouts: 6.68 us -> 3.29 us
    pallas_call x1, Pallas kernels: 11.7 us -> 4.35 us  [factor(): pl.pallas_call(factor_kernel, in_specs=[VMEM] * 2, out_specs=VMEM, out_sh...]
    ppermute x18, waiting for transfers between devices: 41.2 us -> 47.8 us  [to(): return lax.ppermute(block, axis, route)]
    unnamed x10 -> x8, local copies, waits for them, and re-layouts: 6.68 us -> 3.29 us
    ppermute x3, waiting for transfers between devices: 27.3 us -> 24.3 us  [to_both(): return lax.ppermute(block, ('tm', 'chan'), route)]
    ppermute x3, starting transfers between devices: 7.12 us -> 9.66 us  [to_both(): return lax.ppermute(block, ('tm', 'chan'), route)]
    pallas_call x1 -> x3, Pallas kernels: 1.62 us -> 3.34 us  [finish(): pl.pallas_call(functools.partial(finish_kernel, count), grid=(1,), in_spe...]
  transfers between devices with their start and end apart: 21 -> 21, of which waited for: 14 -> 13; matrix products, arithmetic and copies ran while one was open for 1% -> 1% of each run, Pallas kernels for 17% -> 11%
where the time goes in v3:
time: 167 us
  waiting for transfers between devices  72 us (43%)
  Pallas kernels  55.1 us (33%)
  starting transfers between devices  34.1 us (20%)
  local copies, waits for them, and re-layouts  3.29 us (2%)
    ppermute x18, waiting for transfers between devices, to(): return lax.ppermute(block, axis, route)  47.8 us
    ppermute x18, starting transfers between devices, to(): return lax.ppermute(block, axis, route)  24.4 us
    ppermute x3, waiting for transfers between devices, to_both(): return lax.ppermute(block, ('tm', 'chan'), route)  24.3 us
    pallas_call x1, Pallas kernels, sketch(): pl.pallas_call(sketch_kernel, grid=(STEP // 2,), in_specs=[SMEM, VMEM, VM...  19.2 us
    pallas_call x5, Pallas kernels, lagged(): pl.pallas_call(functools.partial(lagged_kernel, places), grid=(lags // 2,...  15.8 us
    ppermute x3, starting transfers between devices, to_both(): return lax.ppermute(block, ('tm', 'chan'), route)  9.66 us
    pallas_call x8, Pallas kernels, turn(): pl.pallas_call(turn_kernel, in_specs=[VMEM], out_specs=[VMEM] * 2, out_sh...  7.13 us
    pallas_call x1, Pallas kernels, factor(): pl.pallas_call(factor_kernel, in_specs=[VMEM] * 2, out_specs=VMEM, out_sh...  4.35 us
  transfers between devices with their start and end apart: 21, of which 13 were waited for; matrix products, arithmetic and copies ran while one was open for 1% of the time, Pallas kernels for 11%

profile of v3, /device:TPU:0, one launch (start us, length us, event | category | flops | bytes accessed | tf_op | source)
XLA Modules:
  0.0 166.9 jit_solution(13033104058825382098)
XLA Ops:
  0.6 0.1 pad_add_fusion.place_ref
  0.7 1.3 shard_map.41
  2.1 3.0 %collective-permute-start = (f32[64,256]{1,0:T(8,128)S(1)}, f32[64,256]{1,0:T(8,128)S(1)}, u32[]{:S(2)}, u32[]{:S(2)}) collective-permute-start(f32[64,256]{1,0:T(8,128)S(1)} %get-tuple-element.27), channel_id=1, source_target_pairs={{0,4},{4,0},{8,12},{12,8},{16,20},{20,16},{24,28},{28,24},{1,5},{5... | collective-permute-start | bytes 196616 | tf_op jit(solution)/shard_map/ppermute | solution.py:429
  5.1 0.7 collective-permute-start.1
  5.8 1.6 collective-permute-done.beside_ref
  7.3 19.2 %sketch.1 = (f32[2,272,128]{2,1,0:T(8,128)S(1)}, f32[2,272,128]{2,1,0:T(8,128)S(1)}) custom-call(s32[4]{0:T(128)S(1)} %pad_add_fusion.place_ref, f32[64,256]{1,0:T(8,128)S(1)} %collective-permute-done.beside_ref, f32[1024,256]{1,0:T(8,128)} %block_ref.1, f32[64,256]{1,0:T(8,128)S(1)} %collective-permute-done.1.beyond_ref, f32[4,16,256,128]{3,2,1,0:T(8,128)} %bitcast.14), custom_call_target="tpu_custom_call" | custom-call | flops 13690208256 | bytes 10125312 | tf_op jit(solution)/shard_map/sketch/pallas_call | solution.py:106
  26.5 0.1 collective-permute-start.2
  26.6 1.5 collective-permute-done.2.got_ref
  28.2 2.1 %collective-permute-start.3 = (f32[1,272,128]{2,1,0:T(8,128)S(1)}, f32[1,272,128]{2,1,0:T(8,128)S(1)}, u32[]{:S(2)}, u32[]{:S(2)}) collective-permute-start(f32[1,272,128]{2,1,0:T(8,128)S(1)} %get-tuple-element.32), channel_id=1, source_target_pairs={{0,2},{1,3},{2,0},{3,1},{4,6},{5,7},{6,4},{7,5},{8,10},{9,11},{10,... | collective-permute-start | bytes 417800 | tf_op jit(solution)/shard_map/ppermute | solution.py:429
  30.3 4.0 %collective-permute-done.3.got_ref = f32[1,272,128]{2,1,0:T(8,128)S(1)} collective-permute-done((f32[1,272,128]{2,1,0:T(8,128)S(1)}, f32[1,272,128]{2,1,0:T(8,128)S(1)}, u32[]{:S(2)}, u32[]{:S(2)}) %collective-permute-start.3) | collective-permute-done | bytes 139296 | tf_op jit(solution)/shard_map/ppermute | solution.py:429
  34.3 0.6 shard_map.43.a_ref
  34.9 1.8 %collective-permute-start.4 = (f32[1,272,128]{2,1,0:T(8,128)S(1)}, f32[1,272,128]{2,1,0:T(8,128)S(1)}, u32[]{:S(2)}, u32[]{:S(2)}) collective-permute-start(f32[1,272,128]{2,1,0:T(8,128)S(1)} %shard_map.43.a_ref), channel_id=1, source_target_pairs={{0,2},{1,17},{2,0},{3,19},{4,6},{5,21},{6,4},{7,23},{8,10},{9,25},... | collective-permute-start | bytes 417800 | tf_op jit(solution)/shard_map/ppermute | solution.py:437
  36.7 3.3 %collective-permute-done.4.b_ref = f32[1,272,128]{2,1,0:T(8,128)S(1)} collective-permute-done((f32[1,272,128]{2,1,0:T(8,128)S(1)}, f32[1,272,128]{2,1,0:T(8,128)S(1)}, u32[]{:S(2)}, u32[]{:S(2)}) %collective-permute-start.4) | collective-permute-done | bytes 139296 | tf_op jit(solution)/shard_map/ppermute | solution.py:437
  40.0 7.1 %collective-permute-start.5 = (f32[2,272,128]{2,1,0:T(8,128)S(1)}, f32[2,272,128]{2,1,0:T(8,128)S(1)}, u32[]{:S(2)}, u32[]{:S(2)}) collective-permute-start(f32[2,272,128]{2,1,0:T(8,128)S(1)} %shard_map.44.a_ref), channel_id=1, source_target_pairs={{0,16},{1,5},{2,18},{3,7},{4,20},{5,1},{6,22},{7,3},{8,24},{9,13},... | collective-permute-start | bytes 835592 | tf_op jit(solution)/shard_map/ppermute | solution.py:437
  47.1 7.5 %collective-permute-done.5.b_ref = f32[2,272,128]{2,1,0:T(8,128)S(1)} collective-permute-done((f32[2,272,128]{2,1,0:T(8,128)S(1)}, f32[2,272,128]{2,1,0:T(8,128)S(1)}, u32[]{:S(2)}, u32[]{:S(2)}) %collective-permute-start.5) | collective-permute-done | bytes 278560 | tf_op jit(solution)/shard_map/ppermute | solution.py:437
  54.7 0.7 collective-permute-start.6
  55.4 1.4 collective-permute-start.13
  56.8 0.0 collective-permute-start.10
  56.8 13.4 %collective-permute-done.6.b_ref = f32[4,272,128]{2,1,0:T(8,128)S(1)} collective-permute-done((f32[4,272,128]{2,1,0:T(8,128)S(1)}, f32[4,272,128]{2,1,0:T(8,128)S(1)}, u32[]{:S(2)}, u32[]{:S(2)}) %collective-permute-start.6) | collective-permute-done | bytes 557088 | tf_op jit(solution)/shard_map/ppermute | solution.py:437
  70.3 0.1 shard_map.46.own_ref
  70.3 0.1 collective-permute-start.7
  70.4 0.1 collective-permute-start.11
  70.5 2.9 %collective-permute-start.12 = (f32[256,256]{1,0:T(8,128)S(1)}, f32[256,256]{1,0:T(8,128)S(1)}, u32[]{:S(2)}, u32[]{:S(2)}) collective-permute-start(f32[256,256]{1,0:T(8,128)S(1)} %get-tuple-element.38), channel_id=1, source_target_pairs={{0,16},{4,20},{8,24},{12,28},{16,0},{20,4},{24,8},{28,12},{1,17},{... | collective-permute-start | bytes 786440 | tf_op jit(solution)/shard_map/ppermute | solution.py:429
  73.4 6.6 %collective-permute-start.14 = (f32[512,256]{1,0:T(8,128)}, f32[512,256]{1,0:T(8,128)}, u32[]{:S(2)}, u32[]{:S(2)}) collective-permute-start(f32[512,256]{1,0:T(8,128)} %collective-permute-done.10.block_ref), channel_id=1, source_target_pairs={{0,4},{4,0},{8,12},{12,8},{16,20},{20,16},{24,28},{28,24},{1,5},{5... | collective-permute-start | bytes 1572872 | tf_op jit(solution)/shard_map/ppermute | solution.py:429
  80.0 1.8 %gram.1.a_ref = f32[128,128]{1,0:T(8,128)S(1)} custom-call(s32[4]{0:T(128)S(1)} %pad_add_fusion.place_ref, f32[8,272,128]{2,1,0:T(8,128)S(1)} %shard_map.46.own_ref), custom_call_target="tpu_custom_call" | custom-call | flops 427819008 | bytes 1114112 | tf_op jit(solution)/shard_map/gram/pallas_call | solution.py:215
  81.8 14.6 %collective-permute-done.11.block_ref = f32[256,256]{1,0:T(8,128)S(1)} collective-permute-done((f32[256,256]{1,0:T(8,128)S(1)}, f32[256,256]{1,0:T(8,128)S(1)}, u32[]{:S(2)}, u32[]{:S(2)}) %collective-permute-start.11) | collective-permute-done | bytes 262176 | tf_op jit(solution)/shard_map/ppermute | solution.py:429
  96.4 1.7 %collective-permute-start.8 = (f32[128,128]{1,0:T(8,128)S(1)}, f32[128,128]{1,0:T(8,128)S(1)}, u32[]{:S(2)}, u32[]{:S(2)}) collective-permute-start(f32[128,128]{1,0:T(8,128)S(1)} %gram.1.a_ref), channel_id=1, source_target_pairs={{0,8},{4,12},{8,0},{12,4},{16,24},{20,28},{24,16},{28,20},{1,9},{5... | collective-permute-start | bytes 196616 | tf_op jit(solution)/shard_map/ppermute | solution.py:429
  98.1 4.0 %collective-permute-done.12.block_ref = f32[256,256]{1,0:T(8,128)S(1)} collective-permute-done((f32[256,256]{1,0:T(8,128)S(1)}, f32[256,256]{1,0:T(8,128)S(1)}, u32[]{:S(2)}, u32[]{:S(2)}) %collective-permute-start.12) | collective-permute-done | bytes 262176 | tf_op jit(solution)/shard_map/ppermute | solution.py:429
  102.1 0.3 collective-permute-start.15
  102.4 0.7 copy-done
  103.1 0.3 collective-permute-done.8.b_ref
  103.4 1.4 collective-permute-start.16
  104.8 0.6 shard_map.47.gram_ref
  105.4 5.8 %collective-permute-done.15.block_ref = f32[256,256]{1,0:T(8,128)S(1)} collective-permute-done((f32[256,256]{1,0:T(8,128)S(1)}, f32[256,256]{1,0:T(8,128)S(1)}, u32[]{:S(2)}, u32[]{:S(2)}) %collective-permute-start.15) | collective-permute-done | bytes 262176 | tf_op jit(solution)/shard_map/ppermute | solution.py:429
  111.3 0.7 copy-done.2
  112.0 1.6 turn.8
  113.6 0.0 copy-start.1
  113.6 0.9 copy-done.1
  114.5 0.1 turn.10
  114.7 0.1 turn.11
  114.8 1.2 turn.9
  116.1 0.9 copy-done.3
  117.0 0.1 turn.14
  117.2 1.1 turn.15
  118.3 1.6 turn.12
  119.9 1.2 turn.13
  121.1 4.3 %factor.1.inverse_ref = f32[128,128]{1,0:T(8,128)S(1)} custom-call(f32[128,128]{1,0:T(8,128)} %shard_map.47.gram_ref, f32[128,128]{1,0:T(8,128)} %collective-permute-done.9.other_ref), custom_call_target="tpu_custom_call" | custom-call | flops 3000000000 | bytes 131072 | tf_op jit(solution)/shard_map/factor/pallas_call | solution.py:268
  125.5 0.9 assemble.1.refs_16_
  126.4 2.0 %lagged.9 = f32[2,256,128]{2,1,0:T(8,128)S(1)} custom-call(s32[1]{0:T(128)} %bitcast.10.lag_ref, bf16[256,1024]{1,0:T(8,128)(2,1)S(1)} %get-tuple-element.33.refs_0_, bf16[256,512]{1,0:T(8,128)(2,1)S(1)} %get-tuple-element.35.refs_1_, bf16[256,256]{1,0:T(8,128)(2,1)S(1)} %get-tuple-element.37.refs_2_, bf16[256,256]{1,0:T(8,128)(2,1)S(1)} %get-tuple-element.39.refs_3_, ...), custom_call_target="tpu_custom_call" | custom-call | flops 1610612736 | bytes 6684672 | tf_op jit(solution)/shard_map/lagged/pallas_call | solution.py:305
  128.4 2.0 %lagged.8 = f32[2,256,128]{2,1,0:T(8,128)S(1)} custom-call(s32[1]{0:T(128)} %bitcast.9.lag_ref, bf16[256,1024]{1,0:T(8,128)(2,1)S(1)} %get-tuple-element.33.refs_0_, bf16[256,512]{1,0:T(8,128)(2,1)S(1)} %get-tuple-element.35.refs_1_, bf16[256,256]{1,0:T(8,128)(2,1)S(1)} %get-tuple-element.37.refs_2_, bf16[256,256]{1,0:T(8,128)(2,1)S(1)} %get-tuple-element.39.refs_3_, ...), custom_call_target="tpu_custom_call" | custom-call | flops 1610612736 | bytes 6684672 | tf_op jit(solution)/shard_map/lagged/pallas_call | solution.py:305
  130.3 2.0 %lagged.7 = f32[2,256,128]{2,1,0:T(8,128)S(1)} custom-call(s32[1]{0:T(128)} %bitcast.8.lag_ref, bf16[256,1024]{1,0:T(8,128)(2,1)S(1)} %get-tuple-element.33.refs_0_, bf16[256,512]{1,0:T(8,128)(2,1)S(1)} %get-tuple-element.35.refs_1_, bf16[256,256]{1,0:T(8,128)(2,1)S(1)} %get-tuple-element.37.refs_2_, bf16[256,256]{1,0:T(8,128)(2,1)S(1)} %get-tuple-element.39.refs_3_, ...), custom_call_target="tpu_custom_call" | custom-call | flops 1610612736 | bytes 6684672 | tf_op jit(solution)/shard_map/lagged/pallas_call | solution.py:305
  132.3 7.8 %lagged.5.kept_ref = f32[8,256,128]{2,1,0:T(8,128)S(1)} custom-call(s32[1]{0:T(128)} %bitcast.6.lag_ref, bf16[256,1024]{1,0:T(8,128)(2,1)S(1)} %get-tuple-element.33.refs_0_, bf16[256,512]{1,0:T(8,128)(2,1)S(1)} %get-tuple-element.35.refs_1_, bf16[256,256]{1,0:T(8,128)(2,1)S(1)} %get-tuple-element.37.refs_2_, ...), custom_call_target="tpu_custom_call" | custom-call | flops 6442450944 | bytes 7471104 | tf_op jit(solution)/shard_map/lagged/pallas_call | solution.py:305
  140.2 1.7 %collective-permute-start.18 = (f32[2,256,128]{2,1,0:T(8,128)S(1)}, f32[2,256,128]{2,1,0:T(8,128)S(1)}, u32[]{:S(2)}, u32[]{:S(2)}) collective-permute-start(f32[2,256,128]{2,1,0:T(8,128)S(1)} %lagged.7), channel_id=1, source_target_pairs={{0,8},{4,12},{8,0},{12,4},{16,24},{20,28},{24,16},{28,20},{1,9},{5... | collective-permute-start | bytes 786440 | tf_op jit(solution)/shard_map/ppermute | solution.py:429
  141.9 0.3 collective-permute-start.19
  142.3 1.7 %collective-permute-start.20 = (f32[2,256,128]{2,1,0:T(8,128)S(1)}, f32[2,256,128]{2,1,0:T(8,128)S(1)}, u32[]{:S(2)}, u32[]{:S(2)}) collective-permute-start(f32[2,256,128]{2,1,0:T(8,128)S(1)} %lagged.9), channel_id=1, source_target_pairs={{0,8},{4,12},{8,0},{12,4},{16,24},{20,28},{24,16},{28,20},{1,9},{5... | collective-permute-start | bytes 786440 | tf_op jit(solution)/shard_map/ppermute | solution.py:429
  144.0 2.0 %lagged.6 = f32[2,256,128]{2,1,0:T(8,128)S(1)} custom-call(s32[1]{0:T(128)} %bitcast.7.lag_ref, bf16[256,1024]{1,0:T(8,128)(2,1)S(1)} %get-tuple-element.33.refs_0_, bf16[256,512]{1,0:T(8,128)(2,1)S(1)} %get-tuple-element.35.refs_1_, bf16[256,256]{1,0:T(8,128)(2,1)S(1)} %get-tuple-element.37.refs_2_, bf16[256,256]{1,0:T(8,128)(2,1)S(1)} %get-tuple-element.39.refs_3_, ...), custom_call_target="tpu_custom_call" | custom-call | flops 1610612736 | bytes 6684672 | tf_op jit(solution)/shard_map/lagged/pallas_call | solution.py:305
  145.9 0.4 collective-permute-start.17
  146.3 1.4 convolution_multiply_fusion
  147.7 7.4 %collective-permute-done.19.refs_0_ = f32[2,256,128]{2,1,0:T(8,128)S(1)} collective-permute-done((f32[2,256,128]{2,1,0:T(8,128)S(1)}, f32[2,256,128]{2,1,0:T(8,128)S(1)}, u32[]{:S(2)}, u32[]{:S(2)}) %collective-permute-start.19) | collective-permute-done | bytes 262176 | tf_op jit(solution)/shard_map/ppermute | solution.py:429
  155.0 5.6 %collective-permute-done.20.refs_1_ = f32[2,256,128]{2,1,0:T(8,128)S(1)} collective-permute-done((f32[2,256,128]{2,1,0:T(8,128)S(1)}, f32[2,256,128]{2,1,0:T(8,128)S(1)}, u32[]{:S(2)}, u32[]{:S(2)}) %collective-permute-start.20) | collective-permute-done | bytes 262176 | tf_op jit(solution)/shard_map/ppermute | solution.py:429
  160.7 1.2 finish.3.refs_1_
  161.9 1.0 finish.4.refs_1_
  163.0 2.9 %collective-permute-done.17.refs_0_ = f32[2,256,128]{2,1,0:T(8,128)S(1)} collective-permute-done((f32[2,256,128]{2,1,0:T(8,128)S(1)}, f32[2,256,128]{2,1,0:T(8,128)S(1)}, u32[]{:S(2)}, u32[]{:S(2)}) %collective-permute-start.17) | collective-permute-done | bytes 262176 | tf_op jit(solution)/shard_map/ppermute | solution.py:429
  165.8 1.0 finish.5
  (15 shorter events, 0.1 us)
Async XLA Ops:
  2.1 5.3 %collective-permute-start = (f32[64,256]{1,0:T(8,128)S(1)}, f32[64,256]{1,0:T(8,128)S(1)}, u32[]{:S(2)}, u32[]{:S(2)}) collective-permute-start(f32[64,256]{1,0:T(8,128)S(1)} %get-tuple-element.27), channel_id=1, source_target_pairs={{0,4},{4,0},{8,12},{12,8},{16,20},{20,16},{24,28},{28,24},{1,5},{5... | collective-permute-start | bytes 196616 | tf_op jit(solution)/shard_map/ppermute | solution.py:429
  5.1 2.2 %collective-permute-start.1 = (f32[64,256]{1,0:T(8,128)S(1)}, f32[64,256]{1,0:T(8,128)S(1)}, u32[]{:S(2)}, u32[]{:S(2)}) collective-permute-start(f32[64,256]{1,0:T(8,128)S(1)} %get-tuple-element.28), channel_id=1, source_target_pairs={{4,8},{8,4},{12,16},{16,12},{20,24},{24,20},{5,9},{9,5},{13,17},{1... | collective-permute-start | bytes 196616 | tf_op jit(solution)/shard_map/ppermute | solution.py:429
  26.5 1.6 collective-permute-start.2
  28.2 6.1 %collective-permute-start.3 = (f32[1,272,128]{2,1,0:T(8,128)S(1)}, f32[1,272,128]{2,1,0:T(8,128)S(1)}, u32[]{:S(2)}, u32[]{:S(2)}) collective-permute-start(f32[1,272,128]{2,1,0:T(8,128)S(1)} %get-tuple-element.32), channel_id=1, source_target_pairs={{0,2},{1,3},{2,0},{3,1},{4,6},{5,7},{6,4},{7,5},{8,10},{9,11},{10,... | collective-permute-start | bytes 417800 | tf_op jit(solution)/shard_map/ppermute | solution.py:429
  34.9 5.1 %collective-permute-start.4 = (f32[1,272,128]{2,1,0:T(8,128)S(1)}, f32[1,272,128]{2,1,0:T(8,128)S(1)}, u32[]{:S(2)}, u32[]{:S(2)}) collective-permute-start(f32[1,272,128]{2,1,0:T(8,128)S(1)} %shard_map.43.a_ref), channel_id=1, source_target_pairs={{0,2},{1,17},{2,0},{3,19},{4,6},{5,21},{6,4},{7,23},{8,10},{9,25},... | collective-permute-start | bytes 417800 | tf_op jit(solution)/shard_map/ppermute | solution.py:437
  40.0 14.7 %collective-permute-start.5 = (f32[2,272,128]{2,1,0:T(8,128)S(1)}, f32[2,272,128]{2,1,0:T(8,128)S(1)}, u32[]{:S(2)}, u32[]{:S(2)}) collective-permute-start(f32[2,272,128]{2,1,0:T(8,128)S(1)} %shard_map.44.a_ref), channel_id=1, source_target_pairs={{0,16},{1,5},{2,18},{3,7},{4,20},{5,1},{6,22},{7,3},{8,24},{9,13},... | collective-permute-start | bytes 835592 | tf_op jit(solution)/shard_map/ppermute | solution.py:437
  54.7 15.6 %collective-permute-start.6 = (f32[4,272,128]{2,1,0:T(8,128)S(1)}, f32[4,272,128]{2,1,0:T(8,128)S(1)}, u32[]{:S(2)}, u32[]{:S(2)}) collective-permute-start(f32[4,272,128]{2,1,0:T(8,128)S(1)} %shard_map.45.a_ref), channel_id=1, source_target_pairs={{0,4},{1,3},{2,6},{3,1},{4,0},{5,7},{6,2},{7,5},{8,12},{9,11},{10,... | collective-permute-start | bytes 1671176 | tf_op jit(solution)/shard_map/ppermute | solution.py:437
  55.4 62.9 %collective-permute-start.13 = (f32[1024,256]{1,0:T(8,128)}, f32[1024,256]{1,0:T(8,128)}, u32[]{:S(2)}, u32[]{:S(2)}) collective-permute-start(f32[1024,256]{1,0:T(8,128)} %block_ref.1), channel_id=1, source_target_pairs={{0,4},{4,0},{8,12},{12,8},{16,20},{20,16},{24,28},{28,24},{1,5},{5... | collective-permute-start | bytes 3145736 | tf_op jit(solution)/shard_map/ppermute | solution.py:429
  56.8 16.6 %collective-permute-start.10 = (f32[512,256]{1,0:T(8,128)S(1)}, f32[512,256]{1,0:T(8,128)}, u32[]{:S(2)}, u32[]{:S(2)}) collective-permute-start(f32[512,256]{1,0:T(8,128)S(1)} %get-tuple-element.34), channel_id=1, source_target_pairs={{0,16},{4,20},{8,24},{12,28},{16,0},{20,4},{24,8},{28,12},{1,17},{... | collective-permute-start | bytes 1572872 | tf_op jit(solution)/shard_map/ppermute | solution.py:429
  70.3 55.1 %collective-permute-start.7 = (f32[8,272,128]{2,1,0:T(8,128)S(1)}, f32[8,272,128]{2,1,0:T(8,128)S(1)}, u32[]{:S(2)}, u32[]{:S(2)}) collective-permute-start(f32[8,272,128]{2,1,0:T(8,128)S(1)} %shard_map.46.own_ref), channel_id=1, source_target_pairs={{0,1},{1,0},{2,3},{3,2},{4,5},{5,4},{6,7},{7,6},{8,9},{9,8},{10,11... | collective-permute-start | bytes 3342344 | tf_op jit(solution)/shard_map/ppermute | solution.py:429
  70.4 26.0 %collective-permute-start.11 = (f32[256,256]{1,0:T(8,128)S(1)}, f32[256,256]{1,0:T(8,128)S(1)}, u32[]{:S(2)}, u32[]{:S(2)}) collective-permute-start(f32[256,256]{1,0:T(8,128)S(1)} %get-tuple-element.36), channel_id=1, source_target_pairs={{0,16},{4,20},{8,24},{12,28},{16,0},{20,4},{24,8},{28,12},{1,17},{... | collective-permute-start | bytes 786440 | tf_op jit(solution)/shard_map/ppermute | solution.py:429
  70.5 31.6 %collective-permute-start.12 = (f32[256,256]{1,0:T(8,128)S(1)}, f32[256,256]{1,0:T(8,128)S(1)}, u32[]{:S(2)}, u32[]{:S(2)}) collective-permute-start(f32[256,256]{1,0:T(8,128)S(1)} %get-tuple-element.38), channel_id=1, source_target_pairs={{0,16},{4,20},{8,24},{12,28},{16,0},{20,4},{24,8},{28,12},{1,17},{... | collective-permute-start | bytes 786440 | tf_op jit(solution)/shard_map/ppermute | solution.py:429
  73.4 46.4 %collective-permute-start.14 = (f32[512,256]{1,0:T(8,128)}, f32[512,256]{1,0:T(8,128)}, u32[]{:S(2)}, u32[]{:S(2)}) collective-permute-start(f32[512,256]{1,0:T(8,128)} %collective-permute-done.10.block_ref), channel_id=1, source_target_pairs={{0,4},{4,0},{8,12},{12,8},{16,20},{20,16},{24,28},{28,24},{1,5},{5... | collective-permute-start | bytes 1572872 | tf_op jit(solution)/shard_map/ppermute | solution.py:429
  96.4 7.0 %collective-permute-start.8 = (f32[128,128]{1,0:T(8,128)S(1)}, f32[128,128]{1,0:T(8,128)S(1)}, u32[]{:S(2)}, u32[]{:S(2)}) collective-permute-start(f32[128,128]{1,0:T(8,128)S(1)} %gram.1.a_ref), channel_id=1, source_target_pairs={{0,8},{4,12},{8,0},{12,4},{16,24},{20,28},{24,16},{28,20},{1,9},{5... | collective-permute-start | bytes 196616 | tf_op jit(solution)/shard_map/ppermute | solution.py:429
  102.1 9.2 %collective-permute-start.15 = (f32[256,256]{1,0:T(8,128)S(1)}, f32[256,256]{1,0:T(8,128)S(1)}, u32[]{:S(2)}, u32[]{:S(2)}) collective-permute-start(f32[256,256]{1,0:T(8,128)S(1)} %collective-permute-done.11.block_ref), channel_id=1, source_target_pairs={{0,4},{4,0},{8,12},{12,8},{16,20},{20,16},{24,28},{28,24},{1,5},{5... | collective-permute-start | bytes 786440 | tf_op jit(solution)/shard_map/ppermute | solution.py:429
  102.3 0.7 copy-start
  103.4 13.8 %collective-permute-start.16 = (f32[256,256]{1,0:T(8,128)S(1)}, f32[256,256]{1,0:T(8,128)}, u32[]{:S(2)}, u32[]{:S(2)}) collective-permute-start(f32[256,256]{1,0:T(8,128)S(1)} %collective-permute-done.12.block_ref), channel_id=1, source_target_pairs={{0,4},{4,0},{8,12},{12,8},{16,20},{20,16},{24,28},{28,24},{1,5},{5... | collective-permute-start | bytes 786440 | tf_op jit(solution)/shard_map/ppermute | solution.py:429
  111.3 0.7 copy-start.2
  112.0 9.1 %collective-permute-start.9 = (f32[128,128]{1,0:T(8,128)}, f32[128,128]{1,0:T(8,128)}, u32[]{:S(2)}, u32[]{:S(2)}) collective-permute-start(f32[128,128]{1,0:T(8,128)} %shard_map.47.gram_ref), channel_id=1, source_target_pairs={{0,1},{1,0},{2,3},{3,2},{4,5},{5,4},{6,7},{7,6},{8,9},{9,8},{10,11... | collective-permute-start | bytes 196616 | tf_op jit(solution)/shard_map/ppermute | solution.py:429
  113.6 1.0 copy-start.1
  116.1 1.0 copy-start.3
  140.2 21.7 %collective-permute-start.18 = (f32[2,256,128]{2,1,0:T(8,128)S(1)}, f32[2,256,128]{2,1,0:T(8,128)S(1)}, u32[]{:S(2)}, u32[]{:S(2)}) collective-permute-start(f32[2,256,128]{2,1,0:T(8,128)S(1)} %lagged.7), channel_id=1, source_target_pairs={{0,8},{4,12},{8,0},{12,4},{16,24},{20,28},{24,16},{28,20},{1,9},{5... | collective-permute-start | bytes 786440 | tf_op jit(solution)/shard_map/ppermute | solution.py:429
  141.9 13.1 %collective-permute-start.19 = (f32[2,256,128]{2,1,0:T(8,128)S(1)}, f32[2,256,128]{2,1,0:T(8,128)S(1)}, u32[]{:S(2)}, u32[]{:S(2)}) collective-permute-start(f32[2,256,128]{2,1,0:T(8,128)S(1)} %lagged.8), channel_id=1, source_target_pairs={{0,8},{4,12},{8,0},{12,4},{16,24},{20,28},{24,16},{28,20},{1,9},{5... | collective-permute-start | bytes 786440 | tf_op jit(solution)/shard_map/ppermute | solution.py:429
  142.3 18.4 %collective-permute-start.20 = (f32[2,256,128]{2,1,0:T(8,128)S(1)}, f32[2,256,128]{2,1,0:T(8,128)S(1)}, u32[]{:S(2)}, u32[]{:S(2)}) collective-permute-start(f32[2,256,128]{2,1,0:T(8,128)S(1)} %lagged.9), channel_id=1, source_target_pairs={{0,8},{4,12},{8,0},{12,4},{16,24},{20,28},{24,16},{28,20},{1,9},{5... | collective-permute-start | bytes 786440 | tf_op jit(solution)/shard_map/ppermute | solution.py:429
  145.9 19.9 %collective-permute-start.17 = (f32[2,256,128]{2,1,0:T(8,128)S(1)}, f32[2,256,128]{2,1,0:T(8,128)S(1)}, u32[]{:S(2)}, u32[]{:S(2)}) collective-permute-start(f32[2,256,128]{2,1,0:T(8,128)S(1)} %lagged.6), channel_id=1, source_target_pairs={{0,8},{4,12},{8,0},{12,4},{16,24},{20,28},{24,16},{28,20},{1,9},{5... | collective-permute-start | bytes 786440 | tf_op jit(solution)/shard_map/ppermute | solution.py:429

commit v4 on v3

--- a/solution.py
+++ b/solution.py
@@ -30,7 +30,7 @@
     return dot(a_high, b_high) + dot(a_high, b_low) + dot(a_low, b_high)
 
 
-def sketch_kernel(place_ref, beside_ref, record_ref, beyond_ref, weight_ref, *refs):
+def sketch_kernel(place_ref, record_ref, weight_ref, *refs):
     keep_ref, give_ref, high, low, even, odd, total, buffer, arrived = refs
     pair = pl.program_id(0)
     rows, width = total.shape
@@ -53,24 +53,12 @@
 
     @pl.when(pair == 0)
     def _():
-        def place_rows(first, ref):
-            part = slice(first, first + ref.shape[0])
-            high[part], low[part] = split(ref[...])
-
-        rim = beside_ref.shape[0]
-        last = rim + record_ref.shape[0]
-        place_rows(rim, record_ref)
-
-        @pl.when(lax.rem(place_ref[1], 2) == 0)
-        def _():
-            place_rows(0, beyond_ref)
-            place_rows(last, beside_ref)
-
-        @pl.when(lax.rem(place_ref[1], 2) == 1)
-        def _():
-            place_rows(0, beside_ref)
-            place_rows(last, beyond_ref)
-
+        rim = rows - record_ref.shape[0]
+        last = high.shape[0] - rim
+        for ref, value in ((high, 0), (low, 1)):
+            ref[:rim] = jnp.zeros((rim, ref.shape[1]), BF16)
+            ref[last:] = jnp.zeros((rim, ref.shape[1]), BF16)
+            ref[rim:last] = split(record_ref[...])[value]
         total[...] = jnp.zeros_like(total)
 
     fetch(pair).wait()
@@ -98,15 +86,15 @@
                 ref[n] = total[pl.ds(pl.multiple_of(owner * share, 8), share), :]
 
 
-def sketch(place, beside, record, beyond, weights, shares):
+def sketch(place, record, weights, shares):
     lags, chans, width = weights.shape
-    rows = beside.shape[0] + record.shape[0]
-    length = rows + beyond.shape[0]
+    rows = lags + record.shape[0]
+    length = rows + lags
     share = rows // shares
     return pl.pallas_call(
         sketch_kernel,
         grid=(STEP // 2,),
-        in_specs=[SMEM, VMEM, VMEM, VMEM, pl.BlockSpec(memory_space=pltpu.HBM)],
+        in_specs=[SMEM, VMEM, pl.BlockSpec(memory_space=pltpu.HBM)],
         out_specs=[VMEM] * 2,
         out_shape=[jax.ShapeDtypeStruct((2, share, width), F32)] * 2,
         scratch_shapes=[
@@ -124,7 +112,13 @@
             4 * (lags * chans * width + length * chans + rows * width),
         ),
         name="sketch",
-    )(place, beside, record, beyond, pltpu.with_memory_space_constraint(weights.reshape(lags // STEP, STEP, chans, width), pltpu.HBM))
+    )(
+        place,
+        record,
+        pltpu.with_memory_space_constraint(
+            weights.reshape(lags // STEP, STEP, chans, width), pltpu.HBM
+        ),
+    )
 
 
 def turn_kernel(block_ref, high_ref, low_ref):
@@ -144,19 +138,40 @@
     )(block)
 
 
-def assemble_kernel(place_ref, own_ref, got_ref, out_ref):
-    pieces, share, _ = own_ref.shape
-    blocks = pieces // 2
-    low, high = place_ref[2], place_ref[3]
+def even_piece(block, pair):
+    return 4 * (block // 2) + 2 * pair + block % 2
+
+
+def assemble_kernel(mids, place_ref, own_ref, got_ref, edge_own_ref, edge_got_ref, out_ref):
+    _, share, _ = own_ref.shape
+    blocks, rim, _ = edge_own_ref.shape
+    low, high, outer, middle = place_ref[2], place_ref[3], place_ref[5], place_ref[6]
+    end = out_ref.shape[1] - rim
 
     def place(first_ref, second_ref):
         for b in range(blocks):
             for q in range(2):
                 owner = 2 * jnp.bitwise_xor(high, q)
                 first = pl.multiple_of(owner * share, 8)
-                out_ref[b, pl.ds(first, share), :] = first_ref[2 * b + q]
+                out_ref[b, pl.ds(first, share), :] = first_ref[even_piece(b, q)]
                 out_ref[b, pl.ds(pl.multiple_of(first + share, 8), share), :] = second_ref[blocks * q + b]
 
+    def edges(inner, heads_ref, tails_ref):
+        for z in range(2):
+            left, right = (z, z + 2) if inner == 0 else (z + 2, z)
+            side = jnp.bitwise_xor(outer, z)
+            value = out_ref[left, end:] + out_ref[right, :rim]
+            out_ref[left, end:] = value
+            out_ref[right, :rim] = value
+            tail = 2 * (1 - inner)
+            value = jnp.where(middle > 0, tails_ref[tail + z], tails_ref[tail + 1 - z])
+            some = (middle > 0) | (side == 1)
+            out_ref[left, :rim] = jnp.where(some, out_ref[left, :rim] + value, 0.0)
+            head = 2 * inner
+            value = jnp.where(middle < mids - 1, heads_ref[head + z], heads_ref[head + 1 - z])
+            some = (middle < mids - 1) | (side == 0)
+            out_ref[right, end:] = out_ref[right, end:] + jnp.where(some, value, 0.0)
+
     @pl.when(low == 0)
     def _():
         place(own_ref, got_ref)
@@ -165,49 +180,58 @@
     def _():
         place(got_ref, own_ref)
 
-
-def assemble(place, own, got, shares):
+    for inner in range(2):
+
+        @pl.when((place_ref[4] == inner) & (low == 0))
+        def _():
+            edges(inner, edge_own_ref, edge_got_ref)
+
+        @pl.when((place_ref[4] == inner) & (low == 1))
+        def _():
+            edges(inner, edge_got_ref, edge_own_ref)
+
+
+def assemble(place, own, got, edge_own, edge_got, shares, mids):
     pieces, share, width = own.shape
     blocks = pieces // 2
     return pl.pallas_call(
-        assemble_kernel,
-        in_specs=[SMEM, VMEM, VMEM],
+        functools.partial(assemble_kernel, mids),
+        in_specs=[SMEM, VMEM, VMEM, VMEM, VMEM],
         out_specs=VMEM,
         out_shape=jax.ShapeDtypeStruct((blocks, shares * share, width), F32),
-        compiler_params=pltpu.CompilerParams(vmem_limit_bytes=20 * 2**20),
+        compiler_params=pltpu.CompilerParams(vmem_limit_bytes=12 * 2**20),
         cost_estimate=cost(0, 8 * blocks * shares * share * width),
         name="assemble",
-    )(place, own, got)
+    )(place, own, got, edge_own, edge_got)
 
 
 def gram_kernel(rim, place_ref, own_ref, out_ref):
     pieces, share, width = own_ref.shape
     blocks = pieces // 2
     low, high = place_ref[2], place_ref[3]
-    kept = lax.broadcasted_iota(jnp.int32, (share, width), 0) >= rim
+    row = lax.broadcasted_iota(jnp.int32, (share, width), 0)
 
     def gram(value):
         return lax.dot_general(
             value, value, (((0,), (0,)), ((), ())), precision=HIGHEST, preferred_element_type=F32
         )
 
-    @pl.when(low == 0)
-    def _():
+    def both(kept, piece):
         halves = []
         for q in range(2):
             value = jnp.concatenate(
-                [jnp.where(kept | (high != q), own_ref[2 * b + q], 0.0) for b in range(blocks)], axis=0
+                [jnp.where(kept(q), own_ref[piece(b, q)], 0.0) for b in range(blocks)], axis=0
             )
             halves.append(gram(value))
         out_ref[...] = halves[0] + halves[1]
 
+    @pl.when(low == 0)
+    def _():
+        both(lambda q: (row >= rim) | (high != q), even_piece)
+
     @pl.when(low == 1)
     def _():
-        halves = []
-        for q in range(2):
-            value = jnp.concatenate([own_ref[blocks * q + b] for b in range(blocks)], axis=0)
-            halves.append(gram(value))
-        out_ref[...] = halves[0] + halves[1]
+        both(lambda q: (row < share - rim) | (high == q), lambda b, q: blocks * q + b)
 
 
 def gram_of(place, own, rim):
@@ -354,27 +378,13 @@
         in_specs=[SMEM] * smem + [VMEM] * (len(args) - smem),
         out_specs=[VMEM] * len(shapes),
         out_shape=shapes,
-        compiler_params=pltpu.CompilerParams(vmem_limit_bytes=6 * 2**20),
+        compiler_params=pltpu.CompilerParams(vmem_limit_bytes=8 * 2**20),
         cost_estimate=cost(size, 4 * size),
     )(*args)
     return outs[0] if len(outs) == 1 else outs
 
 
-def cut_kernel(place_ref, record_ref, *outs):
-    rows = record_ref.shape[0]
-    beside_ref, beyond_ref, *parts = outs
-    rim = beside_ref.shape[0]
-
-    @pl.when(lax.rem(place_ref[1], 2) == 0)
-    def _():
-        beside_ref[...] = record_ref[rows - rim :]
-        beyond_ref[...] = record_ref[:rim]
-
-    @pl.when(lax.rem(place_ref[1], 2) == 1)
-    def _():
-        beside_ref[...] = record_ref[:rim]
-        beyond_ref[...] = record_ref[rows - rim :]
-
+def cut_kernel(record_ref, *parts):
     first = 0
     for ref in parts:
         ref[...] = record_ref[first : first + ref.shape[0]]
@@ -382,15 +392,33 @@
 
 
 def add_pair_kernel(keep_ref, got_ref, own_ref, pass_ref):
-    own_ref[...] = keep_ref[:1] + got_ref[:1]
-    pass_ref[...] = keep_ref[1:] + got_ref[1:]
-
-
-def add_masked_kernel(rim, place_ref, own_ref, got_ref, out_ref):
-    value = own_ref[...] + got_ref[...]
-    row = lax.broadcasted_iota(jnp.int32, value.shape, 1)
-    kept = (row >= rim) | (place_ref[0] > 0) | (place_ref[1] > 0)
-    out_ref[...] = jnp.where(kept, value, 0.0)
+    own_ref[0] = keep_ref[0] + got_ref[0]
+    pass_ref[0] = keep_ref[1] + got_ref[1]
+
+
+def join_edges_kernel(place_ref, a_ref, b_ref, out_ref, edge_ref):
+    join_kernel(a_ref, b_ref, out_ref)
+    blocks, rim, _ = edge_ref.shape
+    share = a_ref.shape[1]
+    for high in range(2):
+
+        @pl.when((place_ref[2] == 0) & (place_ref[3] == high))
+        def _():
+            for b in range(blocks):
+                edge_ref[b] = out_ref[even_piece(b, high), :rim]
+
+        @pl.when((place_ref[2] == 1) & (place_ref[3] == high))
+        def _():
+            for b in range(blocks):
+                edge_ref[b] = out_ref[blocks * (1 - high) + b, share - rim :]
+
+
+def edge_gram_kernel(rim, sketch_ref, a_ref, b_ref, out_ref):
+    blocks, length, _ = sketch_ref.shape
+    value = jnp.concatenate([sketch_ref[b, length - rim :] for b in range(blocks)], axis=0)
+    out_ref[...] = (a_ref[...] + b_ref[...]) + lax.dot_general(
+        value, value, (((0,), (0,)), ((), ())), precision=HIGHEST, preferred_element_type=F32
+    )
 
 
 def join_kernel(a_ref, b_ref, out_ref):
@@ -421,7 +449,9 @@
     mids = n_time // 4
     per = lags // n_time
     rim = lags
-    place = jnp.stack([mine, here, mine % 2, mine // 2])
+    place = jnp.stack(
+        [mine, here, mine % 2, mine // 2, here % 2, here // half, (here % half) // 2]
+    ).astype(jnp.int32)
 
     def to(block, target, axis="tm"):
         count = lax.axis_size(axis)
@@ -433,8 +463,12 @@
         for t in range(n_time):
             for c in range(n_chan):
                 a, b = target(t, c)
-                route.append((t * n_chan + c, a * n_chan + b))
+                if 0 <= a < n_time:
+                    route.append((t * n_chan + c, a * n_chan + b))
         return lax.ppermute(block, ("tm", "chan"), route)
+
+    def even(c):
+        return c % 2 == 0
 
     def beside(t):
         return t ^ 1
@@ -443,39 +477,43 @@
         return (t + half) % n_time
 
     cut = [0, rows // 2, 3 * rows // 4, rows]
-    sizes = [rim, rim] + [b - a for a, b in zip(cut, cut[1:])]
-    at_beside, at_beyond, *parts = small(cut_kernel, [(n, chans) for n in sizes], place, record, smem=1)
-    at_beyond = to(at_beyond, lambda i: i - 1 + 2 * (i % 2))
-    at_beside = to(at_beside, beside)
+    parts = small(cut_kernel, [(b - a, chans) for a, b in zip(cut, cut[1:])], record)
     beside_record = to(record, beside)
     across_parts = [to(part, across) for part in parts]
     both_parts = [to(part, beside) for part in across_parts]
 
-    keep, give = sketch(place, at_beside, record, at_beyond, test_matrix, n_chan)
+    keep, give = sketch(place, record, test_matrix, n_chan)
     share = keep.shape[1]
     got = to(give, lambda i: i ^ 1, "chan")
     own, passed = small(add_pair_kernel, [(1, share, width)] * 2, keep, got)
-    got = to(passed, lambda i: i ^ 2, "chan")
-    own = small(functools.partial(add_masked_kernel, rim), [own.shape], place, own, got, smem=1)
-
-    def even(c):
-        return c % 2 == 0
-
-    got = to_both(own, lambda t, c: (t, c ^ 2) if even(c) else (across(t), c))
-    own = joined(own, got)
-    got = to_both(own, lambda t, c: (across(t), c) if even(c) else (beside(t), c))
+    own = added(own, to(passed, lambda i: i ^ 2, "chan"))
+
+    own = joined(own, to_both(own, lambda t, c: (across(t), c)))
+    got = to_both(own, lambda t, c: (t, c ^ 2) if even(c) else (beside(t), c))
     own = joined(own, got)
     got = to_both(own, lambda t, c: (beside(t), c) if even(c) else (t, c ^ 2))
-    own = joined(own, got)
+    own, edge = small(
+        join_edges_kernel, [(2 * own.shape[0], share, width), (own.shape[0], rim, width)], place, own, got, smem=1
+    )
     got = to(own, lambda i: i ^ 1, "chan")
+
+    def neighbour(t, step):
+        middle = (t % half) // 2
+        return t - 2 * middle + 2 * ((middle + step) % mids)
+
+    edge = to_both(edge, lambda t, c: (neighbour(t, -1 if even(c) else 1), c))
+    edge_got = to(edge, lambda i: i ^ 1, "chan")
     gram = gram_of(place, own, rim)
+    gram_got = to(gram, lambda i: i ^ 1, "chan")
+    sketches = assemble(place, own, got, edge, edge_got, n_chan, mids)
+    gram = small(functools.partial(edge_gram_kernel, rim), [gram.shape], sketches, gram, gram_got)
+    other = jnp.zeros_like(gram)
     distance = 2
     while distance < half:
+        if distance > 2:
+            gram = added(gram, other)
         other = to(gram, lambda i: i ^ distance)
-        gram = added(gram, other)
         distance *= 2
-    gram_other = to(gram, lambda i: i ^ 1, "chan")
-    sketches = assemble(place, own, got, n_chan)
 
     turned = [turn(record)]
     turned += [turn(p) for p in across_parts]
@@ -494,14 +532,13 @@
     received = []
     for s in range(1, mids):
         def route(i):
-            m = (i % half) // 2
-            return i - 2 * m + 2 * ((m + s) % mids)
+            return neighbour(i, s)
 
         for n in range(chunks):
             part = lagged(owner_lag(s) + n * size, turned, places, sketches, size)
             received.append(to(part, route))
     kept = lagged(owner_lag(0), turned, places, sketches, per)
-    inverse = factor(gram, gram_other)
+    inverse = factor(gram, other)
 
     def whitened(x):
         return lax.dot_general(

time: 167 us -> 181 us (1.084)
  waiting for transfers between devices: 72 us -> 95.2 us
  starting transfers between devices: 34.1 us -> 23 us
    ppermute x18 -> x17, waiting for transfers between devices: 47.8 us -> 70.8 us  [to(): return lax.ppermute(block, axis, route)]
    ppermute x18 -> x17, starting transfers between devices: 24.4 us -> 17.1 us  [to(): return lax.ppermute(block, axis, route)]
    ppermute x3 -> x4, starting transfers between devices: 9.66 us -> 5.91 us  [to_both(): return lax.ppermute(block, ('tm', 'chan'), route)]
    unnamed x8 -> x12, local copies, waits for them, and re-layouts: 3.29 us -> 4.94 us
    ppermute x3 -> x4, waiting for transfers between devices: 24.3 us -> 24.5 us  [to_both(): return lax.ppermute(block, ('tm', 'chan'), route)]
  transfers between devices with their start and end apart: 21 -> 21, of which waited for: 13 -> 12; matrix products, arithmetic and copies ran while one was open for 1% -> 1% of each run, Pallas kernels for 11% -> 18%
where the time goes in v4:
time: 181 us
  waiting for transfers between devices  95.2 us (53%)
  Pallas kernels  55.2 us (30%)
  starting transfers between devices  23 us (13%)
  local copies, waits for them, and re-layouts  5.02 us (3%)
    ppermute x17, waiting for transfers between devices, to(): return lax.ppermute(block, axis, route)  70.8 us
    ppermute x4, waiting for transfers between devices, to_both(): return lax.ppermute(block, ('tm', 'chan'), route)  24.5 us
    pallas_call x1, Pallas kernels, sketch(): pl.pallas_call(sketch_kernel, grid=(STEP // 2,), in_specs=[SMEM, VMEM, pl...  19.2 us
    ppermute x17, starting transfers between devices, to(): return lax.ppermute(block, axis, route)  17.1 us
    pallas_call x5, Pallas kernels, lagged(): pl.pallas_call(functools.partial(lagged_kernel, places), grid=(lags // 2,...  16 us
    pallas_call x8, Pallas kernels, turn(): pl.pallas_call(turn_kernel, in_specs=[VMEM], out_specs=[VMEM] * 2, out_sh...  6.18 us
    ppermute x4, starting transfers between devices, to_both(): return lax.ppermute(block, ('tm', 'chan'), route)  5.91 us
    unnamed x12, local copies, waits for them, and re-layouts  4.94 us
  transfers between devices with their start and end apart: 21, of which 12 were waited for; matrix products, arithmetic and copies ran while one was open for 1% of the time, Pallas kernels for 18%

profile of v4, /device:TPU:0, one launch (start us, length us, event | category | flops | bytes accessed | tf_op | source)
XLA Modules:
  0.0 180.8 jit_solution(7456766690276067721)
XLA Ops:
  0.7 0.1 stack.31.place_ref
  0.8 19.2 %sketch.1 = (f32[2,272,128]{2,1,0:T(8,128)S(1)}, f32[2,272,128]{2,1,0:T(8,128)S(1)}) custom-call(s32[7]{0:T(128)S(1)} %stack.31.place_ref, f32[1024,256]{1,0:T(8,128)} %record_ref.3, f32[4,16,256,128]{3,2,1,0:T(8,128)} %bitcast.17), custom_call_target="tpu_custom_call" | custom-call | flops 13690208256 | bytes 10125312 | tf_op jit(solution)/shard_map/sketch/pallas_call | solution.py:94
  20.0 0.6 collective-permute-start
  20.5 1.2 collective-permute-done.got_ref
  21.8 2.9 %collective-permute-start.1 = (f32[1,272,128]{2,1,0:T(8,128)S(1)}, f32[1,272,128]{2,1,0:T(8,128)S(1)}, u32[]{:S(2)}, u32[]{:S(2)}) collective-permute-start(f32[1,272,128]{2,1,0:T(8,128)S(1)} %get-tuple-element.30), channel_id=1, source_target_pairs={{0,2},{1,3},{2,0},{3,1},{4,6},{5,7},{6,4},{7,5},{8,10},{9,11},{10,... | collective-permute-start | bytes 417800 | tf_op jit(solution)/shard_map/ppermute | solution.py:459
  24.7 4.0 %collective-permute-done.1.b_ref = f32[1,272,128]{2,1,0:T(8,128)S(1)} collective-permute-done((f32[1,272,128]{2,1,0:T(8,128)S(1)}, f32[1,272,128]{2,1,0:T(8,128)S(1)}, u32[]{:S(2)}, u32[]{:S(2)}) %collective-permute-start.1) | collective-permute-done | bytes 139296 | tf_op jit(solution)/shard_map/ppermute | solution.py:459
  28.7 2.9 %collective-permute-start.2 = (f32[1,272,128]{2,1,0:T(8,128)S(1)}, f32[1,272,128]{2,1,0:T(8,128)S(1)}, u32[]{:S(2)}, u32[]{:S(2)}) collective-permute-start(f32[1,272,128]{2,1,0:T(8,128)S(1)} %shard_map.42.a_ref), channel_id=1, source_target_pairs={{0,16},{1,17},{2,18},{3,19},{4,20},{5,21},{6,22},{7,23},{8,24},{9,... | collective-permute-start | bytes 417800 | tf_op jit(solution)/shard_map/ppermute | solution.py:468
  31.6 6.2 %collective-permute-done.2.b_ref = f32[1,272,128]{2,1,0:T(8,128)S(1)} collective-permute-done((f32[1,272,128]{2,1,0:T(8,128)S(1)}, f32[1,272,128]{2,1,0:T(8,128)S(1)}, u32[]{:S(2)}, u32[]{:S(2)}) %collective-permute-start.2) | collective-permute-done | bytes 139296 | tf_op jit(solution)/shard_map/ppermute | solution.py:468
  37.8 1.5 collective-permute-start.3
  39.3 5.1 %collective-permute-done.3.b_ref = f32[2,272,128]{2,1,0:T(8,128)S(1)} collective-permute-done((f32[2,272,128]{2,1,0:T(8,128)S(1)}, f32[2,272,128]{2,1,0:T(8,128)S(1)}, u32[]{:S(2)}, u32[]{:S(2)}) %collective-permute-start.3) | collective-permute-done | bytes 278560 | tf_op jit(solution)/shard_map/ppermute | solution.py:468
  44.5 1.5 collective-permute-start.4
  46.0 8.1 %collective-permute-done.4.b_ref = f32[4,272,128]{2,1,0:T(8,128)S(1)} collective-permute-done((f32[4,272,128]{2,1,0:T(8,128)S(1)}, f32[4,272,128]{2,1,0:T(8,128)S(1)}, u32[]{:S(2)}, u32[]{:S(2)}) %collective-permute-start.4) | collective-permute-done | bytes 557088 | tf_op jit(solution)/shard_map/ppermute | solution.py:468
  54.1 0.6 shard_map.45
  54.7 0.1 collective-permute-start.5
  54.8 1.3 shard_map.47
  56.1 0.1 collective-permute-start.10
  56.2 1.5 collective-permute-start.13
  57.7 2.8 %collective-permute-start.11 = (f32[256,256]{1,0:T(8,128)S(1)}, f32[256,256]{1,0:T(8,128)S(1)}, u32[]{:S(2)}, u32[]{:S(2)}) collective-permute-start(f32[256,256]{1,0:T(8,128)S(1)} %get-tuple-element.36), channel_id=1, source_target_pairs={{0,16},{4,20},{8,24},{12,28},{16,0},{20,4},{24,8},{28,12},{1,17},{... | collective-permute-start | bytes 786440 | tf_op jit(solution)/shard_map/ppermute | solution.py:459
  60.5 0.1 collective-permute-start.12
  60.6 33.8 %collective-permute-done.10.block_ref = f32[512,256]{1,0:T(8,128)} collective-permute-done((f32[512,256]{1,0:T(8,128)S(1)}, f32[512,256]{1,0:T(8,128)}, u32[]{:S(2)}, u32[]{:S(2)}) %collective-permute-start.10) | collective-permute-done | bytes 524320 | tf_op jit(solution)/shard_map/ppermute | solution.py:459
  94.4 1.4 collective-permute-start.14
  95.9 4.1 %collective-permute-done.11.block_ref = f32[256,256]{1,0:T(8,128)S(1)} collective-permute-done((f32[256,256]{1,0:T(8,128)S(1)}, f32[256,256]{1,0:T(8,128)S(1)}, u32[]{:S(2)}, u32[]{:S(2)}) %collective-permute-start.11) | collective-permute-done | bytes 262176 | tf_op jit(solution)/shard_map/ppermute | solution.py:459
  99.9 1.4 collective-permute-start.15
  101.4 3.7 %collective-permute-done.12.block_ref = f32[256,256]{1,0:T(8,128)S(1)} collective-permute-done((f32[256,256]{1,0:T(8,128)S(1)}, f32[256,256]{1,0:T(8,128)S(1)}, u32[]{:S(2)}, u32[]{:S(2)}) %collective-permute-start.12) | collective-permute-done | bytes 262176 | tf_op jit(solution)/shard_map/ppermute | solution.py:459
  105.1 1.4 collective-permute-start.16
  106.5 0.7 copy-done
  107.2 7.8 %collective-permute-done.15.block_ref = f32[256,256]{1,0:T(8,128)S(1)} collective-permute-done((f32[256,256]{1,0:T(8,128)S(1)}, f32[256,256]{1,0:T(8,128)S(1)}, u32[]{:S(2)}, u32[]{:S(2)}) %collective-permute-start.15) | collective-permute-done | bytes 262176 | tf_op jit(solution)/shard_map/ppermute | solution.py:459
  115.0 0.7 copy-done.2
  115.8 5.1 %collective-permute-done.6.edge_own_ref = f32[4,64,128]{2,1,0:T(8,128)} collective-permute-done((f32[4,64,128]{2,1,0:T(8,128)S(1)}, f32[4,64,128]{2,1,0:T(8,128)}, u32[]{:S(2)}, u32[]{:S(2)}) %collective-permute-start.6) | collective-permute-done | bytes 131104 | tf_op jit(solution)/shard_map/ppermute | solution.py:468
  120.8 2.4 %gram.1.a_ref = f32[128,128]{1,0:T(8,128)} custom-call(s32[7]{0:T(128)S(1)} %stack.31.place_ref, f32[8,272,128]{2,1,0:T(8,128)S(1)} %get-tuple-element.31.own_ref), custom_call_target="tpu_custom_call" | custom-call | flops 427819008 | bytes 1114112 | tf_op jit(solution)/shard_map/gram/pallas_call | solution.py:239
  123.3 0.7 copy-done.4
  124.0 0.5 collective-permute-start.8
  124.5 1.6 turn.8
  126.1 0.1 turn.10
  126.2 0.0 copy-start.1
  126.2 0.9 copy-done.1
  127.2 0.1 turn.11
  127.3 1.2 turn.9
  128.6 0.0 copy-start.3
  128.6 0.9 copy-done.3
  129.5 0.1 turn.14
  129.7 0.9 copy-done.5
  130.6 0.1 turn.15
  130.7 1.2 turn.13
  132.0 1.6 turn.12
  133.6 1.4 assemble.1.sketch_ref.refs_16_
  135.0 1.2 shard_map.46.gram_ref
  136.2 0.1 collective-permute-start.9
  136.3 2.0 %lagged.9 = f32[2,256,128]{2,1,0:T(8,128)S(1)} custom-call(s32[1]{0:T(128)} %bitcast.13.lag_ref, bf16[256,1024]{1,0:T(8,128)(2,1)S(1)} %get-tuple-element.33.refs_0_, bf16[256,512]{1,0:T(8,128)(2,1)S(1)} %get-tuple-element.35.refs_1_, bf16[256,256]{1,0:T(8,128)(2,1)S(1)} %get-tuple-element.37.refs_2_, bf16[256,256]{1,0:T(8,128)(2,1)S(1)} %get-tuple-element.39.refs_3_, ...), custom_call_target="tpu_custom_call" | custom-call | flops 1610612736 | bytes 6684672 | tf_op jit(solution)/shard_map/lagged/pallas_call | solution.py:329
  138.3 2.0 %lagged.8 = f32[2,256,128]{2,1,0:T(8,128)S(1)} custom-call(s32[1]{0:T(128)} %bitcast.12.lag_ref, bf16[256,1024]{1,0:T(8,128)(2,1)S(1)} %get-tuple-element.33.refs_0_, bf16[256,512]{1,0:T(8,128)(2,1)S(1)} %get-tuple-element.35.refs_1_, bf16[256,256]{1,0:T(8,128)(2,1)S(1)} %get-tuple-element.37.refs_2_, bf16[256,256]{1,0:T(8,128)(2,1)S(1)} %get-tuple-element.39.refs_3_, ...), custom_call_target="tpu_custom_call" | custom-call | flops 1610612736 | bytes 6684672 | tf_op jit(solution)/shard_map/lagged/pallas_call | solution.py:329
  140.2 2.0 %lagged.7 = f32[2,256,128]{2,1,0:T(8,128)S(1)} custom-call(s32[1]{0:T(128)} %bitcast.11.lag_ref, bf16[256,1024]{1,0:T(8,128)(2,1)S(1)} %get-tuple-element.33.refs_0_, bf16[256,512]{1,0:T(8,128)(2,1)S(1)} %get-tuple-element.35.refs_1_, bf16[256,256]{1,0:T(8,128)(2,1)S(1)} %get-tuple-element.37.refs_2_, bf16[256,256]{1,0:T(8,128)(2,1)S(1)} %get-tuple-element.39.refs_3_, ...), custom_call_target="tpu_custom_call" | custom-call | flops 1610612736 | bytes 6684672 | tf_op jit(solution)/shard_map/lagged/pallas_call | solution.py:329
  142.2 8.0 %lagged.5.kept_ref = f32[8,256,128]{2,1,0:T(8,128)S(1)} custom-call(s32[1]{0:T(128)} %bitcast.9.lag_ref, bf16[256,1024]{1,0:T(8,128)(2,1)S(1)} %get-tuple-element.33.refs_0_, bf16[256,512]{1,0:T(8,128)(2,1)S(1)} %get-tuple-element.35.refs_1_, bf16[256,256]{1,0:T(8,128)(2,1)S(1)} %get-tuple-element.37.refs_2_, ...), custom_call_target="tpu_custom_call" | custom-call | flops 6442450944 | bytes 7471104 | tf_op jit(solution)/shard_map/lagged/pallas_call | solution.py:329
  150.3 2.0 %lagged.6 = f32[2,256,128]{2,1,0:T(8,128)S(1)} custom-call(s32[1]{0:T(128)} %bitcast.10.lag_ref, bf16[256,1024]{1,0:T(8,128)(2,1)S(1)} %get-tuple-element.33.refs_0_, bf16[256,512]{1,0:T(8,128)(2,1)S(1)} %get-tuple-element.35.refs_1_, bf16[256,256]{1,0:T(8,128)(2,1)S(1)} %get-tuple-element.37.refs_2_, bf16[256,256]{1,0:T(8,128)(2,1)S(1)} %get-tuple-element.39.refs_3_, ...), custom_call_target="tpu_custom_call" | custom-call | flops 1610612736 | bytes 6684672 | tf_op jit(solution)/shard_map/lagged/pallas_call | solution.py:329
  152.3 2.0 %collective-permute-start.17 = (f32[2,256,128]{2,1,0:T(8,128)S(1)}, f32[2,256,128]{2,1,0:T(8,128)S(1)}, u32[]{:S(2)}, u32[]{:S(2)}) collective-permute-start(f32[2,256,128]{2,1,0:T(8,128)S(1)} %lagged.6), channel_id=1, source_target_pairs={{0,8},{4,12},{8,0},{12,4},{16,24},{20,28},{24,16},{28,20},{1,9},{5... | collective-permute-start | bytes 786440 | tf_op jit(solution)/shard_map/ppermute | solution.py:459
  154.3 0.1 collective-permute-start.18
  154.4 1.9 %collective-permute-start.19 = (f32[2,256,128]{2,1,0:T(8,128)S(1)}, f32[2,256,128]{2,1,0:T(8,128)S(1)}, u32[]{:S(2)}, u32[]{:S(2)}) collective-permute-start(f32[2,256,128]{2,1,0:T(8,128)S(1)} %lagged.8), channel_id=1, source_target_pairs={{0,8},{4,12},{8,0},{12,4},{16,24},{20,28},{24,16},{28,20},{1,9},{5... | collective-permute-start | bytes 786440 | tf_op jit(solution)/shard_map/ppermute | solution.py:459
  156.3 0.1 collective-permute-start.20
  156.4 3.5 %factor.1.inverse_ref = f32[128,128]{1,0:T(8,128)S(1)} custom-call(f32[128,128]{1,0:T(8,128)S(1)} %shard_map.46.gram_ref, f32[128,128]{1,0:T(8,128)S(1)} %collective-permute-done.9.other_ref), custom_call_target="tpu_custom_call" | custom-call | flops 3000000000 | bytes 131072 | tf_op jit(solution)/shard_map/factor/pallas_call | solution.py:292
  159.9 1.4 convolution_multiply_fusion
  161.3 11.5 %collective-permute-done.19.refs_0_ = f32[2,256,128]{2,1,0:T(8,128)S(1)} collective-permute-done((f32[2,256,128]{2,1,0:T(8,128)S(1)}, f32[2,256,128]{2,1,0:T(8,128)S(1)}, u32[]{:S(2)}, u32[]{:S(2)}) %collective-permute-start.19) | collective-permute-done | bytes 262176 | tf_op jit(solution)/shard_map/ppermute | solution.py:459
  172.8 4.7 %collective-permute-done.20.refs_1_ = f32[2,256,128]{2,1,0:T(8,128)S(1)} collective-permute-done((f32[2,256,128]{2,1,0:T(8,128)S(1)}, f32[2,256,128]{2,1,0:T(8,128)S(1)}, u32[]{:S(2)}, u32[]{:S(2)}) %collective-permute-start.20) | collective-permute-done | bytes 262176 | tf_op jit(solution)/shard_map/ppermute | solution.py:459
  177.4 1.3 finish.3.refs_1_
  178.7 1.0 finish.4.refs_1_
  179.7 1.0 finish.5
  (19 shorter events, 0.1 us)
Async XLA Ops:
  20.0 1.7 collective-permute-start
  21.8 6.9 %collective-permute-start.1 = (f32[1,272,128]{2,1,0:T(8,128)S(1)}, f32[1,272,128]{2,1,0:T(8,128)S(1)}, u32[]{:S(2)}, u32[]{:S(2)}) collective-permute-start(f32[1,272,128]{2,1,0:T(8,128)S(1)} %get-tuple-element.30), channel_id=1, source_target_pairs={{0,2},{1,3},{2,0},{3,1},{4,6},{5,7},{6,4},{7,5},{8,10},{9,11},{10,... | collective-permute-start | bytes 417800 | tf_op jit(solution)/shard_map/ppermute | solution.py:459
  28.7 9.1 %collective-permute-start.2 = (f32[1,272,128]{2,1,0:T(8,128)S(1)}, f32[1,272,128]{2,1,0:T(8,128)S(1)}, u32[]{:S(2)}, u32[]{:S(2)}) collective-permute-start(f32[1,272,128]{2,1,0:T(8,128)S(1)} %shard_map.42.a_ref), channel_id=1, source_target_pairs={{0,16},{1,17},{2,18},{3,19},{4,20},{5,21},{6,22},{7,23},{8,24},{9,... | collective-permute-start | bytes 417800 | tf_op jit(solution)/shard_map/ppermute | solution.py:468
  37.8 6.6 %collective-permute-start.3 = (f32[2,272,128]{2,1,0:T(8,128)S(1)}, f32[2,272,128]{2,1,0:T(8,128)S(1)}, u32[]{:S(2)}, u32[]{:S(2)}) collective-permute-start(f32[2,272,128]{2,1,0:T(8,128)S(1)} %shard_map.43.a_ref), channel_id=1, source_target_pairs={{0,2},{1,5},{2,0},{3,7},{4,6},{5,1},{6,4},{7,3},{8,10},{9,13},{10,... | collective-permute-start | bytes 835592 | tf_op jit(solution)/shard_map/ppermute | solution.py:468
  44.5 9.6 %collective-permute-start.4 = (f32[4,272,128]{2,1,0:T(8,128)S(1)}, f32[4,272,128]{2,1,0:T(8,128)S(1)}, u32[]{:S(2)}, u32[]{:S(2)}) collective-permute-start(f32[4,272,128]{2,1,0:T(8,128)S(1)} %shard_map.44.a_ref), channel_id=1, source_target_pairs={{0,4},{1,3},{2,6},{3,1},{4,0},{5,7},{6,2},{7,5},{8,12},{9,11},{10,... | collective-permute-start | bytes 1671176 | tf_op jit(solution)/shard_map/ppermute | solution.py:468
  54.7 78.9 %collective-permute-start.5 = (f32[8,272,128]{2,1,0:T(8,128)S(1)}, f32[8,272,128]{2,1,0:T(8,128)S(1)}, u32[]{:S(2)}, u32[]{:S(2)}) collective-permute-start(f32[8,272,128]{2,1,0:T(8,128)S(1)} %get-tuple-element.31.own_ref), channel_id=1, source_target_pairs={{0,1},{1,0},{2,3},{3,2},{4,5},{5,4},{6,7},{7,6},{8,9},{9,8},{10,11... | collective-permute-start | bytes 3342344 | tf_op jit(solution)/shard_map/ppermute | solution.py:459
  56.1 38.3 %collective-permute-start.10 = (f32[512,256]{1,0:T(8,128)S(1)}, f32[512,256]{1,0:T(8,128)}, u32[]{:S(2)}, u32[]{:S(2)}) collective-permute-start(f32[512,256]{1,0:T(8,128)S(1)} %get-tuple-element.34), channel_id=1, source_target_pairs={{0,16},{4,20},{8,24},{12,28},{16,0},{20,4},{24,8},{28,12},{1,17},{... | collective-permute-start | bytes 1572872 | tf_op jit(solution)/shard_map/ppermute | solution.py:459
  56.2 75.8 %collective-permute-start.13 = (f32[1024,256]{1,0:T(8,128)}, f32[1024,256]{1,0:T(8,128)}, u32[]{:S(2)}, u32[]{:S(2)}) collective-permute-start(f32[1024,256]{1,0:T(8,128)} %record_ref.3), channel_id=1, source_target_pairs={{0,4},{4,0},{8,12},{12,8},{16,20},{20,16},{24,28},{28,24},{1,5},{5... | collective-permute-start | bytes 3145736 | tf_op jit(solution)/shard_map/ppermute | solution.py:459
  57.7 42.3 %collective-permute-start.11 = (f32[256,256]{1,0:T(8,128)S(1)}, f32[256,256]{1,0:T(8,128)S(1)}, u32[]{:S(2)}, u32[]{:S(2)}) collective-permute-start(f32[256,256]{1,0:T(8,128)S(1)} %get-tuple-element.36), channel_id=1, source_target_pairs={{0,16},{4,20},{8,24},{12,28},{16,0},{20,4},{24,8},{28,12},{1,17},{... | collective-permute-start | bytes 786440 | tf_op jit(solution)/shard_map/ppermute | solution.py:459
  60.5 44.6 %collective-permute-start.12 = (f32[256,256]{1,0:T(8,128)S(1)}, f32[256,256]{1,0:T(8,128)S(1)}, u32[]{:S(2)}, u32[]{:S(2)}) collective-permute-start(f32[256,256]{1,0:T(8,128)S(1)} %get-tuple-element.38), channel_id=1, source_target_pairs={{0,16},{4,20},{8,24},{12,28},{16,0},{20,4},{24,8},{28,12},{1,17},{... | collective-permute-start | bytes 786440 | tf_op jit(solution)/shard_map/ppermute | solution.py:459
  94.4 36.3 %collective-permute-start.14 = (f32[512,256]{1,0:T(8,128)}, f32[512,256]{1,0:T(8,128)}, u32[]{:S(2)}, u32[]{:S(2)}) collective-permute-start(f32[512,256]{1,0:T(8,128)} %collective-permute-done.10.block_ref), channel_id=1, source_target_pairs={{0,4},{4,0},{8,12},{12,8},{16,20},{20,16},{24,28},{28,24},{1,5},{5... | collective-permute-start | bytes 1572872 | tf_op jit(solution)/shard_map/ppermute | solution.py:459
  99.9 15.1 %collective-permute-start.15 = (f32[256,256]{1,0:T(8,128)S(1)}, f32[256,256]{1,0:T(8,128)S(1)}, u32[]{:S(2)}, u32[]{:S(2)}) collective-permute-start(f32[256,256]{1,0:T(8,128)S(1)} %collective-permute-done.11.block_ref), channel_id=1, source_target_pairs={{0,4},{4,0},{8,12},{12,8},{16,20},{20,16},{24,28},{28,24},{1,5},{5... | collective-permute-start | bytes 786440 | tf_op jit(solution)/shard_map/ppermute | solution.py:459
  105.1 18.2 %collective-permute-start.16 = (f32[256,256]{1,0:T(8,128)S(1)}, f32[256,256]{1,0:T(8,128)S(1)}, u32[]{:S(2)}, u32[]{:S(2)}) collective-permute-start(f32[256,256]{1,0:T(8,128)S(1)} %collective-permute-done.12.block_ref), channel_id=1, source_target_pairs={{0,4},{4,0},{8,12},{12,8},{16,20},{20,16},{24,28},{28,24},{1,5},{5... | collective-permute-start | bytes 786440 | tf_op jit(solution)/shard_map/ppermute | solution.py:459
  106.5 0.7 copy-start
  115.0 0.7 copy-start.2
  115.8 5.1 %collective-permute-start.6 = (f32[4,64,128]{2,1,0:T(8,128)S(1)}, f32[4,64,128]{2,1,0:T(8,128)}, u32[]{:S(2)}, u32[]{:S(2)}) collective-permute-start(f32[4,64,128]{2,1,0:T(8,128)S(1)} %get-tuple-element.32), channel_id=1, source_target_pairs={{0,8},{1,9},{2,10},{3,11},{4,12},{5,13},{6,14},{7,15},{8,0},{9,1},... | collective-permute-start | bytes 393224 | tf_op jit(solution)/shard_map/ppermute | solution.py:468
  120.8 12.8 %collective-permute-start.7 = (f32[4,64,128]{2,1,0:T(8,128)}, f32[4,64,128]{2,1,0:T(8,128)}, u32[]{:S(2)}, u32[]{:S(2)}) collective-permute-start(f32[4,64,128]{2,1,0:T(8,128)} %collective-permute-done.6.edge_own_ref), channel_id=1, source_target_pairs={{0,1},{1,0},{2,3},{3,2},{4,5},{5,4},{6,7},{7,6},{8,9},{9,8},{10,11... | collective-permute-start | bytes 393224 | tf_op jit(solution)/shard_map/ppermute | solution.py:459
  123.3 0.7 copy-start.4
  124.0 11.0 %collective-permute-start.8 = (f32[128,128]{1,0:T(8,128)}, f32[128,128]{1,0:T(8,128)}, u32[]{:S(2)}, u32[]{:S(2)}) collective-permute-start(f32[128,128]{1,0:T(8,128)} %gram.1.a_ref), channel_id=1, source_target_pairs={{0,1},{1,0},{2,3},{3,2},{4,5},{5,4},{6,7},{7,6},{8,9},{9,8},{10,11... | collective-permute-start | bytes 196616 | tf_op jit(solution)/shard_map/ppermute | solution.py:459
  126.2 1.0 copy-start.1
  128.6 1.0 copy-start.3
  129.6 1.0 copy-start.5
  136.2 20.2 %collective-permute-start.9 = (f32[128,128]{1,0:T(8,128)S(1)}, f32[128,128]{1,0:T(8,128)S(1)}, u32[]{:S(2)}, u32[]{:S(2)}) collective-permute-start(f32[128,128]{1,0:T(8,128)S(1)} %shard_map.46.gram_ref), channel_id=1, source_target_pairs={{0,8},{4,12},{8,0},{12,4},{16,24},{20,28},{24,16},{28,20},{1,9},{5... | collective-permute-start | bytes 196616 | tf_op jit(solution)/shard_map/ppermute | solution.py:459
  152.3 27.5 %collective-permute-start.17 = (f32[2,256,128]{2,1,0:T(8,128)S(1)}, f32[2,256,128]{2,1,0:T(8,128)S(1)}, u32[]{:S(2)}, u32[]{:S(2)}) collective-permute-start(f32[2,256,128]{2,1,0:T(8,128)S(1)} %lagged.6), channel_id=1, source_target_pairs={{0,8},{4,12},{8,0},{12,4},{16,24},{20,28},{24,16},{28,20},{1,9},{5... | collective-permute-start | bytes 786440 | tf_op jit(solution)/shard_map/ppermute | solution.py:459
  154.3 24.4 %collective-permute-start.18 = (f32[2,256,128]{2,1,0:T(8,128)S(1)}, f32[2,256,128]{2,1,0:T(8,128)S(1)}, u32[]{:S(2)}, u32[]{:S(2)}) collective-permute-start(f32[2,256,128]{2,1,0:T(8,128)S(1)} %lagged.7), channel_id=1, source_target_pairs={{0,8},{4,12},{8,0},{12,4},{16,24},{20,28},{24,16},{28,20},{1,9},{5... | collective-permute-start | bytes 786440 | tf_op jit(solution)/shard_map/ppermute | solution.py:459
  154.4 18.4 %collective-permute-start.19 = (f32[2,256,128]{2,1,0:T(8,128)S(1)}, f32[2,256,128]{2,1,0:T(8,128)S(1)}, u32[]{:S(2)}, u32[]{:S(2)}) collective-permute-start(f32[2,256,128]{2,1,0:T(8,128)S(1)} %lagged.8), channel_id=1, source_target_pairs={{0,8},{4,12},{8,0},{12,4},{16,24},{20,28},{24,16},{28,20},{1,9},{5... | collective-permute-start | bytes 786440 | tf_op jit(solution)/shard_map/ppermute | solution.py:459
  156.3 21.1 %collective-permute-start.20 = (f32[2,256,128]{2,1,0:T(8,128)S(1)}, f32[2,256,128]{2,1,0:T(8,128)S(1)}, u32[]{:S(2)}, u32[]{:S(2)}) collective-permute-start(f32[2,256,128]{2,1,0:T(8,128)S(1)} %lagged.9), channel_id=1, source_target_pairs={{0,8},{4,12},{8,0},{12,4},{16,24},{20,28},{24,16},{28,20},{1,9},{5... | collective-permute-start | bytes 786440 | tf_op jit(solution)/shard_map/ppermute | solution.py:459

commit v5 on v4

--- a/solution.py
+++ b/solution.py
@@ -121,21 +121,24 @@
     )
 
 
-def turn_kernel(block_ref, high_ref, low_ref):
-    high_ref[...], low_ref[...] = split(block_ref[...].T)
-
-
-def turn(block):
-    rows, chans = block.shape
-    return pl.pallas_call(
+def turn_kernel(*refs):
+    count = len(refs) // 3
+    for n in range(count):
+        refs[count + 2 * n][...], refs[count + 2 * n + 1][...] = split(refs[n][...].T)
+
+
+def turn(blocks):
+    size = sum(b.size for b in blocks)
+    outs = pl.pallas_call(
         turn_kernel,
-        in_specs=[VMEM],
-        out_specs=[VMEM] * 2,
-        out_shape=[jax.ShapeDtypeStruct((chans, rows), BF16)] * 2,
+        in_specs=[VMEM] * len(blocks),
+        out_specs=[VMEM] * (2 * len(blocks)),
+        out_shape=[jax.ShapeDtypeStruct(b.shape[::-1], BF16) for b in blocks for _ in range(2)],
         compiler_params=pltpu.CompilerParams(vmem_limit_bytes=12 * 2**20),
-        cost_estimate=cost(0, 8 * rows * chans),
+        cost_estimate=cost(0, 8 * size),
         name="turn",
-    )(block)
+    )(*blocks)
+    return list(zip(outs[::2], outs[1::2]))
 
 
 def even_piece(block, pair):
@@ -341,25 +344,31 @@
     )(lag.reshape(1), *[h for h, _ in turned], *[l for _, l in turned], sketches)
 
 
-def finish_kernel(chunks, inverse_ref, kept_ref, *refs):
-    received, out_ref = refs[:chunks], refs[-1]
-    size, chans, width = received[0].shape
+def finish_kernel(inverse_ref, kept_ref, *refs):
+    out_ref = refs[-1]
+    size, chans, width = out_ref.shape
     inverse_high, inverse_low = split(inverse_ref[...].T)
-    for n, ref in enumerate(received):
-        part = slice(n * size, (n + 1) * size)
-        high, low = split((kept_ref[part] + ref[...]).reshape(size * chans, width))
-        out_ref[part] = three(high, low, inverse_high, inverse_low).reshape(size, chans, width)
+
+    def put(received_ref):
+        high, low = split((kept_ref[...] + received_ref[...]).reshape(size * chans, width))
+        out_ref[...] = three(high, low, inverse_high, inverse_low).reshape(size, chans, width)
+
+    for n in range(pl.num_programs(0)):
+
+        @pl.when(pl.program_id(0) == n)
+        def _():
+            put(refs[n])
 
 
 def finish(inverse, kept, received, first, out=None):
     _, chans, width = kept.shape
     size = received[0].shape[0]
     count = len(received)
-    block = pl.BlockSpec((count * size, chans, width), lambda i: (first // count, 0, 0))
+    block = pl.BlockSpec((size, chans, width), lambda i: (first + i, 0, 0))
     extra = [] if out is None else [out]
     return pl.pallas_call(
-        functools.partial(finish_kernel, count),
-        grid=(1,),
+        finish_kernel,
+        grid=(count,),
         in_specs=[VMEM, block] + [VMEM] * count + [pl.BlockSpec(memory_space=pl.ANY)] * len(extra),
         out_specs=block,
         out_shape=jax.ShapeDtypeStruct(kept.shape, F32),
@@ -384,11 +393,31 @@
     return outs[0] if len(outs) == 1 else outs
 
 
-def cut_kernel(record_ref, *parts):
-    first = 0
-    for ref in parts:
-        ref[...] = record_ref[first : first + ref.shape[0]]
+def cut_kernel(record_ref, *refs):
+    *parts, arrived = refs
+    copies, first = [], 0
+    for n, ref in enumerate(parts):
+        rows = pl.ds(first, ref.shape[0])
+        copies.append(pltpu.make_async_copy(record_ref.at[rows], ref, arrived.at[n]))
         first += ref.shape[0]
+    for copy in copies:
+        copy.start()
+    for copy in copies:
+        copy.wait()
+
+
+def cut_up(record, sizes):
+    chans = record.shape[1]
+    return pl.pallas_call(
+        cut_kernel,
+        in_specs=[pl.BlockSpec(memory_space=pltpu.HBM)],
+        out_specs=[VMEM] * len(sizes),
+        out_shape=[jax.ShapeDtypeStruct((n, chans), F32) for n in sizes],
+        scratch_shapes=[pltpu.SemaphoreType.DMA((len(sizes),))],
+        compiler_params=pltpu.CompilerParams(vmem_limit_bytes=4 * 2**20),
+        cost_estimate=cost(0, 8 * record.size),
+        name="cut",
+    )(record)
 
 
 def add_pair_kernel(keep_ref, got_ref, own_ref, pass_ref):
@@ -396,21 +425,20 @@
     pass_ref[0] = keep_ref[1] + got_ref[1]
 
 
-def join_edges_kernel(place_ref, a_ref, b_ref, out_ref, edge_ref):
-    join_kernel(a_ref, b_ref, out_ref)
+def edges_kernel(place_ref, own_ref, edge_ref):
     blocks, rim, _ = edge_ref.shape
-    share = a_ref.shape[1]
+    share = own_ref.shape[1]
     for high in range(2):
 
         @pl.when((place_ref[2] == 0) & (place_ref[3] == high))
         def _():
             for b in range(blocks):
-                edge_ref[b] = out_ref[even_piece(b, high), :rim]
+                edge_ref[b] = own_ref[even_piece(b, high), :rim]
 
         @pl.when((place_ref[2] == 1) & (place_ref[3] == high))
         def _():
             for b in range(blocks):
-                edge_ref[b] = out_ref[blocks * (1 - high) + b, share - rim :]
+                edge_ref[b] = own_ref[blocks * (1 - high) + b, share - rim :]
 
 
 def edge_gram_kernel(rim, sketch_ref, a_ref, b_ref, out_ref):
@@ -421,6 +449,12 @@
     )
 
 
+def basis_kernel(root, inverse_ref, sketch_ref, out_ref):
+    rim = sketch_ref.shape[1] - out_ref.shape[0]
+    value = three(*split(sketch_ref[0, rim:]), *split(inverse_ref[...].T))
+    out_ref[...] = value * root
+
+
 def join_kernel(a_ref, b_ref, out_ref):
     out_ref[: a_ref.shape[0]] = a_ref[...]
     out_ref[a_ref.shape[0] :] = b_ref[...]
@@ -439,7 +473,7 @@
 
 
 def on_device(record, test_matrix):
-    rows, chans = record.shape
+    rows, _ = record.shape
     lags, _, width = test_matrix.shape
     n_time = lax.axis_size("tm")
     n_chan = lax.axis_size("chan")
@@ -477,7 +511,7 @@
         return (t + half) % n_time
 
     cut = [0, rows // 2, 3 * rows // 4, rows]
-    parts = small(cut_kernel, [(b - a, chans) for a, b in zip(cut, cut[1:])], record)
+    parts = cut_up(record, [b - a for a, b in zip(cut, cut[1:])])
     beside_record = to(record, beside)
     across_parts = [to(part, across) for part in parts]
     both_parts = [to(part, beside) for part in across_parts]
@@ -492,9 +526,8 @@
     got = to_both(own, lambda t, c: (t, c ^ 2) if even(c) else (beside(t), c))
     own = joined(own, got)
     got = to_both(own, lambda t, c: (beside(t), c) if even(c) else (t, c ^ 2))
-    own, edge = small(
-        join_edges_kernel, [(2 * own.shape[0], share, width), (own.shape[0], rim, width)], place, own, got, smem=1
-    )
+    own = joined(own, got)
+    edge = small(edges_kernel, [(own.shape[0] // 2, rim, width)], place, own, smem=1)
     got = to(own, lambda i: i ^ 1, "chan")
 
     def neighbour(t, step):
@@ -515,10 +548,9 @@
         other = to(gram, lambda i: i ^ distance)
         distance *= 2
 
-    turned = [turn(record)]
-    turned += [turn(p) for p in across_parts]
-    turned += [turn(beside_record)]
-    turned += [turn(p) for p in both_parts]
+    early = turn([record, beside_record, *across_parts[:2], both_parts[0]])
+    late = turn([across_parts[2], *both_parts[1:]])
+    turned = [early[0], early[2], early[3], late[0], early[1], early[4], late[1], late[2]]
     places = [(0, 0, rim)] + [(1, a, rim) for a in cut[:-1]] + [(2, 0, rim)] + [(3, a, rim) for a in cut[:-1]]
 
     middle = (here % half) // 2
@@ -540,12 +572,12 @@
     kept = lagged(owner_lag(0), turned, places, sketches, per)
     inverse = factor(gram, other)
 
-    def whitened(x):
-        return lax.dot_general(
-            x, inverse, (((x.ndim - 1,), (1,)), ((), ())), precision=HIGHEST, preferred_element_type=F32
-        )
-
-    basis = whitened(sketches[0, rim:]) * jnp.sqrt(F32(rows * n_time))
+    basis = small(
+        functools.partial(basis_kernel, float(rows * n_time) ** 0.5),
+        [(rows, width)],
+        inverse,
+        sketches,
+    )
     totals = []
     for n in range(chunks):
         total = received[n]
@@ -553,7 +585,7 @@
             total = added(total, more)
         totals.append(total)
     coeffs = None
-    for first, count in ((0, chunks // 2), (chunks // 2, chunks // 4), (3 * chunks // 4, chunks - 3 * chunks // 4)):
+    for first, count in ((0, chunks - 1), (chunks - 1, 1)):
         if count:
             coeffs = finish(inverse, kept, totals[first : first + count], first, coeffs)
     return basis, coeffs

time: 181 us -> 177 us (0.978)
  Pallas kernels: 55.2 us -> 52.8 us
    pallas_call x11 -> x5, Pallas kernels: 9.54 us -> 7.18 us  [the longest x2 3.17 us: finish(): pl.pallas_call(finish_kernel, grid=(count,), in_specs=[VMEM, block] + [VM...]
  transfers between devices with their start and end apart: 21 -> 21, of which waited for: 12 -> 13; matrix products, arithmetic and copies ran while one was open for 1% -> 0% of each run, Pallas kernels for 18% -> 18%
where the time goes in v5:
time: 177 us
  waiting for transfers between devices  95.4 us (54%)
  Pallas kernels  52.8 us (30%)
  starting transfers between devices  23.1 us (13%)
  local copies, waits for them, and re-layouts  4.34 us (2%)
    ppermute x17, waiting for transfers between devices, to(): return lax.ppermute(block, axis, route)  71 us
    ppermute x4, waiting for transfers between devices, to_both(): return lax.ppermute(block, ('tm', 'chan'), route)  24.5 us
    pallas_call x1, Pallas kernels, sketch(): pl.pallas_call(sketch_kernel, grid=(STEP // 2,), in_specs=[SMEM, VMEM, pl...  19.2 us
    ppermute x17, starting transfers between devices, to(): return lax.ppermute(block, axis, route)  17.2 us
    pallas_call x5, Pallas kernels, lagged(): pl.pallas_call(functools.partial(lagged_kernel, places), grid=(lags // 2,...  16 us
    ppermute x4, starting transfers between devices, to_both(): return lax.ppermute(block, ('tm', 'chan'), route)  5.91 us
    unnamed x12, local copies, waits for them, and re-layouts  4.25 us
  transfers between devices with their start and end apart: 21, of which 13 were waited for; matrix products, arithmetic and copies ran while one was open for 0% of the time, Pallas kernels for 18%

profile of v5, /device:TPU:0, one launch (start us, length us, event | category | flops | bytes accessed | tf_op | source)
XLA Modules:
  0.0 176.5 jit_solution(15138093695821959061)
XLA Ops:
  0.7 0.1 stack.31.place_ref
  0.8 19.2 %sketch.1 = (f32[2,272,128]{2,1,0:T(8,128)S(1)}, f32[2,272,128]{2,1,0:T(8,128)S(1)}) custom-call(s32[7]{0:T(128)S(1)} %stack.31.place_ref, f32[1024,256]{1,0:T(8,128)} %refs_0_.1, f32[4,16,256,128]{3,2,1,0:T(8,128)} %bitcast.13), custom_call_target="tpu_custom_call" | custom-call | flops 13690208256 | bytes 10125312 | tf_op jit(solution)/shard_map/sketch/pallas_call | solution.py:94
  20.0 0.6 collective-permute-start
  20.5 1.2 collective-permute-done.got_ref
  21.8 2.9 %collective-permute-start.1 = (f32[1,272,128]{2,1,0:T(8,128)S(1)}, f32[1,272,128]{2,1,0:T(8,128)S(1)}, u32[]{:S(2)}, u32[]{:S(2)}) collective-permute-start(f32[1,272,128]{2,1,0:T(8,128)S(1)} %get-tuple-element.28), channel_id=1, source_target_pairs={{0,2},{1,3},{2,0},{3,1},{4,6},{5,7},{6,4},{7,5},{8,10},{9,11},{10,... | collective-permute-start | bytes 417800 | tf_op jit(solution)/shard_map/ppermute | solution.py:493
  24.7 4.0 %collective-permute-done.1.b_ref = f32[1,272,128]{2,1,0:T(8,128)S(1)} collective-permute-done((f32[1,272,128]{2,1,0:T(8,128)S(1)}, f32[1,272,128]{2,1,0:T(8,128)S(1)}, u32[]{:S(2)}, u32[]{:S(2)}) %collective-permute-start.1) | collective-permute-done | bytes 139296 | tf_op jit(solution)/shard_map/ppermute | solution.py:493
  28.7 2.9 %collective-permute-start.2 = (f32[1,272,128]{2,1,0:T(8,128)S(1)}, f32[1,272,128]{2,1,0:T(8,128)S(1)}, u32[]{:S(2)}, u32[]{:S(2)}) collective-permute-start(f32[1,272,128]{2,1,0:T(8,128)S(1)} %shard_map.42.a_ref), channel_id=1, source_target_pairs={{0,16},{1,17},{2,18},{3,19},{4,20},{5,21},{6,22},{7,23},{8,24},{9,... | collective-permute-start | bytes 417800 | tf_op jit(solution)/shard_map/ppermute | solution.py:502
  31.6 6.2 %collective-permute-done.2.b_ref = f32[1,272,128]{2,1,0:T(8,128)S(1)} collective-permute-done((f32[1,272,128]{2,1,0:T(8,128)S(1)}, f32[1,272,128]{2,1,0:T(8,128)S(1)}, u32[]{:S(2)}, u32[]{:S(2)}) %collective-permute-start.2) | collective-permute-done | bytes 139296 | tf_op jit(solution)/shard_map/ppermute | solution.py:502
  37.8 1.5 collective-permute-start.3
  39.3 5.1 %collective-permute-done.3.b_ref = f32[2,272,128]{2,1,0:T(8,128)S(1)} collective-permute-done((f32[2,272,128]{2,1,0:T(8,128)S(1)}, f32[2,272,128]{2,1,0:T(8,128)S(1)}, u32[]{:S(2)}, u32[]{:S(2)}) %collective-permute-start.3) | collective-permute-done | bytes 278560 | tf_op jit(solution)/shard_map/ppermute | solution.py:502
  44.5 1.5 collective-permute-start.4
  46.0 8.1 %collective-permute-done.4.b_ref = f32[4,272,128]{2,1,0:T(8,128)S(1)} collective-permute-done((f32[4,272,128]{2,1,0:T(8,128)S(1)}, f32[4,272,128]{2,1,0:T(8,128)S(1)}, u32[]{:S(2)}, u32[]{:S(2)}) %collective-permute-start.4) | collective-permute-done | bytes 557088 | tf_op jit(solution)/shard_map/ppermute | solution.py:502
  54.1 0.1 shard_map.45.own_ref
  54.1 0.1 collective-permute-start.5
  54.2 1.2 cut.1
  55.4 0.1 collective-permute-start.11
  55.5 1.5 collective-permute-start.10
  57.0 2.8 %collective-permute-start.12 = (f32[256,256]{1,0:T(8,128)S(1)}, f32[256,256]{1,0:T(8,128)S(1)}, u32[]{:S(2)}, u32[]{:S(2)}) collective-permute-start(f32[256,256]{1,0:T(8,128)S(1)} %get-tuple-element.30), channel_id=1, source_target_pairs={{0,16},{4,20},{8,24},{12,28},{16,0},{20,4},{24,8},{28,12},{1,17},{... | collective-permute-start | bytes 786440 | tf_op jit(solution)/shard_map/ppermute | solution.py:493
  59.9 0.1 collective-permute-start.14
  59.9 33.8 %collective-permute-done.11.refs_2_ = f32[512,256]{1,0:T(8,128)} collective-permute-done((f32[512,256]{1,0:T(8,128)S(1)}, f32[512,256]{1,0:T(8,128)}, u32[]{:S(2)}, u32[]{:S(2)}) %collective-permute-start.11) | collective-permute-done | bytes 524320 | tf_op jit(solution)/shard_map/ppermute | solution.py:493
  93.8 1.4 collective-permute-start.13
  95.2 4.1 %collective-permute-done.12.refs_3_ = f32[256,256]{1,0:T(8,128)S(1)} collective-permute-done((f32[256,256]{1,0:T(8,128)S(1)}, f32[256,256]{1,0:T(8,128)S(1)}, u32[]{:S(2)}, u32[]{:S(2)}) %collective-permute-start.12) | collective-permute-done | bytes 262176 | tf_op jit(solution)/shard_map/ppermute | solution.py:493
  99.3 1.4 collective-permute-start.15
  100.7 3.7 %collective-permute-done.14.refs_0_ = f32[256,256]{1,0:T(8,128)S(1)} collective-permute-done((f32[256,256]{1,0:T(8,128)S(1)}, f32[256,256]{1,0:T(8,128)S(1)}, u32[]{:S(2)}, u32[]{:S(2)}) %collective-permute-start.14) | collective-permute-done | bytes 262176 | tf_op jit(solution)/shard_map/ppermute | solution.py:493
  104.4 1.4 collective-permute-start.16
  105.9 0.6 shard_map.46
  106.5 7.9 %collective-permute-done.15.refs_1_ = f32[256,256]{1,0:T(8,128)S(1)} collective-permute-done((f32[256,256]{1,0:T(8,128)S(1)}, f32[256,256]{1,0:T(8,128)S(1)}, u32[]{:S(2)}, u32[]{:S(2)}) %collective-permute-start.15) | collective-permute-done | bytes 262176 | tf_op jit(solution)/shard_map/ppermute | solution.py:493
  114.4 0.7 copy-done
  115.1 0.0 collective-permute-start.6
  115.1 5.1 %collective-permute-done.6.edge_own_ref = f32[4,64,128]{2,1,0:T(8,128)} collective-permute-done((f32[4,64,128]{2,1,0:T(8,128)S(1)}, f32[4,64,128]{2,1,0:T(8,128)}, u32[]{:S(2)}, u32[]{:S(2)}) %collective-permute-start.6) | collective-permute-done | bytes 131104 | tf_op jit(solution)/shard_map/ppermute | solution.py:502
  120.2 2.4 %gram.1.a_ref = f32[128,128]{1,0:T(8,128)} custom-call(s32[7]{0:T(128)S(1)} %stack.31.place_ref, f32[8,272,128]{2,1,0:T(8,128)S(1)} %shard_map.45.own_ref), custom_call_target="tpu_custom_call" | custom-call | flops 427819008 | bytes 1114112 | tf_op jit(solution)/shard_map/gram/pallas_call | solution.py:242
  122.6 0.0 collective-permute-done.16.refs_2_
  122.6 0.7 copy-done.2
  123.3 0.5 collective-permute-start.8
  123.8 0.9 copy-done.1
  124.8 0.9 copy-done.3
  125.7 0.3 turn.3
  126.0 0.0 collective-permute-done.13.refs_4_
  126.0 0.0 collective-permute-done.10.refs_1_
  126.0 0.0 copy-start.5
  126.0 0.9 copy-done.5
  127.0 2.5 %turn.2 = (bf16[256,1024]{1,0:T(8,128)(2,1)S(1)}, bf16[256,1024]{1,0:T(8,128)(2,1)S(1)}, bf16[256,1024]{1,0:T(8,128)(2,1)S(1)}, bf16[256,1024]{1,0:T(8,128)(2,1)...) custom-call(f32[1024,256]{1,0:T(8,128)} %refs_0_.1, ...), custom_call_target="tpu_custom_call" | custom-call | bytes 6815744 | tf_op jit(solution)/shard_map/turn/pallas_call | solution.py:132
  129.5 0.0 collective-permute-done.5.got_ref
  129.5 1.4 assemble.1.sketch_ref.refs_16_
  130.9 0.0 collective-permute-done.8.b_ref
  130.9 1.2 shard_map.47.gram_ref
  132.1 0.1 collective-permute-start.9
  132.2 2.0 %lagged.9 = f32[2,256,128]{2,1,0:T(8,128)S(1)} custom-call(s32[1]{0:T(128)} %bitcast.12.lag_ref, bf16[256,1024]{1,0:T(8,128)(2,1)S(1)} %get-tuple-element.31.refs_0_, bf16[256,512]{1,0:T(8,128)(2,1)S(1)} %get-tuple-element.32.refs_1_, bf16[256,256]{1,0:T(8,128)(2,1)S(1)} %get-tuple-element.33.refs_2_, bf16[256,256]{1,0:T(8,128)(2,1)S(1)} %get-tuple-element.35.refs_3_, ...), custom_call_target="tpu_custom_call" | custom-call | flops 1610612736 | bytes 6684672 | tf_op jit(solution)/shard_map/lagged/pallas_call | solution.py:332
  134.2 2.0 %lagged.8 = f32[2,256,128]{2,1,0:T(8,128)S(1)} custom-call(s32[1]{0:T(128)} %bitcast.11.lag_ref, bf16[256,1024]{1,0:T(8,128)(2,1)S(1)} %get-tuple-element.31.refs_0_, bf16[256,512]{1,0:T(8,128)(2,1)S(1)} %get-tuple-element.32.refs_1_, bf16[256,256]{1,0:T(8,128)(2,1)S(1)} %get-tuple-element.33.refs_2_, bf16[256,256]{1,0:T(8,128)(2,1)S(1)} %get-tuple-element.35.refs_3_, ...), custom_call_target="tpu_custom_call" | custom-call | flops 1610612736 | bytes 6684672 | tf_op jit(solution)/shard_map/lagged/pallas_call | solution.py:332
  136.2 2.0 %lagged.7 = f32[2,256,128]{2,1,0:T(8,128)S(1)} custom-call(s32[1]{0:T(128)} %bitcast.10.lag_ref, bf16[256,1024]{1,0:T(8,128)(2,1)S(1)} %get-tuple-element.31.refs_0_, bf16[256,512]{1,0:T(8,128)(2,1)S(1)} %get-tuple-element.32.refs_1_, bf16[256,256]{1,0:T(8,128)(2,1)S(1)} %get-tuple-element.33.refs_2_, bf16[256,256]{1,0:T(8,128)(2,1)S(1)} %get-tuple-element.35.refs_3_, ...), custom_call_target="tpu_custom_call" | custom-call | flops 1610612736 | bytes 6684672 | tf_op jit(solution)/shard_map/lagged/pallas_call | solution.py:332
  138.1 8.0 %lagged.5.kept_ref = f32[8,256,128]{2,1,0:T(8,128)S(1)} custom-call(s32[1]{0:T(128)} %bitcast.8.lag_ref, bf16[256,1024]{1,0:T(8,128)(2,1)S(1)} %get-tuple-element.31.refs_0_, bf16[256,512]{1,0:T(8,128)(2,1)S(1)} %get-tuple-element.32.refs_1_, bf16[256,256]{1,0:T(8,128)(2,1)S(1)} %get-tuple-element.33.refs_2_, ...), custom_call_target="tpu_custom_call" | custom-call | flops 6442450944 | bytes 7471104 | tf_op jit(solution)/shard_map/lagged/pallas_call | solution.py:332
  146.2 2.0 %lagged.6 = f32[2,256,128]{2,1,0:T(8,128)S(1)} custom-call(s32[1]{0:T(128)} %bitcast.9.lag_ref, bf16[256,1024]{1,0:T(8,128)(2,1)S(1)} %get-tuple-element.31.refs_0_, bf16[256,512]{1,0:T(8,128)(2,1)S(1)} %get-tuple-element.32.refs_1_, bf16[256,256]{1,0:T(8,128)(2,1)S(1)} %get-tuple-element.33.refs_2_, bf16[256,256]{1,0:T(8,128)(2,1)S(1)} %get-tuple-element.35.refs_3_, ...), custom_call_target="tpu_custom_call" | custom-call | flops 1610612736 | bytes 6684672 | tf_op jit(solution)/shard_map/lagged/pallas_call | solution.py:332
  148.2 2.1 %collective-permute-start.17 = (f32[2,256,128]{2,1,0:T(8,128)S(1)}, f32[2,256,128]{2,1,0:T(8,128)S(1)}, u32[]{:S(2)}, u32[]{:S(2)}) collective-permute-start(f32[2,256,128]{2,1,0:T(8,128)S(1)} %lagged.6), channel_id=1, source_target_pairs={{0,8},{4,12},{8,0},{12,4},{16,24},{20,28},{24,16},{28,20},{1,9},{5... | collective-permute-start | bytes 786440 | tf_op jit(solution)/shard_map/ppermute | solution.py:493
  150.3 0.1 collective-permute-start.18
  150.3 1.9 %collective-permute-start.19 = (f32[2,256,128]{2,1,0:T(8,128)S(1)}, f32[2,256,128]{2,1,0:T(8,128)S(1)}, u32[]{:S(2)}, u32[]{:S(2)}) collective-permute-start(f32[2,256,128]{2,1,0:T(8,128)S(1)} %lagged.8), channel_id=1, source_target_pairs={{0,8},{4,12},{8,0},{12,4},{16,24},{20,28},{24,16},{28,20},{1,9},{5... | collective-permute-start | bytes 786440 | tf_op jit(solution)/shard_map/ppermute | solution.py:493
  152.3 0.1 collective-permute-start.20
  152.4 0.0 collective-permute-done.9.other_ref
  152.4 3.5 %factor.1.inverse_ref = f32[128,128]{1,0:T(8,128)S(1)} custom-call(f32[128,128]{1,0:T(8,128)S(1)} %shard_map.47.gram_ref, f32[128,128]{1,0:T(8,128)S(1)} %collective-permute-done.9.other_ref), custom_call_target="tpu_custom_call" | custom-call | flops 3000000000 | bytes 131072 | tf_op jit(solution)/shard_map/factor/pallas_call | solution.py:295
  155.9 1.2 shard_map.48
  157.1 5.9 %collective-permute-done.18.refs_0_ = f32[2,256,128]{2,1,0:T(8,128)S(1)} collective-permute-done((f32[2,256,128]{2,1,0:T(8,128)S(1)}, f32[2,256,128]{2,1,0:T(8,128)S(1)}, u32[]{:S(2)}, u32[]{:S(2)}) %collective-permute-start.18) | collective-permute-done | bytes 262176 | tf_op jit(solution)/shard_map/ppermute | solution.py:493
  163.0 5.6 %collective-permute-done.19.refs_1_ = f32[2,256,128]{2,1,0:T(8,128)S(1)} collective-permute-done((f32[2,256,128]{2,1,0:T(8,128)S(1)}, f32[2,256,128]{2,1,0:T(8,128)S(1)}, u32[]{:S(2)}, u32[]{:S(2)}) %collective-permute-start.19) | collective-permute-done | bytes 262176 | tf_op jit(solution)/shard_map/ppermute | solution.py:493
  168.7 4.7 %collective-permute-done.20.refs_2_ = f32[2,256,128]{2,1,0:T(8,128)S(1)} collective-permute-done((f32[2,256,128]{2,1,0:T(8,128)S(1)}, f32[2,256,128]{2,1,0:T(8,128)S(1)}, u32[]{:S(2)}, u32[]{:S(2)}) %collective-permute-start.20) | collective-permute-done | bytes 262176 | tf_op jit(solution)/shard_map/ppermute | solution.py:493
  173.3 2.1 %finish.2.refs_1_ = f32[8,256,128]{2,1,0:T(8,128)} custom-call(f32[128,128]{1,0:T(8,128)S(1)} %factor.1.inverse_ref, f32[8,256,128]{2,1,0:T(8,128)S(1)} %lagged.5.kept_ref, f32[2,256,128]{2,1,0:T(8,128)S(1)} %collective-permute-done.18.refs_0_, f32[2,256,128]{2,1,0:T(8,128)S(1)} %collective-permute-done.19.refs_1_, ...), custom_call_target="tpu_custom_call" | custom-call | flops 150994944 | bytes 2359296 | tf_op jit(solution)/shard_map/finish/pallas_call | solution.py:369
  175.5 1.0 finish.3
  (13 shorter events, 0.1 us)
Async XLA Ops:
  20.0 1.7 collective-permute-start
  21.8 6.9 %collective-permute-start.1 = (f32[1,272,128]{2,1,0:T(8,128)S(1)}, f32[1,272,128]{2,1,0:T(8,128)S(1)}, u32[]{:S(2)}, u32[]{:S(2)}) collective-permute-start(f32[1,272,128]{2,1,0:T(8,128)S(1)} %get-tuple-element.28), channel_id=1, source_target_pairs={{0,2},{1,3},{2,0},{3,1},{4,6},{5,7},{6,4},{7,5},{8,10},{9,11},{10,... | collective-permute-start | bytes 417800 | tf_op jit(solution)/shard_map/ppermute | solution.py:493
  28.7 9.1 %collective-permute-start.2 = (f32[1,272,128]{2,1,0:T(8,128)S(1)}, f32[1,272,128]{2,1,0:T(8,128)S(1)}, u32[]{:S(2)}, u32[]{:S(2)}) collective-permute-start(f32[1,272,128]{2,1,0:T(8,128)S(1)} %shard_map.42.a_ref), channel_id=1, source_target_pairs={{0,16},{1,17},{2,18},{3,19},{4,20},{5,21},{6,22},{7,23},{8,24},{9,... | collective-permute-start | bytes 417800 | tf_op jit(solution)/shard_map/ppermute | solution.py:502
  37.8 6.6 %collective-permute-start.3 = (f32[2,272,128]{2,1,0:T(8,128)S(1)}, f32[2,272,128]{2,1,0:T(8,128)S(1)}, u32[]{:S(2)}, u32[]{:S(2)}) collective-permute-start(f32[2,272,128]{2,1,0:T(8,128)S(1)} %shard_map.43.a_ref), channel_id=1, source_target_pairs={{0,2},{1,5},{2,0},{3,7},{4,6},{5,1},{6,4},{7,3},{8,10},{9,13},{10,... | collective-permute-start | bytes 835592 | tf_op jit(solution)/shard_map/ppermute | solution.py:502
  44.5 9.6 %collective-permute-start.4 = (f32[4,272,128]{2,1,0:T(8,128)S(1)}, f32[4,272,128]{2,1,0:T(8,128)S(1)}, u32[]{:S(2)}, u32[]{:S(2)}) collective-permute-start(f32[4,272,128]{2,1,0:T(8,128)S(1)} %shard_map.44.a_ref), channel_id=1, source_target_pairs={{0,4},{1,3},{2,6},{3,1},{4,0},{5,7},{6,2},{7,5},{8,12},{9,11},{10,... | collective-permute-start | bytes 1671176 | tf_op jit(solution)/shard_map/ppermute | solution.py:502
  54.1 75.4 %collective-permute-start.5 = (f32[8,272,128]{2,1,0:T(8,128)S(1)}, f32[8,272,128]{2,1,0:T(8,128)S(1)}, u32[]{:S(2)}, u32[]{:S(2)}) collective-permute-start(f32[8,272,128]{2,1,0:T(8,128)S(1)} %shard_map.45.own_ref), channel_id=1, source_target_pairs={{0,1},{1,0},{2,3},{3,2},{4,5},{5,4},{6,7},{7,6},{8,9},{9,8},{10,11... | collective-permute-start | bytes 3342344 | tf_op jit(solution)/shard_map/ppermute | solution.py:493
  55.4 38.3 %collective-permute-start.11 = (f32[512,256]{1,0:T(8,128)S(1)}, f32[512,256]{1,0:T(8,128)}, u32[]{:S(2)}, u32[]{:S(2)}) collective-permute-start(f32[512,256]{1,0:T(8,128)S(1)} %get-tuple-element.29), channel_id=1, source_target_pairs={{0,16},{4,20},{8,24},{12,28},{16,0},{20,4},{24,8},{28,12},{1,17},{... | collective-permute-start | bytes 1572872 | tf_op jit(solution)/shard_map/ppermute | solution.py:493
  55.5 70.5 %collective-permute-start.10 = (f32[1024,256]{1,0:T(8,128)}, f32[1024,256]{1,0:T(8,128)S(1)}, u32[]{:S(2)}, u32[]{:S(2)}) collective-permute-start(f32[1024,256]{1,0:T(8,128)} %refs_0_.1), channel_id=1, source_target_pairs={{0,4},{4,0},{8,12},{12,8},{16,20},{20,16},{24,28},{28,24},{1,5},{5... | collective-permute-start | bytes 3145736 | tf_op jit(solution)/shard_map/ppermute | solution.py:493
  57.0 42.3 %collective-permute-start.12 = (f32[256,256]{1,0:T(8,128)S(1)}, f32[256,256]{1,0:T(8,128)S(1)}, u32[]{:S(2)}, u32[]{:S(2)}) collective-permute-start(f32[256,256]{1,0:T(8,128)S(1)} %get-tuple-element.30), channel_id=1, source_target_pairs={{0,16},{4,20},{8,24},{12,28},{16,0},{20,4},{24,8},{28,12},{1,17},{... | collective-permute-start | bytes 786440 | tf_op jit(solution)/shard_map/ppermute | solution.py:493
  59.9 44.6 %collective-permute-start.14 = (f32[256,256]{1,0:T(8,128)S(1)}, f32[256,256]{1,0:T(8,128)S(1)}, u32[]{:S(2)}, u32[]{:S(2)}) collective-permute-start(f32[256,256]{1,0:T(8,128)S(1)} %get-tuple-element.34), channel_id=1, source_target_pairs={{0,16},{4,20},{8,24},{12,28},{16,0},{20,4},{24,8},{28,12},{1,17},{... | collective-permute-start | bytes 786440 | tf_op jit(solution)/shard_map/ppermute | solution.py:493
  93.8 32.2 %collective-permute-start.13 = (f32[512,256]{1,0:T(8,128)}, f32[512,256]{1,0:T(8,128)}, u32[]{:S(2)}, u32[]{:S(2)}) collective-permute-start(f32[512,256]{1,0:T(8,128)} %collective-permute-done.11.refs_2_), channel_id=1, source_target_pairs={{0,4},{4,0},{8,12},{12,8},{16,20},{20,16},{24,28},{28,24},{1,5},{5... | collective-permute-start | bytes 1572872 | tf_op jit(solution)/shard_map/ppermute | solution.py:493
  99.3 15.1 %copy-start.4 = (f32[256,256]{1,0:T(8,128)}, f32[256,256]{1,0:T(8,128)S(1)}, u32[]{:S(2)}) copy-start(f32[256,256]{1,0:T(8,128)S(1)} %collective-permute-done.12.refs_3_) | copy-start | bytes 786436
  99.3 15.1 %collective-permute-start.15 = (f32[256,256]{1,0:T(8,128)S(1)}, f32[256,256]{1,0:T(8,128)S(1)}, u32[]{:S(2)}, u32[]{:S(2)}) collective-permute-start(f32[256,256]{1,0:T(8,128)S(1)} %collective-permute-done.12.refs_3_), channel_id=1, source_target_pairs={{0,4},{4,0},{8,12},{12,8},{16,20},{20,16},{24,28},{28,24},{1,5},{5... | collective-permute-start | bytes 786440 | tf_op jit(solution)/shard_map/ppermute | solution.py:493
  104.4 18.2 %collective-permute-start.16 = (f32[256,256]{1,0:T(8,128)S(1)}, f32[256,256]{1,0:T(8,128)S(1)}, u32[]{:S(2)}, u32[]{:S(2)}) collective-permute-start(f32[256,256]{1,0:T(8,128)S(1)} %collective-permute-done.14.refs_0_), channel_id=1, source_target_pairs={{0,4},{4,0},{8,12},{12,8},{16,20},{20,16},{24,28},{28,24},{1,5},{5... | collective-permute-start | bytes 786440 | tf_op jit(solution)/shard_map/ppermute | solution.py:493
  114.4 0.7 copy-start
  115.1 5.1 %collective-permute-start.6 = (f32[4,64,128]{2,1,0:T(8,128)S(1)}, f32[4,64,128]{2,1,0:T(8,128)}, u32[]{:S(2)}, u32[]{:S(2)}) collective-permute-start(f32[4,64,128]{2,1,0:T(8,128)S(1)} %shard_map.46), channel_id=1, source_target_pairs={{0,8},{1,9},{2,10},{3,11},{4,12},{5,13},{6,14},{7,15},{8,0},{9,1},... | collective-permute-start | bytes 393224 | tf_op jit(solution)/shard_map/ppermute | solution.py:502
  120.2 9.3 %collective-permute-start.7 = (f32[4,64,128]{2,1,0:T(8,128)}, f32[4,64,128]{2,1,0:T(8,128)}, u32[]{:S(2)}, u32[]{:S(2)}) collective-permute-start(f32[4,64,128]{2,1,0:T(8,128)} %collective-permute-done.6.edge_own_ref), channel_id=1, source_target_pairs={{0,1},{1,0},{2,3},{3,2},{4,5},{5,4},{6,7},{7,6},{8,9},{9,8},{10,11... | collective-permute-start | bytes 393224 | tf_op jit(solution)/shard_map/ppermute | solution.py:493
  122.6 0.7 copy-start.2
  123.3 7.6 %collective-permute-start.8 = (f32[128,128]{1,0:T(8,128)}, f32[128,128]{1,0:T(8,128)}, u32[]{:S(2)}, u32[]{:S(2)}) collective-permute-start(f32[128,128]{1,0:T(8,128)} %gram.1.a_ref), channel_id=1, source_target_pairs={{0,1},{1,0},{2,3},{3,2},{4,5},{5,4},{6,7},{7,6},{8,9},{9,8},{10,11... | collective-permute-start | bytes 196616 | tf_op jit(solution)/shard_map/ppermute | solution.py:493
  123.8 0.9 copy-start.1
  124.8 0.9 copy-start.3
  126.0 1.0 copy-start.5
  132.1 20.3 %collective-permute-start.9 = (f32[128,128]{1,0:T(8,128)S(1)}, f32[128,128]{1,0:T(8,128)S(1)}, u32[]{:S(2)}, u32[]{:S(2)}) collective-permute-start(f32[128,128]{1,0:T(8,128)S(1)} %shard_map.47.gram_ref), channel_id=1, source_target_pairs={{0,8},{4,12},{8,0},{12,4},{16,24},{20,28},{24,16},{28,20},{1,9},{5... | collective-permute-start | bytes 196616 | tf_op jit(solution)/shard_map/ppermute | solution.py:493
  148.2 27.3 %collective-permute-start.17 = (f32[2,256,128]{2,1,0:T(8,128)S(1)}, f32[2,256,128]{2,1,0:T(8,128)S(1)}, u32[]{:S(2)}, u32[]{:S(2)}) collective-permute-start(f32[2,256,128]{2,1,0:T(8,128)S(1)} %lagged.6), channel_id=1, source_target_pairs={{0,8},{4,12},{8,0},{12,4},{16,24},{20,28},{24,16},{28,20},{1,9},{5... | collective-permute-start | bytes 786440 | tf_op jit(solution)/shard_map/ppermute | solution.py:493
  150.3 12.8 %collective-permute-start.18 = (f32[2,256,128]{2,1,0:T(8,128)S(1)}, f32[2,256,128]{2,1,0:T(8,128)S(1)}, u32[]{:S(2)}, u32[]{:S(2)}) collective-permute-start(f32[2,256,128]{2,1,0:T(8,128)S(1)} %lagged.7), channel_id=1, source_target_pairs={{0,8},{4,12},{8,0},{12,4},{16,24},{20,28},{24,16},{28,20},{1,9},{5... | collective-permute-start | bytes 786440 | tf_op jit(solution)/shard_map/ppermute | solution.py:493
  150.3 18.3 %collective-permute-start.19 = (f32[2,256,128]{2,1,0:T(8,128)S(1)}, f32[2,256,128]{2,1,0:T(8,128)S(1)}, u32[]{:S(2)}, u32[]{:S(2)}) collective-permute-start(f32[2,256,128]{2,1,0:T(8,128)S(1)} %lagged.8), channel_id=1, source_target_pairs={{0,8},{4,12},{8,0},{12,4},{16,24},{20,28},{24,16},{28,20},{1,9},{5... | collective-permute-start | bytes 786440 | tf_op jit(solution)/shard_map/ppermute | solution.py:493
  152.3 21.0 %collective-permute-start.20 = (f32[2,256,128]{2,1,0:T(8,128)S(1)}, f32[2,256,128]{2,1,0:T(8,128)S(1)}, u32[]{:S(2)}, u32[]{:S(2)}) collective-permute-start(f32[2,256,128]{2,1,0:T(8,128)S(1)} %lagged.9), channel_id=1, source_target_pairs={{0,8},{4,12},{8,0},{12,4},{16,24},{20,28},{24,16},{28,20},{1,9},{5... | collective-permute-start | bytes 786440 | tf_op jit(solution)/shard_map/ppermute | solution.py:493

commit v6 on v5

--- a/solution.py
+++ b/solution.py
@@ -12,6 +12,7 @@
 BF16 = jnp.bfloat16
 HIGHEST = lax.Precision.HIGHEST
 STEP = 16
+LAGS = 4
 SMEM = pl.BlockSpec(memory_space=pltpu.SMEM)
 VMEM = pl.BlockSpec(memory_space=pltpu.VMEM)
 
@@ -31,14 +32,18 @@
 
 
 def sketch_kernel(place_ref, record_ref, weight_ref, *refs):
-    keep_ref, give_ref, high, low, even, odd, total, buffer, arrived = refs
+    keep_ref, give_ref, high, low, sums, total, buffer, arrived = refs
     pair = pl.program_id(0)
     rows, width = total.shape
     groups = weight_ref.shape[0]
 
+    lags = buffer.shape[2]
+
     def fetch(n):
         slot = lax.rem(n, 2)
-        return pltpu.make_async_copy(weight_ref.at[:, pl.ds(2 * n, 2)], buffer.at[slot], arrived.at[slot])
+        return pltpu.make_async_copy(
+            weight_ref.at[:, pl.ds(lags * n, lags)], buffer.at[slot], arrived.at[slot]
+        )
 
     @pl.when(pair == 0)
     def _():
@@ -63,19 +68,24 @@
 
     fetch(pair).wait()
     slot = lax.rem(pair, 2)
-    weight = jnp.concatenate(
-        [jnp.concatenate([buffer[slot, a, 0], buffer[slot, a, 1]], axis=1) for a in range(groups)],
-        axis=0,
-    )
-    weight_high, weight_low = split(weight)
+    weights = []
+    for lag in range(0, lags, 2):
+        weight = [
+            jnp.concatenate([buffer[slot, a, lag], buffer[slot, a, lag + 1]], axis=1) for a in range(groups)
+        ]
+        weights.append(split(jnp.concatenate(weight, axis=0)))
     for first in range(0, tiles * tile, tile):
         starts = [first + a * STEP for a in range(groups)]
         left_high = jnp.concatenate([high[s : s + tile] for s in starts], axis=1)
         left_low = jnp.concatenate([low[s : s + tile] for s in starts], axis=1)
-        value = three(left_high, left_low, weight_high, weight_low)
-        even[first : first + tile] = value[:, :width]
-        odd[first : first + tile] = value[:, width:]
-    total[...] += even[pl.ds(2 * pair, rows), :] + odd[pl.ds(2 * pair + 1, rows), :]
+        for n, weight in enumerate(weights):
+            value = three(left_high, left_low, *weight)
+            sums[2 * n, first : first + tile] = value[:, :width]
+            sums[2 * n + 1, first : first + tile] = value[:, width:]
+    value = total[...]
+    for n in range(lags):
+        value = value + sums[n, pl.ds(lags * pair + n, rows), :]
+    total[...] = value
 
     @pl.when(pair == pl.num_programs(0) - 1)
     def _():
@@ -93,17 +103,16 @@
     share = rows // shares
     return pl.pallas_call(
         sketch_kernel,
-        grid=(STEP // 2,),
+        grid=(STEP // LAGS,),
         in_specs=[SMEM, VMEM, pl.BlockSpec(memory_space=pltpu.HBM)],
         out_specs=[VMEM] * 2,
         out_shape=[jax.ShapeDtypeStruct((2, share, width), F32)] * 2,
         scratch_shapes=[
             pltpu.VMEM((length, chans), BF16),
             pltpu.VMEM((length, chans), BF16),
-            pltpu.VMEM((rows + STEP, width), F32),
-            pltpu.VMEM((rows + STEP, width), F32),
+            pltpu.VMEM((LAGS, rows + STEP, width), F32),
             pltpu.VMEM((rows, width), F32),
-            pltpu.VMEM((2, lags // STEP, 2, chans, width), F32),
+            pltpu.VMEM((2, lags // STEP, LAGS, chans, width), F32),
             pltpu.SemaphoreType.DMA((2,)),
         ],
         compiler_params=pltpu.CompilerParams(vmem_limit_bytes=24 * 2**20),

time: 177 us -> 176 us (level)
  no operation moved by 1% of the time
where the time goes in v6:
time: 176 us
  waiting for transfers between devices  95.5 us (54%)
  Pallas kernels  52 us (30%)
  starting transfers between devices  23 us (13%)
  local copies, waits for them, and re-layouts  4.34 us (2%)
    ppermute x17, waiting for transfers between devices, to(): return lax.ppermute(block, axis, route)  71 us
    ppermute x4, waiting for transfers between devices, to_both(): return lax.ppermute(block, ('tm', 'chan'), route)  24.5 us
    pallas_call x1, Pallas kernels, sketch(): pl.pallas_call(sketch_kernel, grid=(STEP // LAGS,), in_specs=[SMEM, VMEM,...  18.6 us
    ppermute x17, starting transfers between devices, to(): return lax.ppermute(block, axis, route)  17.1 us
    pallas_call x5, Pallas kernels, lagged(): pl.pallas_call(functools.partial(lagged_kernel, places), grid=(lags // 2,...  15.7 us
    ppermute x4, starting transfers between devices, to_both(): return lax.ppermute(block, ('tm', 'chan'), route)  5.9 us
    unnamed x12, local copies, waits for them, and re-layouts  4.25 us
  transfers between devices with their start and end apart: 21, of which 13 were waited for; matrix products, arithmetic and copies ran while one was open for 0% of the time, Pallas kernels for 18%

profile of v6, /device:TPU:0, one launch (start us, length us, event | category | flops | bytes accessed | tf_op | source)
XLA Modules:
  0.0 175.7 jit_solution(8380909788476156852)
XLA Ops:
  0.7 0.1 stack.31.place_ref
  0.8 18.6 %sketch.1 = (f32[2,272,128]{2,1,0:T(8,128)S(1)}, f32[2,272,128]{2,1,0:T(8,128)S(1)}) custom-call(s32[7]{0:T(128)S(1)} %stack.31.place_ref, f32[1024,256]{1,0:T(8,128)} %refs_0_.1, f32[4,16,256,128]{3,2,1,0:T(8,128)} %bitcast.13), custom_call_target="tpu_custom_call" | custom-call | flops 13690208256 | bytes 10125312 | tf_op jit(solution)/shard_map/sketch/pallas_call | solution.py:104
  19.4 0.6 collective-permute-start
  20.0 1.2 collective-permute-done.got_ref
  21.2 2.9 %collective-permute-start.1 = (f32[1,272,128]{2,1,0:T(8,128)S(1)}, f32[1,272,128]{2,1,0:T(8,128)S(1)}, u32[]{:S(2)}, u32[]{:S(2)}) collective-permute-start(f32[1,272,128]{2,1,0:T(8,128)S(1)} %get-tuple-element.28), channel_id=1, source_target_pairs={{0,2},{1,3},{2,0},{3,1},{4,6},{5,7},{6,4},{7,5},{8,10},{9,11},{10,... | collective-permute-start | bytes 417800 | tf_op jit(solution)/shard_map/ppermute | solution.py:502
  24.1 4.0 %collective-permute-done.1.b_ref = f32[1,272,128]{2,1,0:T(8,128)S(1)} collective-permute-done((f32[1,272,128]{2,1,0:T(8,128)S(1)}, f32[1,272,128]{2,1,0:T(8,128)S(1)}, u32[]{:S(2)}, u32[]{:S(2)}) %collective-permute-start.1) | collective-permute-done | bytes 139296 | tf_op jit(solution)/shard_map/ppermute | solution.py:502
  28.1 2.9 %collective-permute-start.2 = (f32[1,272,128]{2,1,0:T(8,128)S(1)}, f32[1,272,128]{2,1,0:T(8,128)S(1)}, u32[]{:S(2)}, u32[]{:S(2)}) collective-permute-start(f32[1,272,128]{2,1,0:T(8,128)S(1)} %shard_map.42.a_ref), channel_id=1, source_target_pairs={{0,16},{1,17},{2,18},{3,19},{4,20},{5,21},{6,22},{7,23},{8,24},{9,... | collective-permute-start | bytes 417800 | tf_op jit(solution)/shard_map/ppermute | solution.py:511
  31.0 6.2 %collective-permute-done.2.b_ref = f32[1,272,128]{2,1,0:T(8,128)S(1)} collective-permute-done((f32[1,272,128]{2,1,0:T(8,128)S(1)}, f32[1,272,128]{2,1,0:T(8,128)S(1)}, u32[]{:S(2)}, u32[]{:S(2)}) %collective-permute-start.2) | collective-permute-done | bytes 139296 | tf_op jit(solution)/shard_map/ppermute | solution.py:511
  37.2 1.5 collective-permute-start.3
  38.8 5.1 %collective-permute-done.3.b_ref = f32[2,272,128]{2,1,0:T(8,128)S(1)} collective-permute-done((f32[2,272,128]{2,1,0:T(8,128)S(1)}, f32[2,272,128]{2,1,0:T(8,128)S(1)}, u32[]{:S(2)}, u32[]{:S(2)}) %collective-permute-start.3) | collective-permute-done | bytes 278560 | tf_op jit(solution)/shard_map/ppermute | solution.py:511
  43.9 1.5 collective-permute-start.4
  45.4 8.1 %collective-permute-done.4.b_ref = f32[4,272,128]{2,1,0:T(8,128)S(1)} collective-permute-done((f32[4,272,128]{2,1,0:T(8,128)S(1)}, f32[4,272,128]{2,1,0:T(8,128)S(1)}, u32[]{:S(2)}, u32[]{:S(2)}) %collective-permute-start.4) | collective-permute-done | bytes 557088 | tf_op jit(solution)/shard_map/ppermute | solution.py:511
  53.5 0.1 shard_map.45.own_ref
  53.6 0.1 collective-permute-start.5
  53.7 1.2 cut.1
  54.9 0.1 collective-permute-start.11
  55.0 1.5 collective-permute-start.10
  56.5 2.8 %collective-permute-start.12 = (f32[256,256]{1,0:T(8,128)S(1)}, f32[256,256]{1,0:T(8,128)S(1)}, u32[]{:S(2)}, u32[]{:S(2)}) collective-permute-start(f32[256,256]{1,0:T(8,128)S(1)} %get-tuple-element.30), channel_id=1, source_target_pairs={{0,16},{4,20},{8,24},{12,28},{16,0},{20,4},{24,8},{28,12},{1,17},{... | collective-permute-start | bytes 786440 | tf_op jit(solution)/shard_map/ppermute | solution.py:502
  59.3 0.1 collective-permute-start.14
  59.4 33.8 %collective-permute-done.11.refs_2_ = f32[512,256]{1,0:T(8,128)} collective-permute-done((f32[512,256]{1,0:T(8,128)S(1)}, f32[512,256]{1,0:T(8,128)}, u32[]{:S(2)}, u32[]{:S(2)}) %collective-permute-start.11) | collective-permute-done | bytes 524320 | tf_op jit(solution)/shard_map/ppermute | solution.py:502
  93.2 1.4 collective-permute-start.13
  94.6 4.1 %collective-permute-done.12.refs_3_ = f32[256,256]{1,0:T(8,128)S(1)} collective-permute-done((f32[256,256]{1,0:T(8,128)S(1)}, f32[256,256]{1,0:T(8,128)S(1)}, u32[]{:S(2)}, u32[]{:S(2)}) %collective-permute-start.12) | collective-permute-done | bytes 262176 | tf_op jit(solution)/shard_map/ppermute | solution.py:502
  98.7 1.4 collective-permute-start.15
  100.2 3.7 %collective-permute-done.14.refs_0_ = f32[256,256]{1,0:T(8,128)S(1)} collective-permute-done((f32[256,256]{1,0:T(8,128)S(1)}, f32[256,256]{1,0:T(8,128)S(1)}, u32[]{:S(2)}, u32[]{:S(2)}) %collective-permute-start.14) | collective-permute-done | bytes 262176 | tf_op jit(solution)/shard_map/ppermute | solution.py:502
  103.9 1.4 collective-permute-start.16
  105.3 0.6 shard_map.46
  105.9 8.0 %collective-permute-done.15.refs_1_ = f32[256,256]{1,0:T(8,128)S(1)} collective-permute-done((f32[256,256]{1,0:T(8,128)S(1)}, f32[256,256]{1,0:T(8,128)S(1)}, u32[]{:S(2)}, u32[]{:S(2)}) %collective-permute-start.15) | collective-permute-done | bytes 262176 | tf_op jit(solution)/shard_map/ppermute | solution.py:502
  113.8 0.7 copy-done
  114.5 0.0 collective-permute-start.6
  114.5 5.1 %collective-permute-done.6.edge_own_ref = f32[4,64,128]{2,1,0:T(8,128)} collective-permute-done((f32[4,64,128]{2,1,0:T(8,128)S(1)}, f32[4,64,128]{2,1,0:T(8,128)}, u32[]{:S(2)}, u32[]{:S(2)}) %collective-permute-start.6) | collective-permute-done | bytes 131104 | tf_op jit(solution)/shard_map/ppermute | solution.py:511
  119.6 2.4 %gram.1.a_ref = f32[128,128]{1,0:T(8,128)} custom-call(s32[7]{0:T(128)S(1)} %stack.31.place_ref, f32[8,272,128]{2,1,0:T(8,128)S(1)} %shard_map.45.own_ref), custom_call_target="tpu_custom_call" | custom-call | flops 427819008 | bytes 1114112 | tf_op jit(solution)/shard_map/gram/pallas_call | solution.py:251
  122.0 0.0 collective-permute-done.16.refs_2_
  122.0 0.7 copy-done.2
  122.7 0.5 collective-permute-start.8
  123.2 0.9 copy-done.1
  124.2 0.9 copy-done.3
  125.1 0.3 turn.3
  125.4 0.0 collective-permute-done.13.refs_4_
  125.4 0.0 collective-permute-done.10.refs_1_
  125.4 0.0 copy-start.5
  125.5 0.9 copy-done.5
  126.4 2.5 %turn.2 = (bf16[256,1024]{1,0:T(8,128)(2,1)S(1)}, bf16[256,1024]{1,0:T(8,128)(2,1)S(1)}, bf16[256,1024]{1,0:T(8,128)(2,1)S(1)}, bf16[256,1024]{1,0:T(8,128)(2,1)...) custom-call(f32[1024,256]{1,0:T(8,128)} %refs_0_.1, ...), custom_call_target="tpu_custom_call" | custom-call | bytes 6815744 | tf_op jit(solution)/shard_map/turn/pallas_call | solution.py:141
  128.9 0.0 collective-permute-done.5.got_ref
  128.9 1.4 assemble.1.sketch_ref.refs_16_
  130.3 1.2 shard_map.47.gram_ref
  131.5 0.1 collective-permute-start.9
  131.6 2.0 %lagged.9 = f32[2,256,128]{2,1,0:T(8,128)S(1)} custom-call(s32[1]{0:T(128)} %bitcast.12.lag_ref, bf16[256,1024]{1,0:T(8,128)(2,1)S(1)} %get-tuple-element.31.refs_0_, bf16[256,512]{1,0:T(8,128)(2,1)S(1)} %get-tuple-element.32.refs_1_, bf16[256,256]{1,0:T(8,128)(2,1)S(1)} %get-tuple-element.33.refs_2_, bf16[256,256]{1,0:T(8,128)(2,1)S(1)} %get-tuple-element.35.refs_3_, ...), custom_call_target="tpu_custom_call" | custom-call | flops 1610612736 | bytes 6684672 | tf_op jit(solution)/shard_map/lagged/pallas_call | solution.py:341
  133.6 2.0 %lagged.8 = f32[2,256,128]{2,1,0:T(8,128)S(1)} custom-call(s32[1]{0:T(128)} %bitcast.11.lag_ref, bf16[256,1024]{1,0:T(8,128)(2,1)S(1)} %get-tuple-element.31.refs_0_, bf16[256,512]{1,0:T(8,128)(2,1)S(1)} %get-tuple-element.32.refs_1_, bf16[256,256]{1,0:T(8,128)(2,1)S(1)} %get-tuple-element.33.refs_2_, bf16[256,256]{1,0:T(8,128)(2,1)S(1)} %get-tuple-element.35.refs_3_, ...), custom_call_target="tpu_custom_call" | custom-call | flops 1610612736 | bytes 6684672 | tf_op jit(solution)/shard_map/lagged/pallas_call | solution.py:341
  135.6 2.0 %lagged.7 = f32[2,256,128]{2,1,0:T(8,128)S(1)} custom-call(s32[1]{0:T(128)} %bitcast.10.lag_ref, bf16[256,1024]{1,0:T(8,128)(2,1)S(1)} %get-tuple-element.31.refs_0_, bf16[256,512]{1,0:T(8,128)(2,1)S(1)} %get-tuple-element.32.refs_1_, bf16[256,256]{1,0:T(8,128)(2,1)S(1)} %get-tuple-element.33.refs_2_, bf16[256,256]{1,0:T(8,128)(2,1)S(1)} %get-tuple-element.35.refs_3_, ...), custom_call_target="tpu_custom_call" | custom-call | flops 1610612736 | bytes 6684672 | tf_op jit(solution)/shard_map/lagged/pallas_call | solution.py:341
  137.6 7.8 %lagged.5.kept_ref = f32[8,256,128]{2,1,0:T(8,128)S(1)} custom-call(s32[1]{0:T(128)} %bitcast.8.lag_ref, bf16[256,1024]{1,0:T(8,128)(2,1)S(1)} %get-tuple-element.31.refs_0_, bf16[256,512]{1,0:T(8,128)(2,1)S(1)} %get-tuple-element.32.refs_1_, bf16[256,256]{1,0:T(8,128)(2,1)S(1)} %get-tuple-element.33.refs_2_, ...), custom_call_target="tpu_custom_call" | custom-call | flops 6442450944 | bytes 7471104 | tf_op jit(solution)/shard_map/lagged/pallas_call | solution.py:341
  145.4 2.0 %lagged.6 = f32[2,256,128]{2,1,0:T(8,128)S(1)} custom-call(s32[1]{0:T(128)} %bitcast.9.lag_ref, bf16[256,1024]{1,0:T(8,128)(2,1)S(1)} %get-tuple-element.31.refs_0_, bf16[256,512]{1,0:T(8,128)(2,1)S(1)} %get-tuple-element.32.refs_1_, bf16[256,256]{1,0:T(8,128)(2,1)S(1)} %get-tuple-element.33.refs_2_, bf16[256,256]{1,0:T(8,128)(2,1)S(1)} %get-tuple-element.35.refs_3_, ...), custom_call_target="tpu_custom_call" | custom-call | flops 1610612736 | bytes 6684672 | tf_op jit(solution)/shard_map/lagged/pallas_call | solution.py:341
  147.4 2.1 %collective-permute-start.17 = (f32[2,256,128]{2,1,0:T(8,128)S(1)}, f32[2,256,128]{2,1,0:T(8,128)S(1)}, u32[]{:S(2)}, u32[]{:S(2)}) collective-permute-start(f32[2,256,128]{2,1,0:T(8,128)S(1)} %lagged.6), channel_id=1, source_target_pairs={{0,8},{4,12},{8,0},{12,4},{16,24},{20,28},{24,16},{28,20},{1,9},{5... | collective-permute-start | bytes 786440 | tf_op jit(solution)/shard_map/ppermute | solution.py:502
  149.5 0.1 collective-permute-start.18
  149.6 1.9 %collective-permute-start.19 = (f32[2,256,128]{2,1,0:T(8,128)S(1)}, f32[2,256,128]{2,1,0:T(8,128)S(1)}, u32[]{:S(2)}, u32[]{:S(2)}) collective-permute-start(f32[2,256,128]{2,1,0:T(8,128)S(1)} %lagged.8), channel_id=1, source_target_pairs={{0,8},{4,12},{8,0},{12,4},{16,24},{20,28},{24,16},{28,20},{1,9},{5... | collective-permute-start | bytes 786440 | tf_op jit(solution)/shard_map/ppermute | solution.py:502
  151.5 0.1 collective-permute-start.20
  151.6 0.0 collective-permute-done.9.other_ref
  151.6 3.5 %factor.1.inverse_ref = f32[128,128]{1,0:T(8,128)S(1)} custom-call(f32[128,128]{1,0:T(8,128)S(1)} %shard_map.47.gram_ref, f32[128,128]{1,0:T(8,128)S(1)} %collective-permute-done.9.other_ref), custom_call_target="tpu_custom_call" | custom-call | flops 3000000000 | bytes 131072 | tf_op jit(solution)/shard_map/factor/pallas_call | solution.py:304
  155.1 1.2 shard_map.48
  156.3 5.9 %collective-permute-done.18.refs_0_ = f32[2,256,128]{2,1,0:T(8,128)S(1)} collective-permute-done((f32[2,256,128]{2,1,0:T(8,128)S(1)}, f32[2,256,128]{2,1,0:T(8,128)S(1)}, u32[]{:S(2)}, u32[]{:S(2)}) %collective-permute-start.18) | collective-permute-done | bytes 262176 | tf_op jit(solution)/shard_map/ppermute | solution.py:502
  162.3 5.6 %collective-permute-done.19.refs_1_ = f32[2,256,128]{2,1,0:T(8,128)S(1)} collective-permute-done((f32[2,256,128]{2,1,0:T(8,128)S(1)}, f32[2,256,128]{2,1,0:T(8,128)S(1)}, u32[]{:S(2)}, u32[]{:S(2)}) %collective-permute-start.19) | collective-permute-done | bytes 262176 | tf_op jit(solution)/shard_map/ppermute | solution.py:502
  167.9 4.7 %collective-permute-done.20.refs_2_ = f32[2,256,128]{2,1,0:T(8,128)S(1)} collective-permute-done((f32[2,256,128]{2,1,0:T(8,128)S(1)}, f32[2,256,128]{2,1,0:T(8,128)S(1)}, u32[]{:S(2)}, u32[]{:S(2)}) %collective-permute-start.20) | collective-permute-done | bytes 262176 | tf_op jit(solution)/shard_map/ppermute | solution.py:502
  172.5 2.1 %finish.2.refs_1_ = f32[8,256,128]{2,1,0:T(8,128)} custom-call(f32[128,128]{1,0:T(8,128)S(1)} %factor.1.inverse_ref, f32[8,256,128]{2,1,0:T(8,128)S(1)} %lagged.5.kept_ref, f32[2,256,128]{2,1,0:T(8,128)S(1)} %collective-permute-done.18.refs_0_, f32[2,256,128]{2,1,0:T(8,128)S(1)} %collective-permute-done.19.refs_1_, ...), custom_call_target="tpu_custom_call" | custom-call | flops 150994944 | bytes 2359296 | tf_op jit(solution)/shard_map/finish/pallas_call | solution.py:378
  174.7 0.0 collective-permute-done.17.refs_0_
  174.7 1.0 finish.3
  (13 shorter events, 0.1 us)
Async XLA Ops:
  19.4 1.7 collective-permute-start
  21.2 6.9 %collective-permute-start.1 = (f32[1,272,128]{2,1,0:T(8,128)S(1)}, f32[1,272,128]{2,1,0:T(8,128)S(1)}, u32[]{:S(2)}, u32[]{:S(2)}) collective-permute-start(f32[1,272,128]{2,1,0:T(8,128)S(1)} %get-tuple-element.28), channel_id=1, source_target_pairs={{0,2},{1,3},{2,0},{3,1},{4,6},{5,7},{6,4},{7,5},{8,10},{9,11},{10,... | collective-permute-start | bytes 417800 | tf_op jit(solution)/shard_map/ppermute | solution.py:502
  28.1 9.1 %collective-permute-start.2 = (f32[1,272,128]{2,1,0:T(8,128)S(1)}, f32[1,272,128]{2,1,0:T(8,128)S(1)}, u32[]{:S(2)}, u32[]{:S(2)}) collective-permute-start(f32[1,272,128]{2,1,0:T(8,128)S(1)} %shard_map.42.a_ref), channel_id=1, source_target_pairs={{0,16},{1,17},{2,18},{3,19},{4,20},{5,21},{6,22},{7,23},{8,24},{9,... | collective-permute-start | bytes 417800 | tf_op jit(solution)/shard_map/ppermute | solution.py:511
  37.2 6.6 %collective-permute-start.3 = (f32[2,272,128]{2,1,0:T(8,128)S(1)}, f32[2,272,128]{2,1,0:T(8,128)S(1)}, u32[]{:S(2)}, u32[]{:S(2)}) collective-permute-start(f32[2,272,128]{2,1,0:T(8,128)S(1)} %shard_map.43.a_ref), channel_id=1, source_target_pairs={{0,2},{1,5},{2,0},{3,7},{4,6},{5,1},{6,4},{7,3},{8,10},{9,13},{10,... | collective-permute-start | bytes 835592 | tf_op jit(solution)/shard_map/ppermute | solution.py:511
  43.9 9.6 %collective-permute-start.4 = (f32[4,272,128]{2,1,0:T(8,128)S(1)}, f32[4,272,128]{2,1,0:T(8,128)S(1)}, u32[]{:S(2)}, u32[]{:S(2)}) collective-permute-start(f32[4,272,128]{2,1,0:T(8,128)S(1)} %shard_map.44.a_ref), channel_id=1, source_target_pairs={{0,4},{1,3},{2,6},{3,1},{4,0},{5,7},{6,2},{7,5},{8,12},{9,11},{10,... | collective-permute-start | bytes 1671176 | tf_op jit(solution)/shard_map/ppermute | solution.py:511
  53.6 75.4 %collective-permute-start.5 = (f32[8,272,128]{2,1,0:T(8,128)S(1)}, f32[8,272,128]{2,1,0:T(8,128)S(1)}, u32[]{:S(2)}, u32[]{:S(2)}) collective-permute-start(f32[8,272,128]{2,1,0:T(8,128)S(1)} %shard_map.45.own_ref), channel_id=1, source_target_pairs={{0,1},{1,0},{2,3},{3,2},{4,5},{5,4},{6,7},{7,6},{8,9},{9,8},{10,11... | collective-permute-start | bytes 3342344 | tf_op jit(solution)/shard_map/ppermute | solution.py:502
  54.9 38.3 %collective-permute-start.11 = (f32[512,256]{1,0:T(8,128)S(1)}, f32[512,256]{1,0:T(8,128)}, u32[]{:S(2)}, u32[]{:S(2)}) collective-permute-start(f32[512,256]{1,0:T(8,128)S(1)} %get-tuple-element.29), channel_id=1, source_target_pairs={{0,16},{4,20},{8,24},{12,28},{16,0},{20,4},{24,8},{28,12},{1,17},{... | collective-permute-start | bytes 1572872 | tf_op jit(solution)/shard_map/ppermute | solution.py:502
  55.0 70.5 %collective-permute-start.10 = (f32[1024,256]{1,0:T(8,128)}, f32[1024,256]{1,0:T(8,128)S(1)}, u32[]{:S(2)}, u32[]{:S(2)}) collective-permute-start(f32[1024,256]{1,0:T(8,128)} %refs_0_.1), channel_id=1, source_target_pairs={{0,4},{4,0},{8,12},{12,8},{16,20},{20,16},{24,28},{28,24},{1,5},{5... | collective-permute-start | bytes 3145736 | tf_op jit(solution)/shard_map/ppermute | solution.py:502
  56.5 42.3 %collective-permute-start.12 = (f32[256,256]{1,0:T(8,128)S(1)}, f32[256,256]{1,0:T(8,128)S(1)}, u32[]{:S(2)}, u32[]{:S(2)}) collective-permute-start(f32[256,256]{1,0:T(8,128)S(1)} %get-tuple-element.30), channel_id=1, source_target_pairs={{0,16},{4,20},{8,24},{12,28},{16,0},{20,4},{24,8},{28,12},{1,17},{... | collective-permute-start | bytes 786440 | tf_op jit(solution)/shard_map/ppermute | solution.py:502
  59.3 44.6 %collective-permute-start.14 = (f32[256,256]{1,0:T(8,128)S(1)}, f32[256,256]{1,0:T(8,128)S(1)}, u32[]{:S(2)}, u32[]{:S(2)}) collective-permute-start(f32[256,256]{1,0:T(8,128)S(1)} %get-tuple-element.34), channel_id=1, source_target_pairs={{0,16},{4,20},{8,24},{12,28},{16,0},{20,4},{24,8},{28,12},{1,17},{... | collective-permute-start | bytes 786440 | tf_op jit(solution)/shard_map/ppermute | solution.py:502
  93.2 32.2 %collective-permute-start.13 = (f32[512,256]{1,0:T(8,128)}, f32[512,256]{1,0:T(8,128)}, u32[]{:S(2)}, u32[]{:S(2)}) collective-permute-start(f32[512,256]{1,0:T(8,128)} %collective-permute-done.11.refs_2_), channel_id=1, source_target_pairs={{0,4},{4,0},{8,12},{12,8},{16,20},{20,16},{24,28},{28,24},{1,5},{5... | collective-permute-start | bytes 1572872 | tf_op jit(solution)/shard_map/ppermute | solution.py:502
  98.7 15.1 %copy-start.4 = (f32[256,256]{1,0:T(8,128)}, f32[256,256]{1,0:T(8,128)S(1)}, u32[]{:S(2)}) copy-start(f32[256,256]{1,0:T(8,128)S(1)} %collective-permute-done.12.refs_3_) | copy-start | bytes 786436
  98.7 15.1 %collective-permute-start.15 = (f32[256,256]{1,0:T(8,128)S(1)}, f32[256,256]{1,0:T(8,128)S(1)}, u32[]{:S(2)}, u32[]{:S(2)}) collective-permute-start(f32[256,256]{1,0:T(8,128)S(1)} %collective-permute-done.12.refs_3_), channel_id=1, source_target_pairs={{0,4},{4,0},{8,12},{12,8},{16,20},{20,16},{24,28},{28,24},{1,5},{5... | collective-permute-start | bytes 786440 | tf_op jit(solution)/shard_map/ppermute | solution.py:502
  103.9 18.2 %collective-permute-start.16 = (f32[256,256]{1,0:T(8,128)S(1)}, f32[256,256]{1,0:T(8,128)S(1)}, u32[]{:S(2)}, u32[]{:S(2)}) collective-permute-start(f32[256,256]{1,0:T(8,128)S(1)} %collective-permute-done.14.refs_0_), channel_id=1, source_target_pairs={{0,4},{4,0},{8,12},{12,8},{16,20},{20,16},{24,28},{28,24},{1,5},{5... | collective-permute-start | bytes 786440 | tf_op jit(solution)/shard_map/ppermute | solution.py:502
  113.8 0.7 copy-start
  114.5 5.1 %collective-permute-start.6 = (f32[4,64,128]{2,1,0:T(8,128)S(1)}, f32[4,64,128]{2,1,0:T(8,128)}, u32[]{:S(2)}, u32[]{:S(2)}) collective-permute-start(f32[4,64,128]{2,1,0:T(8,128)S(1)} %shard_map.46), channel_id=1, source_target_pairs={{0,8},{1,9},{2,10},{3,11},{4,12},{5,13},{6,14},{7,15},{8,0},{9,1},... | collective-permute-start | bytes 393224 | tf_op jit(solution)/shard_map/ppermute | solution.py:511
  119.6 9.3 %collective-permute-start.7 = (f32[4,64,128]{2,1,0:T(8,128)}, f32[4,64,128]{2,1,0:T(8,128)}, u32[]{:S(2)}, u32[]{:S(2)}) collective-permute-start(f32[4,64,128]{2,1,0:T(8,128)} %collective-permute-done.6.edge_own_ref), channel_id=1, source_target_pairs={{0,1},{1,0},{2,3},{3,2},{4,5},{5,4},{6,7},{7,6},{8,9},{9,8},{10,11... | collective-permute-start | bytes 393224 | tf_op jit(solution)/shard_map/ppermute | solution.py:502
  122.0 0.7 copy-start.2
  122.7 7.6 %collective-permute-start.8 = (f32[128,128]{1,0:T(8,128)}, f32[128,128]{1,0:T(8,128)}, u32[]{:S(2)}, u32[]{:S(2)}) collective-permute-start(f32[128,128]{1,0:T(8,128)} %gram.1.a_ref), channel_id=1, source_target_pairs={{0,1},{1,0},{2,3},{3,2},{4,5},{5,4},{6,7},{7,6},{8,9},{9,8},{10,11... | collective-permute-start | bytes 196616 | tf_op jit(solution)/shard_map/ppermute | solution.py:502
  123.2 0.9 copy-start.1
  124.2 0.9 copy-start.3
  125.4 1.0 copy-start.5
  131.5 20.1 %collective-permute-start.9 = (f32[128,128]{1,0:T(8,128)S(1)}, f32[128,128]{1,0:T(8,128)S(1)}, u32[]{:S(2)}, u32[]{:S(2)}) collective-permute-start(f32[128,128]{1,0:T(8,128)S(1)} %shard_map.47.gram_ref), channel_id=1, source_target_pairs={{0,8},{4,12},{8,0},{12,4},{16,24},{20,28},{24,16},{28,20},{1,9},{5... | collective-permute-start | bytes 196616 | tf_op jit(solution)/shard_map/ppermute | solution.py:502
  147.4 27.3 %collective-permute-start.17 = (f32[2,256,128]{2,1,0:T(8,128)S(1)}, f32[2,256,128]{2,1,0:T(8,128)S(1)}, u32[]{:S(2)}, u32[]{:S(2)}) collective-permute-start(f32[2,256,128]{2,1,0:T(8,128)S(1)} %lagged.6), channel_id=1, source_target_pairs={{0,8},{4,12},{8,0},{12,4},{16,24},{20,28},{24,16},{28,20},{1,9},{5... | collective-permute-start | bytes 786440 | tf_op jit(solution)/shard_map/ppermute | solution.py:502
  149.5 12.8 %collective-permute-start.18 = (f32[2,256,128]{2,1,0:T(8,128)S(1)}, f32[2,256,128]{2,1,0:T(8,128)S(1)}, u32[]{:S(2)}, u32[]{:S(2)}) collective-permute-start(f32[2,256,128]{2,1,0:T(8,128)S(1)} %lagged.7), channel_id=1, source_target_pairs={{0,8},{4,12},{8,0},{12,4},{16,24},{20,28},{24,16},{28,20},{1,9},{5... | collective-permute-start | bytes 786440 | tf_op jit(solution)/shard_map/ppermute | solution.py:502
  149.6 18.3 %collective-permute-start.19 = (f32[2,256,128]{2,1,0:T(8,128)S(1)}, f32[2,256,128]{2,1,0:T(8,128)S(1)}, u32[]{:S(2)}, u32[]{:S(2)}) collective-permute-start(f32[2,256,128]{2,1,0:T(8,128)S(1)} %lagged.8), channel_id=1, source_target_pairs={{0,8},{4,12},{8,0},{12,4},{16,24},{20,28},{24,16},{28,20},{1,9},{5... | collective-permute-start | bytes 786440 | tf_op jit(solution)/shard_map/ppermute | solution.py:502
  151.5 21.0 %collective-permute-start.20 = (f32[2,256,128]{2,1,0:T(8,128)S(1)}, f32[2,256,128]{2,1,0:T(8,128)S(1)}, u32[]{:S(2)}, u32[]{:S(2)}) collective-permute-start(f32[2,256,128]{2,1,0:T(8,128)S(1)} %lagged.9), channel_id=1, source_target_pairs={{0,8},{4,12},{8,0},{12,4},{16,24},{20,28},{24,16},{28,20},{1,9},{5... | collective-permute-start | bytes 786440 | tf_op jit(solution)/shard_map/ppermute | solution.py:502
